TPU v7x, 32 devices: a whole 2x2x4 slice. The times are simulated.
32 devices in a mesh: dp: 8 (over z, core), fsdp: 4 (over y, x).
Axes of the slice: x: 2, y: 2, z: 4, core: 2. Of those that a mesh axis runs over, the one named last changes fastest.
Arguments:
- tokens: bfloat16 [16384, 1280], P(('dp', 'fsdp')), may hold values from -6 to 6
- out_cotangent: bfloat16 [16384, 1280], P(('dp', 'fsdp')), may hold values from -6 to 6
- assignment: int32 [16384, 7], P(('dp', 'fsdp')), may hold values from 0 to 15, all different within a row
- norm_gains: bfloat16 [1280, 2], P(('dp', 'fsdp')), may hold values from 0.5 to 1.5
- attention_weights: bfloat16 [1280, 4, 1280], P(('dp', 'fsdp')), may hold values from -0.67361548 to 0.67361548
- router_weights: bfloat16 [1280, 16], P(('dp', 'fsdp')), may hold values from -0.078125 to 0.078125
- shared_weights: bfloat16 [1280, 3, 896], P(('dp', 'fsdp')), may hold values from -0.15625 to 0.15625
- expert_weights: bfloat16 [16, 3, 1280, 896], P('dp', None, None, 'fsdp'), may hold values from -0.15625 to 0.15625
Outputs:
- block_output: bfloat16 [16384, 1280], P(('dp', 'fsdp'))
- token_gradient: float32 [16384, 1280], P(('dp', 'fsdp'))
- gain_gradient: float32 [1280, 2], P(('dp', 'fsdp'))
- attention_gradient: float32 [1280, 4, 1280], P(('dp', 'fsdp'))
- router_gradient: float32 [1280, 16], P(('dp', 'fsdp'))
- shared_gradient: float32 [1280, 3, 896], P(('dp', 'fsdp'))
- expert_gradient: float32 [16, 3, 1280, 896], P('dp', None, None, 'fsdp')
All inputs are finite; a program needn't handle non-finite values.
Results may differ from a plain program's by a relative error of at most 0.014.
Values may be sent and summed in bfloat16 or wider, within the bound.
No kernel may reach another device: no remote copies, remote signals or barrier semaphores. Data moves between devices by JAX's collectives and lax.ppermute only.
A program may use at most 384 MiB of HBM per device.

v0:
```python
import jax
import jax.numpy as jnp
from jax import lax
from jax.sharding import PartitionSpec as P

HEAD_SIZE = 128
TOPK = 7


EPSILON = 1e-06
MASKED = -1e30


def rotary_tables(sequence_length):
    position = jnp.arange(sequence_length).astype(jnp.float32)
    frequency = 10000.0 ** (-jnp.arange(HEAD_SIZE // 2).astype(jnp.float32) * (2.0 / HEAD_SIZE))
    turned = position[:, None] * frequency[None, :]
    return (jnp.cos(turned)[:, None, :], jnp.sin(turned)[:, None, :])


def rotate(values, cosine_table, sine_table):
    half_size = values.shape[-1] // 2
    first_half = values[..., :half_size]
    second_half = values[..., half_size:]
    return jnp.concatenate(
        [
            first_half * cosine_table - second_half * sine_table,
            second_half * cosine_table + first_half * sine_table,
        ],
        axis=-1,
    )


def unrotate(values, cosine_table, sine_table):
    half_size = values.shape[-1] // 2
    first_half = values[..., :half_size]
    second_half = values[..., half_size:]
    return jnp.concatenate(
        [
            first_half * cosine_table + second_half * sine_table,
            second_half * cosine_table - first_half * sine_table,
        ],
        axis=-1,
    )


def norm_forward(values, gain_vector):
    inverse_root = lax.rsqrt(jnp.mean(values * values, axis=-1, keepdims=True) + EPSILON)
    unit_values = values * inverse_root
    return (unit_values * gain_vector, unit_values, inverse_root)


def norm_backward(upstream, unit_values, inverse_root, gain_vector):
    scaled = upstream * gain_vector
    gain_part = jnp.sum(upstream * unit_values, axis=0)
    input_part = inverse_root * (
        scaled - unit_values * jnp.mean(scaled * unit_values, axis=-1, keepdims=True)
    )
    return (input_part, gain_part)


def silu_parts(gate_value):
    sigmoid_value = jax.nn.sigmoid(gate_value)
    return (gate_value * sigmoid_value, sigmoid_value * (1.0 + gate_value * (1.0 - sigmoid_value)))


def experts_forward(slot_rows, weights):
    gate_value = jnp.einsum(
        "secd,edh->sech", slot_rows, weights[:, 0], preferred_element_type=jnp.float32
    )
    up_value = jnp.einsum(
        "secd,edh->sech", slot_rows, weights[:, 1], preferred_element_type=jnp.float32
    )
    active, slope = silu_parts(gate_value)
    hidden = (active * up_value).astype(jnp.bfloat16)
    return jnp.einsum("sech,edh->secd", hidden, weights[:, 2], preferred_element_type=jnp.float32)


def experts_backward(slot_rows, slot_cotangent, weights):
    gate_value = jnp.einsum(
        "secd,edh->sech", slot_rows, weights[:, 0], preferred_element_type=jnp.float32
    )
    up_value = jnp.einsum(
        "secd,edh->sech", slot_rows, weights[:, 1], preferred_element_type=jnp.float32
    )
    active, slope = silu_parts(gate_value)
    hidden = (active * up_value).astype(jnp.bfloat16)
    hidden_cot = jnp.einsum(
        "secd,edh->sech", slot_cotangent, weights[:, 2], preferred_element_type=jnp.float32
    )
    gate_cotangent = (hidden_cot * up_value * slope).astype(jnp.bfloat16)
    up_cotangent = (hidden_cot * active).astype(jnp.bfloat16)
    gate_weight_part = jnp.einsum(
        "secd,sech->edh", slot_rows, gate_cotangent, preferred_element_type=jnp.float32
    )
    up_weight_part = jnp.einsum(
        "secd,sech->edh", slot_rows, up_cotangent, preferred_element_type=jnp.float32
    )
    down_weight_part = jnp.einsum(
        "secd,sech->edh", slot_cotangent, hidden, preferred_element_type=jnp.float32
    )
    row_cotangent = jnp.einsum(
        "sech,edh->secd", gate_cotangent, weights[:, 0], preferred_element_type=jnp.float32
    ) + jnp.einsum(
        "sech,edh->secd", up_cotangent, weights[:, 1], preferred_element_type=jnp.float32
    )
    return (row_cotangent, jnp.stack([gate_weight_part, up_weight_part, down_weight_part], axis=1))


def shards(
    tokens,
    out_cotangent,
    assignment,
    norm_gains,
    attention_weights,
    router_weights,
    shared_weights,
    expert_weights,
):
    sequence_length = tokens.shape[0]
    width = tokens.shape[1]
    head_count = width // HEAD_SIZE
    outer_ranks = lax.axis_size("dp")
    local_experts = expert_weights.shape[0]
    experts_total = local_experts * outer_ranks
    capacity = sequence_length * 6 // experts_total
    slot_total = experts_total * capacity
    dense = (
        lax.all_gather(norm_gains, ("dp", "fsdp"), axis=0, tiled=True),
        lax.all_gather(attention_weights, ("dp", "fsdp"), axis=0, tiled=True),
        lax.all_gather(router_weights, ("dp", "fsdp"), axis=0, tiled=True),
        lax.all_gather(shared_weights, ("dp", "fsdp"), axis=0, tiled=True),
    )
    gain_full, attention_full, router_full, shared_full = dense
    tokens_float = tokens.astype(jnp.float32)
    gain_one = gain_full[:, 0].astype(jnp.float32)
    gain_two = gain_full[:, 1].astype(jnp.float32)
    normed_one, unit_one, root_one = norm_forward(tokens_float, gain_one)
    normed_one = normed_one.astype(jnp.bfloat16)
    projected = jnp.dot(
        normed_one,
        attention_full[:, :3, :].reshape(width, 3 * width),
        preferred_element_type=jnp.float32,
    )
    cosine_table, sine_table = rotary_tables(sequence_length)
    query_rows = rotate(
        projected[:, :width].reshape(sequence_length, head_count, HEAD_SIZE),
        cosine_table,
        sine_table,
    ).astype(jnp.bfloat16)
    rotated_key_rows = rotate(
        projected[:, width : 2 * width].reshape(sequence_length, head_count, HEAD_SIZE),
        cosine_table,
        sine_table,
    ).astype(jnp.bfloat16)
    value_rows_full = (
        projected[:, 2 * width :]
        .reshape(sequence_length, head_count, HEAD_SIZE)
        .astype(jnp.bfloat16)
    )
    score_scale = HEAD_SIZE ** (-0.5)
    causal = (jnp.arange(sequence_length)[:, None] >= jnp.arange(sequence_length)[None, :])[None]
    score_matrix = (
        jnp.einsum("jus,gus->ujg", query_rows, rotated_key_rows, preferred_element_type=jnp.float32)
        * score_scale
    )
    score_matrix = jnp.where(causal, score_matrix, MASKED)
    peak = jnp.max(score_matrix, axis=-1, keepdims=True)
    expo = jnp.exp(score_matrix - peak)
    totals = jnp.sum(expo, axis=-1, keepdims=True)
    log_total = peak + jnp.log(totals)
    attention_probability = (expo / totals).astype(jnp.bfloat16)
    blended_value_rows = (
        jnp.einsum(
            "lgv,vlp->glp",
            attention_probability,
            value_rows_full,
            preferred_element_type=jnp.float32,
        )
        .reshape(sequence_length, width)
        .astype(jnp.bfloat16)
    )
    hidden_res = tokens_float + jnp.dot(
        blended_value_rows, attention_full[:, 3, :], preferred_element_type=jnp.float32
    )
    normed_two, unit_two, root_two = norm_forward(hidden_res, gain_two)
    normed_two = normed_two.astype(jnp.bfloat16)
    shared_gate = jnp.dot(normed_two, shared_full[:, 0, :], preferred_element_type=jnp.float32)
    shared_up = jnp.dot(normed_two, shared_full[:, 1, :], preferred_element_type=jnp.float32)
    shared_active, shared_slope = silu_parts(shared_gate)
    shared_hidden = (shared_active * shared_up).astype(jnp.bfloat16)
    shared_out = jnp.dot(shared_hidden, shared_full[:, 2, :].T, preferred_element_type=jnp.float32)
    logits = jnp.dot(normed_two, router_full, preferred_element_type=jnp.float32)
    router_probability = jax.nn.softmax(logits, axis=-1)
    chooser = (assignment[:, :, None] == jnp.arange(experts_total)[None, None, :]).astype(
        jnp.float32
    )
    chosen = jnp.sum(chooser * router_probability[:, None, :], axis=-1)
    chosen_total = jnp.sum(chosen, axis=-1, keepdims=True)
    gates = chosen / chosen_total
    pair_count = sequence_length * TOPK
    flat_ids = assignment.reshape(pair_count)
    pair_onehot = (flat_ids[:, None] == jnp.arange(experts_total)[None, :]).astype(jnp.int32)
    earlier = jnp.cumsum(pair_onehot, axis=0) - pair_onehot
    rank = jnp.sum(earlier * pair_onehot, axis=1)
    kept = rank < capacity
    slot_index = jnp.where(kept, flat_ids * capacity + rank, slot_total)
    read_index = jnp.minimum(slot_index, slot_total - 1)
    token_of_pair = jnp.arange(pair_count) // TOPK
    send_rows = (
        jnp.zeros((slot_total, width), jnp.bfloat16)
        .at[slot_index]
        .set(normed_two[token_of_pair], mode="drop")
        .reshape(outer_ranks, local_experts, capacity, width)
    )
    slot_inputs = lax.all_to_all(send_rows, "dp", split_axis=0, concat_axis=0, tiled=True)
    expert_full = lax.all_gather(expert_weights, "fsdp", axis=3, tiled=True)
    slot_out = experts_forward(slot_inputs, expert_full)
    returned = lax.all_to_all(
        slot_out.astype(jnp.bfloat16), "dp", split_axis=0, concat_axis=0, tiled=True
    )
    pair_out = returned.reshape(slot_total, width)[read_index]
    pair_out = jnp.where(kept[:, None], pair_out.astype(jnp.float32), 0.0).reshape(
        sequence_length, TOPK, width
    )
    routed = jnp.sum(gates[:, :, None] * pair_out, axis=1)
    block_output = (hidden_res + shared_out + routed).astype(jnp.bfloat16)
    backward_dense = (
        lax.all_gather(norm_gains, ("dp", "fsdp"), axis=0, tiled=True),
        lax.all_gather(attention_weights, ("dp", "fsdp"), axis=0, tiled=True),
        lax.all_gather(router_weights, ("dp", "fsdp"), axis=0, tiled=True),
        lax.all_gather(shared_weights, ("dp", "fsdp"), axis=0, tiled=True),
    )
    attention_back, router_back, shared_back = (
        backward_dense[1],
        backward_dense[2],
        backward_dense[3],
    )
    cotangent = out_cotangent.astype(jnp.float32)
    gate_cot = jnp.sum(cotangent[:, None, :] * pair_out, axis=-1)
    pair_cot = (
        (gates[:, :, None] * cotangent[:, None, :]).astype(jnp.bfloat16).reshape(pair_count, width)
    )
    send_cot = (
        jnp.zeros((slot_total, width), jnp.bfloat16)
        .at[slot_index]
        .set(pair_cot, mode="drop")
        .reshape(outer_ranks, local_experts, capacity, width)
    )
    slot_cotangent = lax.all_to_all(send_cot, "dp", split_axis=0, concat_axis=0, tiled=True)
    expert_again = lax.all_gather(expert_weights, "fsdp", axis=3, tiled=True)
    slot_input_cot, expert_part = experts_backward(slot_inputs, slot_cotangent, expert_again)
    expert_gradient = lax.psum_scatter(
        expert_part.astype(jnp.bfloat16), "fsdp", scatter_dimension=3, tiled=True
    ).astype(jnp.float32)
    input_back = lax.all_to_all(
        slot_input_cot.astype(jnp.bfloat16), "dp", split_axis=0, concat_axis=0, tiled=True
    )
    pair_in = input_back.reshape(slot_total, width)[read_index]
    pair_in = jnp.where(kept[:, None], pair_in.astype(jnp.float32), 0.0).reshape(
        sequence_length, TOPK, width
    )
    normed_two_cot = jnp.sum(pair_in, axis=1)
    chosen_cot = gate_cot / chosen_total - jnp.sum(gate_cot * chosen, axis=-1, keepdims=True) / (
        chosen_total * chosen_total
    )
    prob_cot = jnp.sum(chooser * chosen_cot[:, :, None], axis=1)
    logit_cot = (
        router_probability
        * (prob_cot - jnp.sum(prob_cot * router_probability, axis=-1, keepdims=True))
    ).astype(jnp.bfloat16)
    router_gradient = jnp.dot(normed_two.T, logit_cot, preferred_element_type=jnp.float32)
    normed_two_cot = normed_two_cot + jnp.dot(
        logit_cot, router_back.T, preferred_element_type=jnp.float32
    )
    shared_hidden_cot = jnp.dot(
        out_cotangent, shared_back[:, 2, :], preferred_element_type=jnp.float32
    )
    shared_gate_cot = (shared_hidden_cot * shared_up * shared_slope).astype(jnp.bfloat16)
    shared_up_cot = (shared_hidden_cot * shared_active).astype(jnp.bfloat16)
    shared_gradient = jnp.stack(
        [
            jnp.dot(normed_two.T, shared_gate_cot, preferred_element_type=jnp.float32),
            jnp.dot(normed_two.T, shared_up_cot, preferred_element_type=jnp.float32),
            jnp.dot(out_cotangent.T, shared_hidden, preferred_element_type=jnp.float32),
        ],
        axis=1,
    )
    normed_two_cot = (
        normed_two_cot
        + jnp.dot(shared_gate_cot, shared_back[:, 0, :].T, preferred_element_type=jnp.float32)
        + jnp.dot(shared_up_cot, shared_back[:, 1, :].T, preferred_element_type=jnp.float32)
    )
    hidden_part, gain_two_grad = norm_backward(normed_two_cot, unit_two, root_two, gain_two)
    hidden_cot = cotangent + hidden_part
    attn_cot = hidden_cot.astype(jnp.bfloat16)
    output_proj_grad = jnp.dot(blended_value_rows.T, attn_cot, preferred_element_type=jnp.float32)
    mixed_cotangent = (
        jnp.dot(attn_cot, attention_back[:, 3, :].T, preferred_element_type=jnp.float32)
        .astype(jnp.bfloat16)
        .reshape(sequence_length, head_count, HEAD_SIZE)
    )
    scores_again = (
        jnp.einsum("jus,gus->ujg", query_rows, rotated_key_rows, preferred_element_type=jnp.float32)
        * score_scale
    )
    prob_float = jnp.exp(jnp.where(causal, scores_again, MASKED) - log_total)
    probability_reduced = prob_float.astype(jnp.bfloat16)
    value_cotangent = jnp.einsum(
        "tae,atn->etn", probability_reduced, mixed_cotangent, preferred_element_type=jnp.float32
    )
    attn_prob_cot = jnp.einsum(
        "jus,gus->ujg", mixed_cotangent, value_rows_full, preferred_element_type=jnp.float32
    )
    row_dot = jnp.sum(prob_float * attn_prob_cot, axis=-1, keepdims=True)
    score_cotangent = (prob_float * (attn_prob_cot - row_dot)).astype(jnp.bfloat16)
    query_cot = (
        jnp.einsum(
            "lgv,vlp->glp", score_cotangent, rotated_key_rows, preferred_element_type=jnp.float32
        )
        * score_scale
    )
    key_cot = (
        jnp.einsum("tae,atn->etn", score_cotangent, query_rows, preferred_element_type=jnp.float32)
        * score_scale
    )
    projected_cot = jnp.concatenate(
        [
            unrotate(query_cot, cosine_table, sine_table)
            .reshape(sequence_length, width)
            .astype(jnp.bfloat16),
            unrotate(key_cot, cosine_table, sine_table)
            .reshape(sequence_length, width)
            .astype(jnp.bfloat16),
            value_cotangent.reshape(sequence_length, width).astype(jnp.bfloat16),
        ],
        axis=1,
    )
    input_proj_grad = jnp.dot(
        normed_one.T, projected_cot, preferred_element_type=jnp.float32
    ).reshape(width, 3, width)
    normed_one_cot = jnp.dot(
        projected_cot,
        attention_back[:, :3, :].reshape(width, 3 * width).T,
        preferred_element_type=jnp.float32,
    )
    token_part, gain_one_grad = norm_backward(normed_one_cot, unit_one, root_one, gain_one)
    token_gradient = hidden_cot + token_part
    attention_grad = jnp.concatenate([input_proj_grad, output_proj_grad[:, None, :]], axis=1)
    gains_grad = jnp.stack([gain_one_grad, gain_two_grad], axis=1)
    gain_gradient, attention_gradient, router_gradient, shared_gradient = (
        lax.psum_scatter(gains_grad, ("dp", "fsdp"), scatter_dimension=0, tiled=True),
        lax.psum_scatter(attention_grad, ("dp", "fsdp"), scatter_dimension=0, tiled=True),
        lax.psum_scatter(router_gradient, ("dp", "fsdp"), scatter_dimension=0, tiled=True),
        lax.psum_scatter(shared_gradient, ("dp", "fsdp"), scatter_dimension=0, tiled=True),
    )
    return (
        block_output,
        token_gradient,
        gain_gradient,
        attention_gradient,
        router_gradient,
        shared_gradient,
        expert_gradient,
    )


def solution(mesh):
    return jax.shard_map(
        shards,
        mesh=mesh,
        in_specs=(
            P(("dp", "fsdp"), None),
            P(("dp", "fsdp"), None),
            P(("dp", "fsdp"), None),
            P(("dp", "fsdp"), None),
            P(("dp", "fsdp"), None, None),
            P(("dp", "fsdp"), None),
            P(("dp", "fsdp"), None, None),
            P("dp", None, None, "fsdp"),
        ),
        out_specs=(
            P(("dp", "fsdp"), None),
            P(("dp", "fsdp"), None),
            P(("dp", "fsdp"), None),
            P(("dp", "fsdp"), None, None),
            P(("dp", "fsdp"), None),
            P(("dp", "fsdp"), None, None),
            P("dp", None, None, "fsdp"),
        ),
        check_vma=False,
    )
```

profile of v0, /device:TPU:0, one launch (start us, length us, event | category | flops | bytes accessed | tf_op | source)
XLA Modules:
  0.0 1793.6 jit_solution(2853201655373087863)
XLA Ops:
  10.0 70.0 %all-gather = bf16[32,40,2]{1,2,0:T(2,128)(2,1)S(1)} all-gather(bf16[1,40,2]{1,2,0:T(2,128)(2,1)} %bitcast.230), channel_id=1, replica_groups=mesh['dp'=8,'fsdp'=4] {'dp','fsdp'}, dimensions={0}, use_global_device_ids=true | all-gather | bytes 5280 | tf_op jit(solution)/shard_map/all_gather | solution.py:129
  80.1 65.0 %all-gather.1 = bf16[32,40,16]{1,2,0:T(8,128)(2,1)S(1)} all-gather(bf16[1,40,16]{1,2,0:T(8,128)(2,1)} %bitcast.229), channel_id=1, replica_groups=mesh['dp'=8,'fsdp'=4] {'dp','fsdp'}, dimensions={0}, use_global_device_ids=true | all-gather | bytes 42240 | tf_op jit(solution)/shard_map/all_gather | solution.py:131
  158.7 19.5 %mul.559 = f32[3584,1280]{1,0:T(8,128)} reshape(f32[512,7,1280]{2,1,0:T(8,128)} %mul.558) | data formatting | bytes 36700160 | tf_op jit(solution)/shard_map/mul | solution.py:242
  180.8 20.0 %copy.191 = bf16[1280,3,1280]{0,2,1:T(8,128)(2,1)} copy(bf16[1280,3,1280]{2,1,0:T(4,128)(2,1)} %bitcast.207) | data formatting | bytes 19660800
  268.1 23.9 %scatter_custom_fusion.1 = bf16[3072,1280]{1,0:T(8,128)(2,1)} fusion(s32[3584]{0:T(1024)S(1)} %get-tuple-element.44, f32[3584,1280]{1,0:T(8,128)} %mul.559, f32[3584]{0:T(1024)S(1)} %div.93, bf16[]{:T(256)} %constant.48.clone.1), kind=kCustom, calls=%fused_computation.35 | custom fusion | flops 9175040 | bytes 26230786 | tf_op jit(solution)/shard_map/scatter | solution.py:247
  304.4 52.8 %scatter_custom_fusion = bf16[3072,1280]{1,0:T(8,128)(2,1)} fusion(s32[3584]{0:T(1024)S(1)} %get-tuple-element.44, bf16[512,1280]{1,0:T(8,128)(2,1)S(1)} %multiply_convert_fusion.3, s32[4096]{0:T(1024)S(1)} %pad_clamp_fusion.1, bf16[]{:T(256)} %constant.48.clone.1), kind=kCustom, calls=%fused_computation.39 | custom fusion | bytes 7864322 | tf_op jit(solution)/shard_map/scatter | solution.py:213
  357.2 112.4 %all-to-all-done.2 = bf16[8,2,192,1280]{3,2,1,0:T(8,128)(2,1)} async-done(((bf16[8,2,192,1280]{3,2,1,0:T(8,128)(2,1)}), bf16[8,2,192,1280]{3,2,1,0:T(8,128)(2,1)}, u32[]{:S(2)}, u32[]{:S(2)}) %all-to-all-start.2) | async-done | bytes 7864352 | tf_op jit(solution)/shard_map/all_to_all | solution.py:250
  474.8 12.4 fusion.95
  487.1 13.7 copy.199
  500.8 13.6 copy.197
  514.4 13.6 copy.198
  528.0 14.3 fusion.15
  542.3 105.1 %all-to-all-done = bf16[8,2,192,1280]{3,2,1,0:T(8,128)(2,1)} async-done(((bf16[8,2,192,1280]{3,2,1,0:T(8,128)(2,1)}), bf16[8,2,192,1280]{3,2,1,0:T(8,128)(2,1)}, u32[]{:S(2)}, u32[]{:S(2)}) %all-to-all-start) | async-done | bytes 7864352 | tf_op jit(solution)/shard_map/all_to_all | solution.py:216
  647.4 14.3 fusion.19
  661.7 21.8 %fusion.3 = (bf16[8,2,192,896]{3,2,0,1:T(8,128)(2,1)}, bf16[8,2,192,896]{3,2,0,1:T(8,128)(2,1)}, bf16[8,2,192,896]{3,2,0,1:T(8,128)(2,1)}) fusion(f32[2,8,192,896]{3,2,1,0:T(8,128)} %fusion.19, f32[2,8,192,896]{3,2,1,0:T(8,128)} %fusion.15, bf16[2,1,1280,896]{3,2,0,1:T(8,128)(2,1)} %copy.198, bf16[8,2,192,1280]{3,2,1,0:T(8,128)(2,1)} %all-to-all-done), kind=kOutput, calls=%fused_computation.19 | convolution fusion | flops 7087718400 | bytes 50987008 | tf_op jit(solution)/shard_map/secd,edh->sech/dot_general | solution.py:71
  683.5 14.0 convert_bitcast_fusion
  710.1 14.8 fusion.31
  724.9 15.9 fusion.24
  747.8 166.8 %all-to-all-done.1 = bf16[8,2,192,1280]{3,2,1,0:T(8,128)(2,1)} async-done(((bf16[8,2,192,1280]{3,2,1,0:T(8,128)(2,1)}), bf16[8,2,192,1280]{3,2,1,0:T(8,128)(2,1)}, u32[]{:S(2)}, u32[]{:S(2)}) %all-to-all-start.1) | async-done | bytes 7864352 | tf_op jit(solution)/shard_map/all_to_all | solution.py:219
  946.6 12.4 fusion.36
  976.7 38.5 %copy.170 = bf16[2,3,1280,896]{2,0,1,3:T(2,128)(2,1)} copy(bf16[2,3,1280,896]{3,2,0,1:T(8,128)(2,1)} %pad_maximum_fusion.2) | data formatting | bytes 27525120 | tf_op jit(solution)/shard_map/stack | solution.py:107
  1015.4 23.8 %gather_fusion = bf16[3584,1280]{1,0:T(8,128)(2,1)} fusion(bf16[3072,1280]{1,0:T(8,128)(2,1)} %bitcast.26, s32[4096]{0:T(1024)S(1)} %pad_clamp_fusion), kind=kCustom, calls=%fused_computation.1 | custom fusion | bytes 18364416 | tf_op jit(solution)/shard_map/gather | solution.py:222
  1039.2 15.5 reshape.407
  1066.3 25.9 %all-to-all-done.3 = bf16[8,2,192,1280]{3,2,1,0:T(8,128)(2,1)} async-done(((bf16[8,2,192,1280]{3,2,1,0:T(8,128)(2,1)}), bf16[8,2,192,1280]{3,2,1,0:T(8,128)(2,1)}, u32[]{:S(2)}, u32[]{:S(2)}) %all-to-all-start.3) | async-done | bytes 7864352 | tf_op jit(solution)/shard_map/all_to_all | solution.py:256
  1092.2 23.5 %gather_fusion.1 = bf16[3584,1280]{1,0:T(8,128)(2,1)} fusion(bf16[3072,1280]{1,0:T(8,128)(2,1)} %bitcast.33, s32[4096]{0:T(1024)S(1)} %pad_clamp_fusion), kind=kCustom, calls=%fused_computation.2 | custom fusion | bytes 18364416 | tf_op jit(solution)/shard_map/gather | solution.py:259
  1115.7 15.4 reshape.408
  1131.2 37.4 %select_reduce_fusion = (f32[512,1280]{1,0:T(8,128)S(1)}, f32[512,1280]{1,0:T(8,128)}) fusion(f32[512,7,1280]{2,1,0:T(8,128)} %reshape.408, pred[512,7]{1,0:T(8,128)(4,1)S(1)} %copy-done.47, f32[512,7,1280]{2,1,0:T(8,128)} %reshape.407, f32[512,7]{1,0:T(8,128)S(1)} %copy-done.36), kind=kLoop, calls=%fused_computation.6 | loop fusion | flops 21626880 | bytes 41960960 | tf_op jit(solution)/shard_map/reduce_sum | solution.py:263
  1229.9 11.7 pad_maximum_fusion
  1241.6 31.3 %copy.165 = f32[1280,4,1280]{2,1,0:T(4,128)} copy(f32[1280,4,1280]{0,2,1:T(8,128)} %pad_maximum_fusion) | data formatting | bytes 52428800 | tf_op jit(solution)/shard_map/concatenate | solution.py:349
  1286.1 12.1 pad_maximum_fusion.1
  1320.9 40.4 %all-reduce = f32[1280,2]{0,1:T(2,128)S(1)} all-reduce(f32[1280,2]{0,1:T(2,128)S(1)} %pad_maximum_fusion.14), channel_id=2, replica_groups=mesh['dp'=8,'fsdp'=4] {'dp','fsdp'}, use_global_device_ids=true, to_apply=%region_24.25.clone | all-reduce | flops 2560 | bytes 20480
  1369.7 413.0 %all-reduce.10.cloned.1.call-done = (f32[1280,4,1280]{2,1,0:T(4,128)}, f32[1280,16]{0,1:T(8,128)}) async-done(((f32[1280,4,1280]{2,1,0:T(4,128)}, f32[1280,16]{0,1:T(8,128)}), (f32[1280,4,1280]{2,1,0:T(4,128)}, f32[1280,16]{0,1:T(8,128)})) %all-reduce.10.cloned.1.call-update) | async-done | bytes 26296336
  (325 shorter events, 291.6 us)
Async XLA Ops:
  8.0 142.7 %copy-start.48 = (s32[512,7]{0,1:T(8,128)S(1)}, s32[512,7]{0,1:T(8,128)}, u32[]{:S(2)}) copy-start(s32[512,7]{0,1:T(8,128)} %param.10) | copy-start | bytes 43012
  8.0 143.1 %copy-start.24 = (bf16[512,1280]{1,0:T(8,128)(2,1)S(1)}, bf16[512,1280]{1,0:T(8,128)(2,1)}, u32[]{:S(2)}) copy-start(bf16[512,1280]{1,0:T(8,128)(2,1)} %param.9) | copy-start | bytes 3932164
  8.0 172.8 %all-gather.6.cloned.1.call-start = ((), (), s32[]{:S(2)}) async-start(), calls=%async_computation.5 | async-start | bytes 13516800 | tf_op jit(solution)/shard_map/all_gather | solution.py:130
  145.4 120.4 %copy-start.43 = (bf16[1280,16]{0,1:T(8,128)(2,1)}, bf16[1280,16]{0,1:T(8,128)(2,1)S(1)}, u32[]{:S(2)}) copy-start(bf16[1280,16]{0,1:T(8,128)(2,1)S(1)} %reshape.452) | copy-start | bytes 122884
  178.3 86.6 %copy-start.56 = (f32[1280]{0:T(1024)}, f32[1280]{0:T(1024)S(1)}, u32[]{:S(2)}) copy-start(f32[1280]{0:T(1024)S(1)} %get-tuple-element.45) | copy-start | bytes 15364
  180.8 56.5 %copy-start.31 = (f32[512,64]{1,0:T(8,128)}, f32[512,64]{1,0:T(8,128)S(1)}, u32[]{:S(2)}) copy-start(f32[512,64]{1,0:T(8,128)S(1)} %get-tuple-element.76) | copy-start | bytes 393220
  180.8 56.5 %copy-start.33 = (f32[512,64]{1,0:T(8,128)}, f32[512,64]{1,0:T(8,128)S(1)}, u32[]{:S(2)}) copy-start(f32[512,64]{1,0:T(8,128)S(1)} %get-tuple-element.77) | copy-start | bytes 393220
  265.8 660.6 %copy-start.4 = (bf16[512,1280]{1,0:T(8,128)(2,1)}, bf16[512,1280]{1,0:T(8,128)(2,1)S(1)}, u32[]{:S(2)}) copy-start(bf16[512,1280]{1,0:T(8,128)(2,1)S(1)} %multiply_convert_fusion.3) | copy-start | bytes 3932164
  267.9 24.1 %copy-start.35 = (f32[512,7]{1,0:T(8,128)}, f32[512,7]{1,0:T(8,128)S(1)}, u32[]{:S(2)}) copy-start(f32[512,7]{1,0:T(8,128)S(1)} %copy.135) | copy-start | bytes 43012
  292.0 177.6 %all-to-all-start.2 = ((bf16[8,2,192,1280]{3,2,1,0:T(8,128)(2,1)}), bf16[8,2,192,1280]{3,2,1,0:T(8,128)(2,1)}, u32[]{:S(2)}, u32[]{:S(2)}) async-start(bf16[8,2,192,1280]{3,2,1,0:T(8,128)(2,1)} %bitcast.206), calls=%async_computation.2 | async-start | bytes 15728640 | tf_op jit(solution)/shard_map/all_to_all | solution.py:250
  296.9 177.8 %all-gather.10.cloned.1.call-start = ((), (), s32[]{:S(2)}) async-start(), calls=%async_computation.7 | async-start | bytes 17203200 | tf_op jit(solution)/shard_map/all_gather | solution.py:217
  469.6 177.8 %all-to-all-start = ((bf16[8,2,192,1280]{3,2,1,0:T(8,128)(2,1)}), bf16[8,2,192,1280]{3,2,1,0:T(8,128)(2,1)}, u32[]{:S(2)}, u32[]{:S(2)}) async-start(bf16[8,2,192,1280]{3,2,1,0:T(8,128)(2,1)} %bitcast.205), calls=%async_computation | async-start | bytes 15728640 | tf_op jit(solution)/shard_map/all_to_all | solution.py:216
  704.5 210.1 %all-to-all-start.1 = ((bf16[8,2,192,1280]{3,2,1,0:T(8,128)(2,1)}), bf16[8,2,192,1280]{3,2,1,0:T(8,128)(2,1)}, u32[]{:S(2)}, u32[]{:S(2)}) async-start(bf16[8,2,192,1280]{3,2,1,0:T(8,128)(2,1)} %copy.145), calls=%async_computation.1 | async-start | bytes 15728640 | tf_op jit(solution)/shard_map/all_to_all | solution.py:219
  709.4 211.4 %all-gather.8.cloned.1.call-start = ((), (), s32[]{:S(2)}) async-start(), calls=%async_computation.6 | async-start | bytes 7096320 | tf_op jit(solution)/shard_map/all_gather | solution.py:132
  747.8 172.0 %copy-start.51 = (s32[3584]{0:T(1024)S(1)}, s32[3584]{0:T(1024)}, u32[]{:S(2)}) copy-start(s32[3584]{0:T(1024)} %copy-done.50) | copy-start | bytes 43012
  747.8 172.9 %copy-start.58 = (s32[3584]{0:T(1024)S(1)}, s32[3584]{0:T(1024)}, u32[]{:S(2)}) copy-start(s32[3584]{0:T(1024)} %get-tuple-element.43) | copy-start | bytes 43012
  747.8 173.0 %copy-start.25 = (bf16[512,1280]{1,0:T(8,128)(2,1)S(1)}, bf16[512,1280]{1,0:T(8,128)(2,1)}, u32[]{:S(2)}) copy-start(bf16[512,1280]{1,0:T(8,128)(2,1)} %param.9) | copy-start | bytes 3932164
  914.6 177.6 %all-to-all-start.3 = ((bf16[8,2,192,1280]{3,2,1,0:T(8,128)(2,1)}), bf16[8,2,192,1280]{3,2,1,0:T(8,128)(2,1)}, u32[]{:S(2)}, u32[]{:S(2)}) async-start(bf16[8,2,192,1280]{3,2,1,0:T(8,128)(2,1)} %copy.148), calls=%async_computation.3 | async-start | bytes 15728640 | tf_op jit(solution)/shard_map/all_to_all | solution.py:256
  919.6 380.5 %all-reduce.8.cloned.1.call-start = ((), (), s32[]{:S(2)}) async-start(), calls=%async_computation.9 | async-start | bytes 27525120
  935.6 23.5 %slice-start.9 = ((s8[5505024]{0:T(1024)(128)(4,1)}), s8[4194304]{0:T(1024)(128)(4,1)S(1)}, s32[]{:S(2)}) async-start(s8[5505024]{0:T(1024)(128)(4,1)} %bitcast.233), calls=%async_computation.20 | async-start | bytes 8388608
  1015.3 767.3 %all-reduce.10.cloned.1.call-start = ((), (), s32[]{:S(2)}) async-start(), calls=%async_computation.10 | async-start | bytes 52592640
  1115.7 56.5 %slice-start.7 = ((s8[6553600]{0:T(1024)(128)(4,1)}), s8[2359296]{0:T(1024)(128)(4,1)S(1)}, s32[]{:S(2)}) async-start(s8[6553600]{0:T(1024)(128)(4,1)} %bitcast.217), calls=%async_computation.18 | async-start | bytes 4718592
  1131.2 37.4 %copy-start.2 = (f32[512,1280]{1,0:T(8,128)S(1)}, f32[512,1280]{1,0:T(8,128)}, u32[]{:S(2)}) copy-start(f32[512,1280]{1,0:T(8,128)} %copy-done.1) | copy-start | bytes 7864324
  1131.2 37.4 %copy-start.29 = (f32[512,1280]{1,0:T(8,128)S(1)}, f32[512,1280]{1,0:T(8,128)}, u32[]{:S(2)}) copy-start(f32[512,1280]{1,0:T(8,128)} %fusion.62) | copy-start | bytes 7864324
  1131.2 37.4 %copy-start.30 = (f32[512,1280]{1,0:T(8,128)S(1)}, f32[512,1280]{1,0:T(8,128)}, u32[]{:S(2)}) copy-start(f32[512,1280]{1,0:T(8,128)} %fusion.64) | copy-start | bytes 7864324
  1131.2 37.4 %copy-start.44 = (bf16[1280,16]{0,1:T(8,128)(2,1)S(1)}, bf16[1280,16]{0,1:T(8,128)(2,1)}, u32[]{:S(2)}) copy-start(bf16[1280,16]{0,1:T(8,128)(2,1)} %copy-done.43) | copy-start | bytes 122884
  1131.2 37.4 %copy-start.57 = (f32[1280]{0:T(1024)S(1)}, f32[1280]{0:T(1024)}, u32[]{:S(2)}) copy-start(f32[1280]{0:T(1024)} %copy-done.56) | copy-start | bytes 15364
  1131.2 37.4 %copy-start.70 = (f32[512]{0:T(512)S(1)}, f32[512]{0:T(512)}, u32[]{:S(2)}) copy-start(f32[512]{0:T(512)} %copy-done.69) | copy-start | bytes 6148
  1131.2 41.0 %slice-start.8 = ((s8[6553600]{0:T(1024)(128)(4,1)}), s8[4194304]{0:T(1024)(128)(4,1)S(1)}, s32[]{:S(2)}) async-start(s8[6553600]{0:T(1024)(128)(4,1)} %bitcast.217), calls=%async_computation.19 | async-start | bytes 8388608
  1241.6 31.3 %copy-start.5 = (bf16[512,1280]{1,0:T(8,128)(2,1)S(1)}, bf16[512,1280]{1,0:T(8,128)(2,1)}, u32[]{:S(2)}) copy-start(bf16[512,1280]{1,0:T(8,128)(2,1)} %copy-done.4) | copy-start | bytes 3932164
  1273.9 512.2 %reduce-scatter.4.cloned.1.call-start = ((), (), s32[]{:S(2)}) async-start(), calls=%async_computation.8 | async-start | bytes 14192640 | tf_op jit(solution)/shard_map/reduce_scatter | solution.py:355
  1309.3 52.6 %copy-start.3 = (f32[512,1280]{1,0:T(8,128)S(1)}, f32[512,1280]{1,0:T(8,128)}, u32[]{:S(2)}) copy-start(f32[512,1280]{1,0:T(8,128)} %copy-done.1) | copy-start | bytes 7864324
  (72 other events, 450.6 us)
Sparse Core Ops, SparseCore 0:
  11.7 102.5 all-gather.5
  713.1 113.2 all-gather.7
  1298.3 406.5 reduce-scatter.3
Sparse Core Ops, SparseCore 1:
  304.3 133.3 all-gather.9
  1015.4 259.5 all-reduce.7
  1281.8 500.8 all-reduce.9
where the time goes:
time: 1810 us; the launch traced here: 1790 us
  waiting for transfers between devices  825 us (46%)
  local copies, waits for them, and re-layouts  388 us (21%)
  matrix products  232 us (13%)
  blocking collectives  175 us (10%)
  other arithmetic  135 us (7%)
  starting transfers between devices  20.7 us (1%)
    unnamed x8, waiting for transfers between devices  414 us
    all_to_all x1, waiting for transfers between devices, shards(): lax.all_to_all(slot_out.astype(jnp.bfloat16), 'dp', split_axis=0, concat_...  167 us
    all_to_all x1, waiting for transfers between devices, shards(): lax.all_to_all(send_cot, 'dp', split_axis=0, concat_axis=0, tiled=True)  112 us
    all_to_all x1, waiting for transfers between devices, shards(): lax.all_to_all(send_rows, 'dp', split_axis=0, concat_axis=0, tiled=True)  105 us
    unnamed x205, local copies, waits for them, and re-layouts  101 us
    all_gather x1, blocking collectives, shards(): lax.all_gather(norm_gains, ('dp', 'fsdp'), axis=0, tiled=True)  70 us
    all_gather x1, blocking collectives, shards(): lax.all_gather(router_weights, ('dp', 'fsdp'), axis=0, tiled=True)  65 us
    scatter x1, local copies, waits for them, and re-layouts, shards(): send_rows = jnp.zeros((slot_total, width), jnp.bfloat16).at[slot_index].s...  52.8 us
  transfers between devices with their start and end apart: 10, of which 5 were waited for; matrix products, arithmetic and copies ran while one was open for 32% of the time, Pallas kernels for 0%

commit v1 on v0

v1 whole, which is shorter than its diff:
```python
import jax
import jax.numpy as jnp
from jax import lax
from jax.experimental import pallas as pl
from jax.experimental.pallas import tpu as pltpu
from jax.sharding import PartitionSpec as P

HEAD_SIZE = 128
TOPK = 7
EPSILON = 1e-06
MASKED = -1e30
LANES = 128
F32 = jnp.float32
BF16 = jnp.bfloat16
VMEM_LIMIT = 58 * 1024 * 1024


def after(value, *others):
    return lax.optimization_barrier((value, *others))[0]


def core_swap(x):
    return lax.ppermute(x, "dp", [(d, d ^ 1) for d in range(lax.axis_size("dp"))])


def fsdp_swap(x, bit):
    return lax.ppermute(x, "fsdp", [(f, f ^ bit) for f in range(lax.axis_size("fsdp"))])


def line_send(x, step, first, last):
    pairs = [(2 * p + c, 2 * (p + step) + c) for p in range(first, last + 1) for c in range(2)]
    return lax.ppermute(x, "dp", pairs)


def line_gather(x):
    n = lax.axis_size("dp") // 2
    p = lax.axis_index("dp") // 2
    right, left = [x], [x]
    for s in range(1, n):
        a = line_send(right[-1], 1, s - 1, n - 2)
        b = line_send(left[-1], -1, 1, n - s)
        a, b = lax.optimization_barrier((a, b))
        right.append(a)
        left.append(b)
    return [x] + [jnp.where(p + r < n, left[r], right[n - r]) for r in range(1, n)]


def line_scatter(slots, kind=BF16):
    n = len(slots)
    right = left = None
    for s in range(1, n):
        a, b = slots[n - s].astype(F32), slots[s].astype(F32)
        if right is not None:
            a, b = a + right.astype(F32), b + left.astype(F32)
        right = line_send(a.astype(kind), 1, 0, s - 1)
        left = line_send(b.astype(kind), -1, n - s, n - 1)
        right, left = lax.optimization_barrier((right, left))
    total = slots[0].astype(F32)
    return total if right is None else total + right.astype(F32) + left.astype(F32)


def cube_size():
    return max(lax.axis_size("fsdp").bit_length() - 1, 1)


def cube_masks(part):
    k = cube_size()
    masks = [0]
    for j in range(k):
        masks = masks + [m ^ (1 << ((part + j) % k)) for m in masks]
    return masks


def cube_gather(x, part):
    k = cube_size()
    known = [x]
    for j in range(k):
        known = known + [fsdp_swap(a, 1 << ((part + j) % k)) for a in known]
    return known


def cube_scatter(x, part, kind=BF16):
    k = cube_size()
    for j in reversed(range(k)):
        half = x.shape[0] // 2
        got = fsdp_swap(x[half:].astype(kind), 1 << ((part + j) % k))
        x = x[:half].astype(F32) + got.astype(F32)
    return x.astype(F32)


def dense_gather(w):
    slots = line_gather(w)
    own = []
    for part in range(cube_size()):
        own += cube_gather(jnp.concatenate(slots[part :: cube_size()], axis=0), part)
    return own + [core_swap(a) for a in own], slots


def block_order():
    n = lax.axis_size("dp") // 2
    d, f = lax.axis_index("dp"), lax.axis_index("fsdp")
    order = []
    for cx in range(2):
        for part in range(cube_size()):
            for m in cube_masks(part):
                for r in range(n)[part :: cube_size()]:
                    device = ((d // 2 + r) % n) * 2 + (d % 2 ^ cx)
                    order.append(device * lax.axis_size("fsdp") + (f ^ m))
    return jnp.stack(order)


def dense_scatter(own, other, kind=BF16):
    n = lax.axis_size("dp") // 2
    k = cube_size()
    total = own.astype(F32) + core_swap(other.astype(kind)).astype(F32)
    rows = total.shape[0] // (n * 2**k)
    slots = [None] * n
    at = 0
    for part in range(k):
        mine = range(n)[part::k]
        size = 2**k * len(mine) * rows
        got = cube_scatter(total[at : at + size], part, kind)
        at += size
        for i, r in enumerate(mine):
            slots[r] = got[i * rows : (i + 1) * rows]
    return line_scatter(slots, kind)


def token_gather(x):
    return [(a, core_swap(a)) for a in line_gather(x)]


def token_scatter(pairs):
    return line_scatter([a.astype(F32) + core_swap(b).astype(F32) for a, b in pairs])


def dot(a, b, dims):
    return lax.dot_general(a, b, (dims, ((), ())), preferred_element_type=F32)


NN = ((1,), (0,))
NT = ((1,), (1,))
TN = ((0,), (0,))


def turn(x, cosine, sine):
    return x * cosine + pltpu.roll(x, HEAD_SIZE // 2, 1) * sine


def causal_scores(q, k):
    scores = dot(k, q, NT) * (HEAD_SIZE ** (-0.5))
    key = lax.broadcasted_iota(jnp.int32, scores.shape, 0)
    query = lax.broadcasted_iota(jnp.int32, scores.shape, 1)
    return jnp.where(key <= query, scores, MASKED)


def attention_forward_kernel(qp, kp, vp, cosine, sine, q_out, k_out, v_out, mixed_out, lse_out):
    q = turn(qp[...], cosine[...], sine[...]).astype(BF16)
    k = turn(kp[...], cosine[...], sine[...]).astype(BF16)
    v = vp[...].astype(BF16)
    q_out[...] = q
    k_out[...] = k
    v_out[...] = v
    scores = causal_scores(q, k)
    peak = jnp.max(scores, axis=0, keepdims=True)
    expo = jnp.exp(scores - peak)
    totals = jnp.sum(expo, axis=0, keepdims=True)
    lse_out[0] = peak + jnp.log(totals)
    probability = (expo * (1.0 / totals)).astype(BF16)
    mixed_out[...] = dot(probability, v, TN).astype(BF16)


def attention_forward(projected, cosine, sine):
    length = projected.shape[0]
    width = projected.shape[1] // 3
    heads = width // HEAD_SIZE
    block = (length, HEAD_SIZE)
    table = pl.BlockSpec(block, lambda h: (0, 0))
    column = pl.BlockSpec(block, lambda h: (0, h))
    rows = jax.ShapeDtypeStruct((length, width), BF16)
    return pl.pallas_call(
        attention_forward_kernel,
        grid=(heads,),
        in_specs=[
            column,
            pl.BlockSpec(block, lambda h: (0, heads + h)),
            pl.BlockSpec(block, lambda h: (0, 2 * heads + h)),
            table,
            table,
        ],
        out_specs=[column] * 4 + [pl.BlockSpec((1, 1, length), lambda h: (h, 0, 0))],
        out_shape=[rows] * 4 + [jax.ShapeDtypeStruct((heads, 1, length), F32)],
        compiler_params=pltpu.CompilerParams(vmem_limit_bytes=VMEM_LIMIT),
        name="attention_forward",
    )(projected, projected, projected, cosine, sine)


def attention_backward_kernel(q_in, k_in, v_in, d_in, lse, cosine, sine, dq_out, dk_out, dv_out):
    q, k, v, d = q_in[...], k_in[...], v_in[...], d_in[...]
    scale = HEAD_SIZE ** (-0.5)
    probability = jnp.exp(causal_scores(q, k) - lse[0])
    dv_out[...] = dot(probability.astype(BF16), d, NN).astype(BF16)
    prob_cot = dot(v, d, NT)
    row_dot = jnp.sum(probability * prob_cot, axis=0, keepdims=True)
    score_cot = (probability * (prob_cot - row_dot)).astype(BF16)
    dk = dot(score_cot, q, NN) * scale
    dq = dot(score_cot, k, TN) * scale
    dq_out[...] = turn(dq, cosine[...], -sine[...]).astype(BF16)
    dk_out[...] = turn(dk, cosine[...], -sine[...]).astype(BF16)


def attention_backward(q, k, v, mixed_cot, lse, cosine, sine):
    length, width = q.shape
    heads = width // HEAD_SIZE
    block = (length, HEAD_SIZE)
    table = pl.BlockSpec(block, lambda h: (0, 0))
    column = pl.BlockSpec(block, lambda h: (0, h))
    return pl.pallas_call(
        attention_backward_kernel,
        grid=(heads,),
        in_specs=[column] * 4
        + [pl.BlockSpec((1, 1, length), lambda h: (h, 0, 0)), table, table],
        out_specs=[column] * 3,
        out_shape=[jax.ShapeDtypeStruct((length, width), BF16)] * 3,
        compiler_params=pltpu.CompilerParams(vmem_limit_bytes=VMEM_LIMIT),
        name="attention_backward",
    )(q, k, v, mixed_cot, lse, cosine, sine)


def silu_parts(gate_value):
    sigmoid_value = jax.nn.sigmoid(gate_value)
    return (gate_value * sigmoid_value, sigmoid_value * (1.0 + gate_value * (1.0 - sigmoid_value)))


def expert_kernel(
    first, x_own, x_other, c_own, c_other, router, weights,
    x_out, c_out, h_out, g_out, u_out, cot_own, cot_other, out_own, out_other, router_out,
    cot_scratch, out_scratch, router_scratch,
):
    length, width = x_own.shape
    capacity = x_out.shape[1] // 2
    experts = router.shape[0]
    local = pl.num_programs(0)
    step = pl.program_id(0)
    sources = ((x_own, c_own), (x_other, c_other))

    @pl.when(step == 0)
    def _():
        cot_scratch[...] = jnp.zeros_like(cot_scratch)
        out_scratch[...] = jnp.zeros_like(out_scratch)
        router_scratch[...] = jnp.zeros_like(router_scratch)

    wanted = first[0] + step
    expert_row = lax.broadcasted_iota(jnp.int32, (experts, length), 0)
    slot_row = lax.broadcasted_iota(jnp.int32, (capacity, length), 0).astype(F32)
    picks, gate_columns, tables = [], [], []
    for at, (x_ref, c_ref) in enumerate(sources):
        x = x_ref[...]
        ranks = c_ref[length : length + experts, :length].astype(F32)
        rank = jnp.sum(jnp.where(expert_row == wanted, ranks, 0.0), axis=0, keepdims=True)
        pick = jnp.where(slot_row == rank, 1.0, 0.0)
        logits = dot(router[...], x, NT)
        expo = jnp.exp(logits - jnp.max(logits, axis=0, keepdims=True))
        probability = expo * (1.0 / jnp.sum(expo, axis=0, keepdims=True))
        chosen = jnp.where(ranks >= 0.0, probability, 0.0)
        chosen_total = jnp.sum(chosen, axis=0, keepdims=True)
        mine = jnp.sum(jnp.where(expert_row == wanted, chosen, 0.0), axis=0, keepdims=True)
        gate = mine / chosen_total
        gate_columns.append(jnp.sum(pick * gate, axis=1, keepdims=True))
        pick16 = pick.astype(BF16)
        picks.append(pick16)
        tables.append((ranks, probability, chosen, chosen_total, mine))
        low, high = at * capacity, (at + 1) * capacity
        x_out[0, low:high, :] = dot(pick16, x, NN).astype(BF16)
        c_out[0, low:high, :] = dot(pick16, c_ref[:length, :], NN).astype(BF16)
    gates = jnp.concatenate(gate_columns, axis=0)
    x = x_out[0]
    c = c_out[0]
    gate_value = dot(x, weights[0, 0], NT)
    up_value = dot(x, weights[0, 1], NT)
    active, slope = silu_parts(gate_value)
    hidden = active * up_value
    raw_cot = dot(c, weights[0, 2], NT)
    hidden16 = hidden.astype(BF16)
    gate_cot = jnp.sum(raw_cot * hidden16.astype(F32), axis=1, keepdims=True)
    hidden_cot = gates * raw_cot
    h_out[0] = hidden16
    g16 = (hidden_cot * up_value * slope).astype(BF16)
    u16 = (hidden_cot * active).astype(BF16)
    g_out[0] = g16
    u_out[0] = u16
    c_out[0] = (gates * c.astype(F32)).astype(BF16)
    x_cot = (dot(g16, weights[0, 0], NN) + dot(u16, weights[0, 1], NN)).astype(BF16)
    y = dot((gates * hidden16.astype(F32)).astype(BF16), weights[0, 2], NN).astype(BF16)
    for at, (x_ref, _) in enumerate(sources):
        low, high = at * capacity, (at + 1) * capacity
        ranks, probability, chosen, chosen_total, mine = tables[at]
        back = jnp.sum(picks[at].astype(F32) * gate_cot[low:high], axis=0, keepdims=True)
        shift = back * mine / (chosen_total * chosen_total)
        direct = jnp.where(expert_row == wanted, back / chosen_total, 0.0)
        prob_cot = jnp.where(ranks >= 0.0, direct - shift, 0.0)
        inner = jnp.sum(prob_cot * probability, axis=0, keepdims=True)
        logit_cot = (probability * (prob_cot - inner)).astype(BF16)
        cot_scratch[at] += dot(picks[at], x_cot[low:high], TN) + dot(logit_cot, router[...], TN)
        out_scratch[at] += dot(picks[at], y[low:high], TN)
        router_scratch[...] += dot(logit_cot, x_ref[...], NN)

    @pl.when(step == local - 1)
    def _():
        cot_own[...] = cot_scratch[0].astype(BF16)
        cot_other[...] = cot_scratch[1].astype(BF16)
        out_own[...] = out_scratch[0].astype(BF16)
        out_other[...] = out_scratch[1].astype(BF16)
        router_out[...] = router_scratch[...]


def expert_chunk(first, x_pair, c_pair, router, weights, capacity):
    length, width = x_pair[0].shape
    local, _, units, _ = weights.shape
    experts = router.shape[0]
    whole = lambda shape: pl.BlockSpec(shape, lambda e, s: (0,) * len(shape))
    per = lambda shape: pl.BlockSpec((1,) + shape, lambda e, s: (e,) + (0,) * len(shape))
    slots = 2 * capacity
    shape = jax.ShapeDtypeStruct
    return pl.pallas_call(
        expert_kernel,
        grid_spec=pltpu.PrefetchScalarGridSpec(
            num_scalar_prefetch=1,
            grid=(local,),
            in_specs=[
                whole((length, width)),
                whole((length, width)),
                whole(c_pair[0].shape),
                whole(c_pair[1].shape),
                whole((experts, width)),
                per((3, units, width)),
            ],
            out_specs=[per((slots, width))] * 2
            + [per((slots, units))] * 3
            + [whole((length, width))] * 4
            + [whole((experts, width))],
            scratch_shapes=[
                pltpu.VMEM((2, length, width), F32),
                pltpu.VMEM((2, length, width), F32),
                pltpu.VMEM((experts, width), F32),
            ],
        ),
        out_shape=[shape((local, slots, width), BF16)] * 2
        + [shape((local, slots, units), BF16)] * 3
        + [shape((length, width), BF16)] * 4
        + [shape((experts, width), F32)],
        compiler_params=pltpu.CompilerParams(vmem_limit_bytes=VMEM_LIMIT),
        name="expert_chunk",
    )(first, *x_pair, *c_pair, router, weights)


def expert_weights_kernel(*refs):
    *inputs, out = refs
    n = len(inputs) // 2
    total = None
    for left, right in zip(inputs[:n], inputs[n:]):
        part = dot(left[0], right[0], TN)
        total = part if total is None else total + part
    out[0] = total.astype(BF16)


def expert_weight_part(left, right):
    local, slots, units = left[0].shape
    width = right[0].shape[2]
    return pl.pallas_call(
        expert_weights_kernel,
        grid=(local,),
        in_specs=[pl.BlockSpec((1, slots, units), lambda e: (e, 0, 0))] * len(left)
        + [pl.BlockSpec((1, slots, width), lambda e: (e, 0, 0))] * len(right),
        out_specs=pl.BlockSpec((1, units, width), lambda e: (e, 0, 0)),
        out_shape=jax.ShapeDtypeStruct((local, units, width), BF16),
        compiler_params=pltpu.CompilerParams(vmem_limit_bytes=VMEM_LIMIT),
        name="expert_weights",
    )(*left, *right)


def split_matmul(values, matrix, dims):
    high = values.astype(BF16)
    low = (values - high.astype(F32)).astype(BF16)
    return dot(high, matrix, dims) + dot(low, matrix, dims)


def exact_matmul(values, matrix, dims):
    return lax.dot_general(
        values, matrix.astype(F32), (dims, ((), ())),
        precision=lax.Precision.HIGHEST, preferred_element_type=F32,
    )


def shards(
    tokens,
    out_cotangent,
    assignment,
    norm_gains,
    attention_weights,
    router_weights,
    shared_weights,
    expert_weights,
):
    length, width = tokens.shape
    rows = attention_weights.shape[0]
    ranks = lax.axis_size("dp")
    local = expert_weights.shape[0]
    experts = local * ranks
    capacity = length * 6 // experts
    units = shared_weights.shape[2]
    n = ranks // 2

    small = jnp.concatenate([norm_gains, router_weights], axis=1)
    small = jnp.pad(small, ((0, 0), (0, LANES - small.shape[1])))
    packed = jnp.concatenate([attention_weights[:, :3].reshape(rows, 3 * width), small], axis=1)
    pieces, line = dense_gather(packed)
    project = jnp.concatenate([a[:, : 3 * width] for a in pieces], axis=0)
    small_full = jnp.concatenate([a[:, 3 * width :] for a in pieces], axis=0)
    out_local, shared_local = attention_weights[:, 3], shared_weights.reshape(rows, 3 * units)
    out_local = after(out_local, *line)
    pieces, line = dense_gather(out_local)
    out_full = jnp.concatenate(pieces, axis=0)
    shared_local = after(shared_local, *line)
    pieces, line = dense_gather(shared_local)
    shared_full = jnp.concatenate(pieces, axis=0)
    shared_gu, shared_down = shared_full[:, : 2 * units], shared_full[:, 2 * units :]

    turned = jnp.transpose(expert_weights, (0, 1, 3, 2))
    routed = [
        jnp.concatenate(cube_gather(turned[e], e % cube_size()), axis=1) for e in range(local)
    ]
    routed = jnp.stack(routed)

    hot = jnp.sum(
        (assignment[:, :, None] == jnp.arange(experts)[None, None, :]).astype(F32), axis=1
    )
    before = (jnp.arange(length)[:, None] < jnp.arange(length)[None, :]).astype(BF16)
    earlier = dot(hot.astype(BF16), before, TN)
    places = jnp.where(hot.T > 0, jnp.minimum(earlier, float(capacity)), -1.0).astype(BF16)
    places = jnp.pad(places, ((0, 0), (0, width - length)))
    sent = jnp.concatenate([out_cotangent, places], axis=0)
    c_pairs = token_gather(after(sent, *line))

    owner = block_order()
    true_row = (owner[:, None] * rows + jnp.arange(rows)[None, :]).reshape(width)
    order = (jnp.arange(width)[:, None] == true_row[None, :]).astype(BF16)
    tokens_float = tokens.astype(F32)
    tokens_rel = dot(tokens, order, NN)
    c_rel = dot(out_cotangent, order, NN).astype(BF16)
    root_one = lax.rsqrt(jnp.mean(tokens_float * tokens_float, axis=-1, keepdims=True) + EPSILON)
    position = jnp.arange(length).astype(F32)
    frequency = 10000.0 ** (-jnp.arange(HEAD_SIZE // 2).astype(F32) * (2.0 / HEAD_SIZE))
    angle = position[:, None] * frequency[None, :]
    cosine = jnp.concatenate([jnp.cos(angle), jnp.cos(angle)], axis=1)
    sine = jnp.concatenate([-jnp.sin(angle), jnp.sin(angle)], axis=1)

    small_true = dot(order, small_full, NN)
    gain_one = small_full[:, 0].astype(F32)
    gain_two = small_true[:, 1]
    router = small_true[:, 2 : 2 + experts].T.astype(BF16)

    unit_one = tokens_rel * root_one
    normed_one = (unit_one * gain_one).astype(BF16)
    projected = dot(normed_one, project, NN)
    query, key, value, mixed, lse = attention_forward(projected, cosine, sine)
    mixed_rel = dot(mixed, order, NN).astype(BF16)
    hidden_res = tokens_float + dot(mixed_rel, out_full, NN)
    root_two = lax.rsqrt(jnp.mean(hidden_res * hidden_res, axis=-1, keepdims=True) + EPSILON)
    unit_two = hidden_res * root_two
    normed_two = (unit_two * gain_two).astype(BF16)
    x_pairs = token_gather(normed_two)

    normed_rel = dot(normed_two, order, NN).astype(BF16)
    gate_up = dot(normed_rel, shared_gu, NN)
    shared_active, shared_slope = silu_parts(gate_up[:, :units])
    shared_up = gate_up[:, units:]
    shared_hidden = (shared_active * shared_up).astype(BF16)
    shared_out = split_matmul(dot(shared_hidden, shared_down, NT), order, NT)
    shared_cot = dot(c_rel, shared_down, NN)
    gate_up_cot = jnp.concatenate(
        [
            (shared_cot * shared_up * shared_slope).astype(BF16),
            (shared_cot * shared_active).astype(BF16),
        ],
        axis=1,
    )
    half = width // 2
    shared_grad = [
        jnp.concatenate(
            [dot(normed_rel[:, cut], gate_up_cot, TN).astype(BF16),
             dot(c_rel[:, cut], shared_hidden, TN).astype(BF16)], axis=1,
        )
        for cut in (slice(0, half), slice(half, width))
    ]
    shared_back = split_matmul(dot(gate_up_cot, shared_gu, NT), order, NT)

    first = (lax.axis_index("dp") * local).astype(jnp.int32).reshape(1)
    done = {}
    for r in [0] + [r for i in range(n // 2, 0, -1) for r in sorted({i, n - i}) if 0 < r < n]:
        done[r] = expert_chunk(first, x_pairs[r], c_pairs[r], router, routed, capacity)
    chunks = [done[r] for r in range(n)]
    back_sum = token_scatter([(a[5], a[6]) for a in chunks])
    router_part = sum(a[9] for a in chunks)
    expert_grads = [
        expert_weight_part([a[i] for a in chunks], [a[j] for a in chunks])
        for i, j in ((3, 0), (4, 0), (2, 1))
    ]
    out_pairs = lax.optimization_barrier(([(a[7], a[8]) for a in chunks], back_sum))[0]
    out_sum = token_scatter(out_pairs)
    block_output = (hidden_res + shared_out + out_sum).astype(BF16)
    expert_gradient = jnp.stack(
        [
            jnp.stack([cube_scatter(g[e], e % cube_size()).T for g in expert_grads])
            for e in range(local)
        ]
    )

    cotangent = out_cotangent.astype(F32)
    normed_two_cot = back_sum + shared_back
    scaled = normed_two_cot * gain_two
    gain_two_grad = jnp.sum(normed_two_cot * unit_two, axis=0)
    hidden_cot = cotangent + root_two * (
        scaled - unit_two * jnp.mean(scaled * unit_two, axis=-1, keepdims=True)
    )
    attn_cot = hidden_cot.astype(BF16)
    mixed_cot = dot(dot(attn_cot, out_full, NT).astype(BF16), order, NT).astype(BF16)
    out_grad = [dot(mixed_rel[:, cut], attn_cot, TN).astype(BF16)
                for cut in (slice(0, half), slice(half, width))]
    cots = attention_backward(query, key, value, mixed_cot, lse, cosine, sine)
    projected_cot = jnp.concatenate(cots, axis=1)
    in_grad = [dot(normed_one[:, cut], projected_cot, TN).astype(BF16)
               for cut in (slice(0, half), slice(half, width))]
    normed_one_cot = dot(projected_cot, project, NT)
    scaled_one = normed_one_cot * gain_one
    gain_one_grad = jnp.sum(normed_one_cot * unit_one, axis=0)
    token_part = root_one * (
        scaled_one - unit_one * jnp.mean(scaled_one * unit_one, axis=-1, keepdims=True)
    )
    token_gradient = hidden_cot + split_matmul(token_part, order, NT)

    shared_gradient = dense_scatter(*shared_grad).reshape(rows, 3, units)
    out_gradient = dense_scatter(*out_grad)
    in_gradient = dense_scatter(*in_grad).reshape(rows, 3, width)
    attention_gradient = jnp.concatenate([in_gradient, out_gradient[:, None, :]], axis=1)
    true_part = exact_matmul(
        jnp.concatenate([gain_two_grad[None, :], router_part], axis=0), order, NN
    )
    small_grad = jnp.concatenate([gain_one_grad[None, :], true_part], axis=0)
    small_grad = jnp.pad(small_grad, ((0, LANES - small_grad.shape[0]), (0, 0))).T
    small_gradient = dense_scatter(small_grad[:half], small_grad[half:], F32)
    return (
        block_output,
        token_gradient,
        small_gradient[:, :2],
        attention_gradient,
        small_gradient[:, 2 : 2 + experts],
        shared_gradient,
        expert_gradient,
    )


def solution(mesh):
    both = ("dp", "fsdp")
    return jax.shard_map(
        shards,
        mesh=mesh,
        in_specs=(
            P(both, None),
            P(both, None),
            P(both, None),
            P(both, None),
            P(both, None, None),
            P(both, None),
            P(both, None, None),
            P("dp", None, None, "fsdp"),
        ),
        out_specs=(
            P(both, None),
            P(both, None),
            P(both, None),
            P(both, None, None),
            P(both, None),
            P(both, None, None),
            P("dp", None, None, "fsdp"),
        ),
        check_vma=False,
    )
```

time: 1810 us -> 1110 us (0.61)
  waiting for transfers between devices: 825 us -> 469 us
  local copies, waits for them, and re-layouts: 388 us -> 36.9 us
  starting transfers between devices: 20.7 us -> 226 us
  Pallas kernels: 0 us -> 195 us
  blocking collectives: 175 us -> 0 us
  matrix products: 232 us -> 93 us
  other arithmetic: 135 us -> 68.6 us
    ppermute x0 -> x162, waiting for transfers between devices: none -> 469 us  [the longest x66 234 us: line_send(): return lax.ppermute(x, 'dp', pairs)]
    unnamed x8 -> x0, waiting for transfers between devices: 414 us -> none
    all_to_all x4 -> x0, waiting for transfers between devices: 410 us -> none  [the longest x1 167 us: shards(): lax.all_to_all(slot_out.astype(jnp.bfloat16), 'dp', split_axis=0, concat_...]
    ppermute x0 -> x162, starting transfers between devices: none -> 226 us  [the longest x66 166 us: line_send(): return lax.ppermute(x, 'dp', pairs)]
    pallas_call x0 -> x9, Pallas kernels: none -> 195 us  [the longest x4 124 us: expert_chunk(): pl.pallas_call(expert_kernel, grid_spec=pltpu.PrefetchScalarGridSpec(num_...]
    dot_general x33 -> x29, matrix products: 232 us -> 93 us  [the longest x28 90.9 us: dot(): return lax.dot_general(a, b, (dims, ((), ())), preferred_element_type=F32)]
    all_gather x2 -> x0, blocking collectives: 135 us -> none  [the longest x1 70 us: shards(): lax.all_gather(norm_gains, ('dp', 'fsdp'), axis=0, tiled=True)]
    unnamed x205 -> x244, local copies, waits for them, and re-layouts: 101 us -> 22.1 us
  transfers between devices with their start and end apart: 10 -> 162, of which waited for: 5 -> 68; matrix products, arithmetic and copies ran while one was open for 32% -> 14% of each run, Pallas kernels for 0% -> 17%
where the time goes in v1:
time: 1110 us; the launch traced here: 1090 us
  waiting for transfers between devices  469 us (42%)
  starting transfers between devices  226 us (20%)
  Pallas kernels  195 us (18%)
  matrix products  93 us (8%)
  other arithmetic  68.6 us (6%)
  local copies, waits for them, and re-layouts  36.9 us (3%)
    ppermute x66, waiting for transfers between devices, line_send(): return lax.ppermute(x, 'dp', pairs)  234 us
    ppermute x52, waiting for transfers between devices, fsdp_swap(): lax.ppermute(x, 'fsdp', [(f, f ^ bit) for f in range(lax.axis_size('fsdp'...  227 us
    ppermute x66, starting transfers between devices, line_send(): return lax.ppermute(x, 'dp', pairs)  166 us
    pallas_call x4, Pallas kernels, expert_chunk(): pl.pallas_call(expert_kernel, grid_spec=pltpu.PrefetchScalarGridSpec(num_...  124 us
    dot_general x28, matrix products, dot(): return lax.dot_general(a, b, (dims, ((), ())), preferred_element_type=F32)  90.9 us
    ppermute x52, starting transfers between devices, fsdp_swap(): lax.ppermute(x, 'fsdp', [(f, f ^ bit) for f in range(lax.axis_size('fsdp'...  51.2 us
    pallas_call x3, Pallas kernels, expert_weight_part(): pl.pallas_call(expert_weights_kernel, grid=(local,), in_specs=[pl.BlockSp...  43.5 us
  transfers between devices with their start and end apart: 162, of which 68 were waited for; matrix products, arithmetic and copies ran while one was open for 14% of the time, Pallas kernels for 17%

profile of v1, /device:TPU:0, one launch (start us, length us, event | category | flops | bytes accessed | tf_op | source)
XLA Modules:
  0.0 1092.3 jit_solution(906393848621484191)
XLA Ops:
  74.6 11.0 %collective-permute-done.5 = bf16[80,3968]{1,0:T(8,128)(2,1)S(1)} collective-permute-done((bf16[80,3968]{1,0:T(8,128)(2,1)S(1)}, bf16[80,3968]{1,0:T(8,128)(2,1)S(1)}, u32[]{:S(2)}, u32[]{:S(2)}) %collective-permute-start.5) | collective-permute-done | bytes 634912 | tf_op jit(solution)/shard_map/ppermute | solution.py:27
  90.0 12.7 %collective-permute-done.26 = bf16[80,1280]{1,0:T(8,128)(2,1)S(1)} collective-permute-done((bf16[80,1280]{1,0:T(8,128)(2,1)S(1)}, bf16[80,1280]{1,0:T(8,128)(2,1)S(1)}, u32[]{:S(2)}, u32[]{:S(2)}) %collective-permute-start.26) | collective-permute-done | bytes 204832 | tf_op jit(solution)/shard_map/ppermute | solution.py:27
  151.3 11.4 %collective-permute-done.43 = bf16[40,2688]{1,0:T(8,128)(2,1)S(1)} collective-permute-done((bf16[40,2688]{1,0:T(8,128)(2,1)S(1)}, bf16[40,2688]{1,0:T(8,128)(2,1)S(1)}, u32[]{:S(2)}, u32[]{:S(2)}) %collective-permute-start.43) | collective-permute-done | bytes 215072 | tf_op jit(solution)/shard_map/ppermute | solution.py:32
  177.7 10.1 collective-permute-done.44
  193.0 36.7 %collective-permute-done.65 = bf16[3,224,1280]{2,1,0:T(8,128)(2,1)} collective-permute-done((bf16[3,224,1280]{2,1,0:T(8,128)(2,1)S(1)}, bf16[3,224,1280]{2,1,0:T(8,128)(2,1)}, u32[]{:S(2)}, u32[]{:S(2)}) %collective-permute-start.65) | collective-permute-done | bytes 1720352 | tf_op jit(solution)/shard_map/ppermute | solution.py:27
  247.5 12.9 %attention_forward.1 = (bf16[512,1280]{1,0:T(8,128)(2,1)}, bf16[512,1280]{1,0:T(8,128)(2,1)}, bf16[512,1280]{1,0:T(8,128)(2,1)}, bf16[512,1280]{1,0:T(8,128)(2,1)}, f32[10,1,512]{2,1,0:T(1,128)}) custom-call(f32[512,3840]{1,0:T(8,128)} %fusion.121.qp.kp.vp, f32[512,3840]{1,0:T(8,128)} %fusion.121.qp.kp.vp, f32[512,3840]{1,0:T(8,128)} %fusion.121.qp.kp.vp, ...), custom_call_target="tpu_custom_call" | custom-call | tf_op jit(solution)/shard_map/attention_forward/pallas_call | solution.py:181
  267.6 10.8 collective-permute-done.46
  282.2 9.2 collective-permute-done.49
  343.4 20.8 %collective-permute-done.68 = bf16[512,1280]{1,0:T(8,128)(2,1)S(1)} collective-permute-done((bf16[512,1280]{1,0:T(8,128)(2,1)S(1)}, bf16[512,1280]{1,0:T(8,128)(2,1)S(1)}, u32[]{:S(2)}, u32[]{:S(2)}) %collective-permute-start.68) | collective-permute-done | bytes 1310752 | tf_op jit(solution)/shard_map/ppermute | solution.py:32
  364.2 15.7 %collective-permute-done.69 = bf16[512,1280]{1,0:T(8,128)(2,1)S(1)} collective-permute-done((bf16[512,1280]{1,0:T(8,128)(2,1)S(1)}, bf16[512,1280]{1,0:T(8,128)(2,1)S(1)}, u32[]{:S(2)}, u32[]{:S(2)}) %collective-permute-start.69) | collective-permute-done | bytes 1310752 | tf_op jit(solution)/shard_map/ppermute | solution.py:32
  398.8 22.3 %collective-permute-done.71 = bf16[512,1280]{1,0:T(8,128)(2,1)} collective-permute-done((bf16[512,1280]{1,0:T(8,128)(2,1)S(1)}, bf16[512,1280]{1,0:T(8,128)(2,1)}, u32[]{:S(2)}, u32[]{:S(2)}) %collective-permute-start.71) | collective-permute-done | bytes 1310752 | tf_op jit(solution)/shard_map/ppermute | solution.py:32
  427.5 30.9 %expert_chunk.4 = (bf16[2,384,1280]{2,1,0:T(8,128)(2,1)}, bf16[2,384,1280]{2,1,0:T(8,128)(2,1)}, bf16[2,384,896]{2,1,0:T(8,128)(2,1)}, bf16[2,384,896]{2,1,0:T(8...) custom-call(s32[1]{0:T(128)} %bitcast.34.first, ...), custom_call_target="tpu_custom_call" | custom-call | tf_op jit(solution)/shard_map/expert_chunk/pallas_call | solution.py:325
  464.5 13.7 %collective-permute-done.73 = bf16[512,1280]{1,0:T(8,128)(2,1)} collective-permute-done((bf16[512,1280]{1,0:T(8,128)(2,1)}, bf16[512,1280]{1,0:T(8,128)(2,1)}, u32[]{:S(2)}, u32[]{:S(2)}) %collective-permute-start.73) | collective-permute-done | bytes 1310752 | tf_op jit(solution)/shard_map/ppermute | solution.py:32
  481.5 23.2 %collective-permute-done.80 = bf16[528,1280]{1,0:T(8,128)(2,1)S(1)} collective-permute-done((bf16[528,1280]{1,0:T(8,128)(2,1)}, bf16[528,1280]{1,0:T(8,128)(2,1)S(1)}, u32[]{:S(2)}, u32[]{:S(2)}) %collective-permute-start.80) | collective-permute-done | bytes 1351712 | tf_op jit(solution)/shard_map/ppermute | solution.py:32
  508.0 30.9 %expert_chunk.6 = (bf16[2,384,1280]{2,1,0:T(8,128)(2,1)}, bf16[2,384,1280]{2,1,0:T(8,128)(2,1)}, bf16[2,384,896]{2,1,0:T(8,128)(2,1)}, bf16[2,384,896]{2,1,0:T(8...) custom-call(s32[1]{0:T(128)} %bitcast.34.first, ...), custom_call_target="tpu_custom_call" | custom-call | tf_op jit(solution)/shard_map/expert_chunk/pallas_call | solution.py:325
  547.4 31.1 %expert_chunk.7 = (bf16[2,384,1280]{2,1,0:T(8,128)(2,1)}, bf16[2,384,1280]{2,1,0:T(8,128)(2,1)}, bf16[2,384,896]{2,1,0:T(8,128)(2,1)}, bf16[2,384,896]{2,1,0:T(8...) custom-call(s32[1]{0:T(128)} %bitcast.34.first, ...), custom_call_target="tpu_custom_call" | custom-call | tf_op jit(solution)/shard_map/expert_chunk/pallas_call | solution.py:325
  579.7 31.3 %expert_chunk.5 = (bf16[2,384,1280]{2,1,0:T(8,128)(2,1)}, bf16[2,384,1280]{2,1,0:T(8,128)(2,1)}, bf16[2,384,896]{2,1,0:T(8,128)(2,1)}, bf16[2,384,896]{2,1,0:T(8...) custom-call(s32[1]{0:T(128)} %bitcast.34.first, ...), custom_call_target="tpu_custom_call" | custom-call | tf_op jit(solution)/shard_map/expert_chunk/pallas_call | solution.py:325
  611.0 14.5 %expert_weights.3 = bf16[2,896,1280]{2,1,0:T(8,128)(2,1)} custom-call(bf16[2,384,896]{2,1,0:T(8,128)(2,1)} %get-tuple-element.237.refs_0_, bf16[2,384,896]{2,1,0:T(8,128)(2,1)} %get-tuple-element.238.refs_1_, bf16[2,384,896]{2,1,0:T(8,128)(2,1)} %get-tuple-element.239.refs_2_, bf16[2,384,896]{2,1,0:T(8,128)(2,1)} %get-tuple-element.240.refs_3_, ...), custom_call_target="tpu_custom_call" | custom-call | tf_op jit(solution)/shard_map/expert_weights/pallas_call | solution.py:370
  630.9 14.3 %expert_weights.4 = bf16[2,896,1280]{2,1,0:T(8,128)(2,1)} custom-call(bf16[2,384,896]{2,1,0:T(8,128)(2,1)} %get-tuple-element.245.refs_0_, bf16[2,384,896]{2,1,0:T(8,128)(2,1)} %get-tuple-element.246.refs_1_, bf16[2,384,896]{2,1,0:T(8,128)(2,1)} %get-tuple-element.247.refs_2_, bf16[2,384,896]{2,1,0:T(8,128)(2,1)} %get-tuple-element.248.refs_3_, ...), custom_call_target="tpu_custom_call" | custom-call | tf_op jit(solution)/shard_map/expert_weights/pallas_call | solution.py:370
  645.2 14.7 %expert_weights.5 = bf16[2,896,1280]{2,1,0:T(8,128)(2,1)} custom-call(bf16[2,384,896]{2,1,0:T(8,128)(2,1)} %get-tuple-element.249.refs_0_, bf16[2,384,896]{2,1,0:T(8,128)(2,1)} %get-tuple-element.250.refs_1_, bf16[2,384,896]{2,1,0:T(8,128)(2,1)} %get-tuple-element.251.refs_2_, bf16[2,384,896]{2,1,0:T(8,128)(2,1)} %get-tuple-element.252.refs_3_, ...), custom_call_target="tpu_custom_call" | custom-call | tf_op jit(solution)/shard_map/expert_weights/pallas_call | solution.py:370
  692.9 22.7 %collective-permute-done.152 = bf16[448,1280]{1,0:T(8,128)(2,1)S(1)} collective-permute-done((bf16[448,1280]{1,0:T(8,128)(2,1)S(1)}, bf16[448,1280]{1,0:T(8,128)(2,1)S(1)}, u32[]{:S(2)}, u32[]{:S(2)}) %collective-permute-start.152) | collective-permute-done | bytes 1146912 | tf_op jit(solution)/shard_map/ppermute | solution.py:27
  724.4 11.1 %collective-permute-done.154 = bf16[448,1280]{1,0:T(8,128)(2,1)S(1)} collective-permute-done((bf16[448,1280]{1,0:T(8,128)(2,1)S(1)}, bf16[448,1280]{1,0:T(8,128)(2,1)S(1)}, u32[]{:S(2)}, u32[]{:S(2)}) %collective-permute-start.154) | collective-permute-done | bytes 1146912 | tf_op jit(solution)/shard_map/ppermute | solution.py:27
  746.1 13.2 %collective-permute-done.151 = bf16[224,1280]{1,0:T(8,128)(2,1)S(1)} collective-permute-done((bf16[224,1280]{1,0:T(8,128)(2,1)S(1)}, bf16[224,1280]{1,0:T(8,128)(2,1)S(1)}, u32[]{:S(2)}, u32[]{:S(2)}) %collective-permute-start.151) | collective-permute-done | bytes 573472 | tf_op jit(solution)/shard_map/ppermute | solution.py:27
  776.5 9.8 collective-permute-done.155
  795.3 14.4 %collective-permute-start.94 = (bf16[512,1280]{1,0:T(8,128)(2,1)S(1)}, bf16[512,1280]{1,0:T(8,128)(2,1)S(1)}, u32[]{:S(2)}, u32[]{:S(2)}) collective-permute-start(bf16[512,1280]{1,0:T(8,128)(2,1)S(1)} %add_convert_fusion.6), channel_id=1, source_target_pairs={{0,8},{4,12},{8,16},{12,20},{16,24},{20,28},{1,9},{5,13},{9,17},{1... | collective-permute-start | bytes 3932168 | tf_op jit(solution)/shard_map/ppermute | solution.py:32
  814.4 18.3 %collective-permute-done.95 = bf16[512,1280]{1,0:T(8,128)(2,1)S(1)} collective-permute-done((bf16[512,1280]{1,0:T(8,128)(2,1)S(1)}, bf16[512,1280]{1,0:T(8,128)(2,1)S(1)}, u32[]{:S(2)}, u32[]{:S(2)}) %collective-permute-start.95) | collective-permute-done | bytes 1310752 | tf_op jit(solution)/shard_map/ppermute | solution.py:32
  847.9 14.1 %attention_backward.1 = (bf16[512,1280]{1,0:T(8,128)(2,1)}, bf16[512,1280]{1,0:T(8,128)(2,1)}, bf16[512,1280]{1,0:T(8,128)(2,1)}) custom-call(bf16[512,1280]{1,0:T(8,128)(2,1)} %get-tuple-element.202.q_in, bf16[512,1280]{1,0:T(8,128)(2,1)} %get-tuple-element.203.k_in, bf16[512,1280]{1,0:T(8,128)(2,1)} %get-tuple-element.204.v_in, ...), custom_call_target="tpu_custom_call" | custom-call | tf_op jit(solution)/shard_map/attention_backward/pallas_call | solution.py:218
  865.5 9.5 multiply_reduce_fusion.1
  907.1 9.2 collective-permute-done.129
  950.3 17.9 %collective-permute-done.135 = bf16[40,1280]{1,0:T(8,128)(2,1)S(1)} collective-permute-done((bf16[40,1280]{1,0:T(8,128)(2,1)S(1)}, bf16[40,1280]{1,0:T(8,128)(2,1)S(1)}, u32[]{:S(2)}, u32[]{:S(2)}) %collective-permute-start.135) | collective-permute-done | bytes 102432 | tf_op jit(solution)/shard_map/ppermute | solution.py:32
  969.0 10.2 collective-permute-start.115
  1045.8 18.0 %collective-permute-done.122 = bf16[40,3840]{1,0:T(8,128)(2,1)S(1)} collective-permute-done((bf16[40,3840]{1,0:T(8,128)(2,1)S(1)}, bf16[40,3840]{1,0:T(8,128)(2,1)S(1)}, u32[]{:S(2)}, u32[]{:S(2)}) %collective-permute-start.122) | collective-permute-done | bytes 307232 | tf_op jit(solution)/shard_map/ppermute | solution.py:32
  (720 shorter events, 541.7 us)
Async XLA Ops:
  13.2 179.2 %collective-permute-start.62 = (bf16[3,224,1280]{2,1,0:T(8,128)(2,1)S(1)}, bf16[3,224,1280]{2,1,0:T(8,128)(2,1)}, u32[]{:S(2)}, u32[]{:S(2)}) collective-permute-start(bf16[3,224,1280]{2,1,0:T(8,128)(2,1)S(1)} %get-tuple-element.319), channel_id=1, source_target_pairs={{0,1},{1,0},{2,3},{3,2},{4,5},{5,4},{6,7},{7,6},{8,9},{9,8},{10,11... | collective-permute-start | bytes 5160968 | tf_op jit(solution)/shard_map/ppermute | solution.py:27
  14.8 286.3 %collective-permute-start.63 = (bf16[3,224,1280]{2,1,0:T(8,128)(2,1)S(1)}, bf16[3,224,1280]{2,1,0:T(8,128)(2,1)}, u32[]{:S(2)}, u32[]{:S(2)}) collective-permute-start(bf16[3,224,1280]{2,1,0:T(8,128)(2,1)S(1)} %get-tuple-element.319), channel_id=1, source_target_pairs={{0,2},{1,3},{2,0},{3,1},{4,6},{5,7},{6,4},{7,5},{8,10},{9,11},{10,... | collective-permute-start | bytes 5160968 | tf_op jit(solution)/shard_map/ppermute | solution.py:27
  190.9 114.1 %collective-permute-start.66 = (bf16[3,224,1280]{2,1,0:T(8,128)(2,1)S(1)}, bf16[3,224,1280]{2,1,0:T(8,128)(2,1)}, u32[]{:S(2)}, u32[]{:S(2)}) collective-permute-start(bf16[3,224,1280]{2,1,0:T(8,128)(2,1)S(1)} %get-tuple-element.320), channel_id=1, source_target_pairs={{0,1},{1,0},{2,3},{3,2},{4,5},{5,4},{6,7},{7,6},{8,9},{9,8},{10,11... | collective-permute-start | bytes 5160968 | tf_op jit(solution)/shard_map/ppermute | solution.py:27
  229.7 72.0 %collective-permute-start.64 = (bf16[3,224,1280]{2,1,0:T(8,128)(2,1)}, bf16[3,224,1280]{2,1,0:T(8,128)(2,1)}, u32[]{:S(2)}, u32[]{:S(2)}) collective-permute-start(bf16[3,224,1280]{2,1,0:T(8,128)(2,1)} %collective-permute-done.62), channel_id=1, source_target_pairs={{0,2},{1,3},{2,0},{3,1},{4,6},{5,7},{6,4},{7,5},{8,10},{9,11},{10,... | collective-permute-start | bytes 5160968 | tf_op jit(solution)/shard_map/ppermute | solution.py:27
  230.2 76.2 %collective-permute-start.67 = (bf16[3,224,1280]{2,1,0:T(8,128)(2,1)}, bf16[3,224,1280]{2,1,0:T(8,128)(2,1)}, u32[]{:S(2)}, u32[]{:S(2)}) collective-permute-start(bf16[3,224,1280]{2,1,0:T(8,128)(2,1)} %collective-permute-done.65), channel_id=1, source_target_pairs={{0,1},{1,0},{2,3},{3,2},{4,5},{5,4},{6,7},{7,6},{8,9},{9,8},{10,11... | collective-permute-start | bytes 5160968 | tf_op jit(solution)/shard_map/ppermute | solution.py:27
  233.7 44.7 %collective-permute-start.46 = (bf16[80,2688]{1,0:T(8,128)(2,1)}, bf16[80,2688]{1,0:T(8,128)(2,1)}, u32[]{:S(2)}, u32[]{:S(2)}) collective-permute-start(bf16[80,2688]{1,0:T(8,128)(2,1)} %collective-permute-done.44), channel_id=1, source_target_pairs={{0,2},{1,3},{2,0},{3,1},{4,6},{5,7},{6,4},{7,5},{8,10},{9,11},{10,... | collective-permute-start | bytes 1290248 | tf_op jit(solution)/shard_map/ppermute | solution.py:27
  305.0 82.4 %collective-permute-start.75 = (bf16[528,1280]{1,0:T(8,128)(2,1)S(1)}, bf16[528,1280]{1,0:T(8,128)(2,1)S(1)}, u32[]{:S(2)}, u32[]{:S(2)}) collective-permute-start(bf16[528,1280]{1,0:T(8,128)(2,1)S(1)} %fusion.62.c_own), channel_id=1, source_target_pairs={{0,8},{4,12},{8,16},{12,20},{16,24},{20,28},{1,9},{5,13},{9,17},{1... | collective-permute-start | bytes 4055048 | tf_op jit(solution)/shard_map/ppermute | solution.py:32
  318.7 74.2 %collective-permute-start.76 = (bf16[528,1280]{1,0:T(8,128)(2,1)S(1)}, bf16[528,1280]{1,0:T(8,128)(2,1)S(1)}, u32[]{:S(2)}, u32[]{:S(2)}) collective-permute-start(bf16[528,1280]{1,0:T(8,128)(2,1)S(1)} %fusion.62.c_own), channel_id=1, source_target_pairs={{8,0},{12,4},{16,8},{20,12},{24,16},{28,20},{9,1},{13,5},{17,9},{2... | collective-permute-start | bytes 4055048 | tf_op jit(solution)/shard_map/ppermute | solution.py:32
  329.4 50.5 %collective-permute-start.69 = (bf16[512,1280]{1,0:T(8,128)(2,1)S(1)}, bf16[512,1280]{1,0:T(8,128)(2,1)S(1)}, u32[]{:S(2)}, u32[]{:S(2)}) collective-permute-start(bf16[512,1280]{1,0:T(8,128)(2,1)S(1)} %multiply_convert_fusion.x_own), channel_id=1, source_target_pairs={{8,0},{12,4},{16,8},{20,12},{24,16},{28,20},{9,1},{13,5},{17,9},{2... | collective-permute-start | bytes 3932168 | tf_op jit(solution)/shard_map/ppermute | solution.py:32
  330.7 95.7 %collective-permute-start.61 = (bf16[528,1280]{1,0:T(8,128)(2,1)S(1)}, bf16[528,1280]{1,0:T(8,128)(2,1)S(1)}, u32[]{:S(2)}, u32[]{:S(2)}) collective-permute-start(bf16[528,1280]{1,0:T(8,128)(2,1)S(1)} %fusion.62.c_own), channel_id=1, source_target_pairs={{0,4},{4,0},{8,12},{12,8},{16,20},{20,16},{24,28},{28,24},{1,5},{5... | collective-permute-start | bytes 4055048 | tf_op jit(solution)/shard_map/ppermute | solution.py:23
  364.2 58.7 %collective-permute-start.60 = (bf16[512,1280]{1,0:T(8,128)(2,1)S(1)}, bf16[512,1280]{1,0:T(8,128)(2,1)S(1)}, u32[]{:S(2)}, u32[]{:S(2)}) collective-permute-start(bf16[512,1280]{1,0:T(8,128)(2,1)S(1)} %multiply_convert_fusion.x_own), channel_id=1, source_target_pairs={{0,4},{4,0},{8,12},{12,8},{16,20},{20,16},{24,28},{28,24},{1,5},{5... | collective-permute-start | bytes 3932168 | tf_op jit(solution)/shard_map/ppermute | solution.py:23
  392.9 67.0 %collective-permute-start.77 = (bf16[528,1280]{1,0:T(8,128)(2,1)S(1)}, bf16[528,1280]{1,0:T(8,128)(2,1)}, u32[]{:S(2)}, u32[]{:S(2)}) collective-permute-start(bf16[528,1280]{1,0:T(8,128)(2,1)S(1)} %collective-permute-done.75), channel_id=1, source_target_pairs={{8,16},{12,20},{16,24},{20,28},{9,17},{13,21},{17,25},{21,29},{10,... | collective-permute-start | bytes 4055048 | tf_op jit(solution)/shard_map/ppermute | solution.py:32
  394.7 65.3 %collective-permute-start.78 = (bf16[528,1280]{1,0:T(8,128)(2,1)S(1)}, bf16[528,1280]{1,0:T(8,128)(2,1)}, u32[]{:S(2)}, u32[]{:S(2)}) collective-permute-start(bf16[528,1280]{1,0:T(8,128)(2,1)S(1)} %collective-permute-done.76), channel_id=1, source_target_pairs={{8,0},{12,4},{16,8},{20,12},{9,1},{13,5},{17,9},{21,13},{10,2},{14... | collective-permute-start | bytes 4055048 | tf_op jit(solution)/shard_map/ppermute | solution.py:32
  422.8 55.3 %collective-permute-start.73 = (bf16[512,1280]{1,0:T(8,128)(2,1)}, bf16[512,1280]{1,0:T(8,128)(2,1)}, u32[]{:S(2)}, u32[]{:S(2)}) collective-permute-start(bf16[512,1280]{1,0:T(8,128)(2,1)} %collective-permute-done.71), channel_id=1, source_target_pairs={{8,0},{12,4},{9,1},{13,5},{10,2},{14,6},{11,3},{15,7}} | collective-permute-start | bytes 3932168 | tf_op jit(solution)/shard_map/ppermute | solution.py:32
  427.5 111.4 %collective-permute-start.139 = (bf16[640,2688]{1,0:T(8,128)(2,1)}, bf16[640,2688]{1,0:T(8,128)(2,1)}, u32[]{:S(2)}, u32[]{:S(2)}) collective-permute-start(bf16[640,2688]{1,0:T(8,128)(2,1)} %pad_maximum_fusion.2), channel_id=1, source_target_pairs={{0,4},{4,0},{8,12},{12,8},{16,20},{20,16},{24,28},{28,24},{1,5},{5... | collective-permute-start | bytes 10321928 | tf_op jit(solution)/shard_map/ppermute | solution.py:23
  481.0 64.7 %collective-permute-start.84 = (bf16[512,1280]{1,0:T(8,128)(2,1)}, bf16[512,1280]{1,0:T(8,128)(2,1)}, u32[]{:S(2)}, u32[]{:S(2)}) collective-permute-start(bf16[512,1280]{1,0:T(8,128)(2,1)} %broadcast_select_fusion.3.x_own), channel_id=1, source_target_pairs={{0,4},{4,0},{8,12},{12,8},{16,20},{20,16},{24,28},{28,24},{1,5},{5... | collective-permute-start | bytes 3932168 | tf_op jit(solution)/shard_map/ppermute | solution.py:23
  504.7 73.8 %collective-permute-start.74 = (bf16[512,1280]{1,0:T(8,128)(2,1)S(1)}, bf16[512,1280]{1,0:T(8,128)(2,1)}, u32[]{:S(2)}, u32[]{:S(2)}) collective-permute-start(bf16[512,1280]{1,0:T(8,128)(2,1)S(1)} %broadcast_select_fusion.5.x_own), channel_id=1, source_target_pairs={{0,4},{4,0},{8,12},{12,8},{16,20},{20,16},{24,28},{28,24},{1,5},{5... | collective-permute-start | bytes 3932168 | tf_op jit(solution)/shard_map/ppermute | solution.py:23
  507.5 71.1 %collective-permute-start.81 = (bf16[528,1280]{1,0:T(8,128)(2,1)S(1)}, bf16[528,1280]{1,0:T(8,128)(2,1)S(1)}, u32[]{:S(2)}, u32[]{:S(2)}) collective-permute-start(bf16[528,1280]{1,0:T(8,128)(2,1)S(1)} %broadcast_select_fusion.2.c_own), channel_id=1, source_target_pairs={{0,4},{4,0},{8,12},{12,8},{16,20},{20,16},{24,28},{28,24},{1,5},{5... | collective-permute-start | bytes 4055048 | tf_op jit(solution)/shard_map/ppermute | solution.py:23
  539.0 225.4 %collective-permute-start.88 = (bf16[512,1280]{1,0:T(8,128)(2,1)}, bf16[512,1280]{1,0:T(8,128)(2,1)}, u32[]{:S(2)}, u32[]{:S(2)}) collective-permute-start(bf16[512,1280]{1,0:T(8,128)(2,1)} %get-tuple-element.179), channel_id=1, source_target_pairs={{0,4},{4,0},{8,12},{12,8},{16,20},{20,16},{24,28},{28,24},{1,5},{5... | collective-permute-start | bytes 3932168 | tf_op jit(solution)/shard_map/ppermute | solution.py:23
  545.6 114.5 %collective-permute-start.140 = (bf16[160,2688]{1,0:T(8,128)(2,1)}, bf16[160,2688]{1,0:T(8,128)(2,1)}, u32[]{:S(2)}, u32[]{:S(2)}) collective-permute-start(bf16[160,2688]{1,0:T(8,128)(2,1)} %get-tuple-element.318), channel_id=1, source_target_pairs={{0,2},{1,3},{2,0},{3,1},{4,6},{5,7},{6,4},{7,5},{8,10},{9,11},{10,... | collective-permute-start | bytes 2580488 | tf_op jit(solution)/shard_map/ppermute | solution.py:27
  546.1 114.0 %collective-permute-start.142 = (bf16[160,2688]{1,0:T(8,128)(2,1)}, bf16[160,2688]{1,0:T(8,128)(2,1)}, u32[]{:S(2)}, u32[]{:S(2)}) collective-permute-start(bf16[160,2688]{1,0:T(8,128)(2,1)} %get-tuple-element.317), channel_id=1, source_target_pairs={{0,1},{1,0},{2,3},{3,2},{4,5},{5,4},{6,7},{7,6},{8,9},{9,8},{10,11... | collective-permute-start | bytes 2580488 | tf_op jit(solution)/shard_map/ppermute | solution.py:27
  628.6 60.6 %collective-permute-start.150 = (bf16[448,1280]{1,0:T(8,128)(2,1)}, bf16[448,1280]{1,0:T(8,128)(2,1)S(1)}, u32[]{:S(2)}, u32[]{:S(2)}) collective-permute-start(bf16[448,1280]{1,0:T(8,128)(2,1)} %get-tuple-element.306), channel_id=1, source_target_pairs={{0,2},{1,3},{2,0},{3,1},{4,6},{5,7},{6,4},{7,5},{8,10},{9,11},{10,... | collective-permute-start | bytes 3440648 | tf_op jit(solution)/shard_map/ppermute | solution.py:27
  630.2 60.7 %collective-permute-start.156 = (bf16[448,1280]{1,0:T(8,128)(2,1)}, bf16[448,1280]{1,0:T(8,128)(2,1)}, u32[]{:S(2)}, u32[]{:S(2)}) collective-permute-start(bf16[448,1280]{1,0:T(8,128)(2,1)} %get-tuple-element.307), channel_id=1, source_target_pairs={{0,1},{1,0},{2,3},{3,2},{4,5},{5,4},{6,7},{7,6},{8,9},{9,8},{10,11... | collective-permute-start | bytes 3440648 | tf_op jit(solution)/shard_map/ppermute | solution.py:27
  689.3 46.3 %collective-permute-start.154 = (bf16[448,1280]{1,0:T(8,128)(2,1)S(1)}, bf16[448,1280]{1,0:T(8,128)(2,1)S(1)}, u32[]{:S(2)}, u32[]{:S(2)}) collective-permute-start(bf16[448,1280]{1,0:T(8,128)(2,1)S(1)} %get-tuple-element.314), channel_id=1, source_target_pairs={{0,2},{1,3},{2,0},{3,1},{4,6},{5,7},{6,4},{7,5},{8,10},{9,11},{10,... | collective-permute-start | bytes 3440648 | tf_op jit(solution)/shard_map/ppermute | solution.py:27
  743.9 90.5 %collective-permute-start.86 = (bf16[512,1280]{1,0:T(8,128)(2,1)S(1)}, bf16[512,1280]{1,0:T(8,128)(2,1)S(1)}, u32[]{:S(2)}, u32[]{:S(2)}) collective-permute-start(bf16[512,1280]{1,0:T(8,128)(2,1)S(1)} %copy-done.75), channel_id=1, source_target_pairs={{0,4},{4,0},{8,12},{12,8},{16,20},{20,16},{24,28},{28,24},{1,5},{5... | collective-permute-start | bytes 3932168 | tf_op jit(solution)/shard_map/ppermute | solution.py:23
  891.2 99.3 %collective-permute-start.117 = (bf16[640,3840]{1,0:T(8,128)(2,1)S(1)}, bf16[640,3840]{1,0:T(8,128)(2,1)S(1)}, u32[]{:S(2)}, u32[]{:S(2)}) collective-permute-start(bf16[640,3840]{1,0:T(8,128)(2,1)S(1)} %convolution_convert_fusion), channel_id=1, source_target_pairs={{0,4},{4,0},{8,12},{12,8},{16,20},{20,16},{24,28},{28,24},{1,5},{5... | collective-permute-start | bytes 14745608 | tf_op jit(solution)/shard_map/ppermute | solution.py:23
  903.0 82.1 %collective-permute-start.98 = (bf16[512,1280]{1,0:T(8,128)(2,1)S(1)}, bf16[512,1280]{1,0:T(8,128)(2,1)S(1)}, u32[]{:S(2)}, u32[]{:S(2)}) collective-permute-start(bf16[512,1280]{1,0:T(8,128)(2,1)S(1)} %copy-done.72), channel_id=1, source_target_pairs={{0,4},{4,0},{8,12},{12,8},{16,20},{20,16},{24,28},{28,24},{1,5},{5... | collective-permute-start | bytes 3932168 | tf_op jit(solution)/shard_map/ppermute | solution.py:23
  934.6 44.7 %collective-permute-start.101 = (bf16[512,1280]{1,0:T(8,128)(2,1)S(1)}, bf16[512,1280]{1,0:T(8,128)(2,1)S(1)}, u32[]{:S(2)}, u32[]{:S(2)}) collective-permute-start(bf16[512,1280]{1,0:T(8,128)(2,1)S(1)} %fusion.55), channel_id=1, source_target_pairs={{24,16},{28,20},{25,17},{29,21},{26,18},{30,22},{27,19},{31,23}} | collective-permute-start | bytes 3932168 | tf_op jit(solution)/shard_map/ppermute | solution.py:32
  935.6 45.0 %collective-permute-start.100 = (bf16[512,1280]{1,0:T(8,128)(2,1)S(1)}, bf16[512,1280]{1,0:T(8,128)(2,1)S(1)}, u32[]{:S(2)}, u32[]{:S(2)}) collective-permute-start(bf16[512,1280]{1,0:T(8,128)(2,1)S(1)} %fusion.56), channel_id=1, source_target_pairs={{0,8},{4,12},{1,9},{5,13},{2,10},{6,14},{3,11},{7,15}} | collective-permute-start | bytes 3932168 | tf_op jit(solution)/shard_map/ppermute | solution.py:32
  1012.3 69.9 %collective-permute-start.96 = (bf16[512,1280]{1,0:T(8,128)(2,1)}, bf16[512,1280]{1,0:T(8,128)(2,1)S(1)}, u32[]{:S(2)}, u32[]{:S(2)}) collective-permute-start(bf16[512,1280]{1,0:T(8,128)(2,1)} %get-tuple-element.189), channel_id=1, source_target_pairs={{0,4},{4,0},{8,12},{12,8},{16,20},{20,16},{24,28},{28,24},{1,5},{5... | collective-permute-start | bytes 3932168 | tf_op jit(solution)/shard_map/ppermute | solution.py:23
  1015.6 53.7 %collective-permute-start.105 = (bf16[512,1280]{1,0:T(8,128)(2,1)S(1)}, bf16[512,1280]{1,0:T(8,128)(2,1)S(1)}, u32[]{:S(2)}, u32[]{:S(2)}) collective-permute-start(bf16[512,1280]{1,0:T(8,128)(2,1)S(1)} %add_convert_fusion.1), channel_id=1, source_target_pairs={{8,0},{12,4},{16,8},{20,12},{24,16},{28,20},{9,1},{13,5},{17,9},{2... | collective-permute-start | bytes 3932168 | tf_op jit(solution)/shard_map/ppermute | solution.py:32
  1025.3 44.0 %collective-permute-start.104 = (bf16[512,1280]{1,0:T(8,128)(2,1)S(1)}, bf16[512,1280]{1,0:T(8,128)(2,1)S(1)}, u32[]{:S(2)}, u32[]{:S(2)}) collective-permute-start(bf16[512,1280]{1,0:T(8,128)(2,1)S(1)} %add_convert_fusion.2), channel_id=1, source_target_pairs={{0,8},{4,12},{8,16},{12,20},{16,24},{20,28},{1,9},{5,13},{9,17},{1... | collective-permute-start | bytes 3932168 | tf_op jit(solution)/shard_map/ppermute | solution.py:32
  (221 other events, 3849.7 us)

commit v2 on v1

v2 whole, which is shorter than its diff:
```python
import jax
import jax.numpy as jnp
from jax import lax
from jax.experimental import pallas as pl
from jax.experimental.pallas import tpu as pltpu
from jax.sharding import PartitionSpec as P

HEAD_SIZE = 128
TOPK = 7
EPSILON = 1e-06
MASKED = -1e30
LANES = 128
F32 = jnp.float32
BF16 = jnp.bfloat16
VMEM_LIMIT = 58 * 1024 * 1024


def after(values, *others):
    return lax.optimization_barrier((values, others))[0]


def core_swap(x):
    return lax.ppermute(x, "dp", [(d, d ^ 1) for d in range(lax.axis_size("dp"))])


def fsdp_swap(x, bit):
    return lax.ppermute(x, "fsdp", [(f, f ^ bit) for f in range(lax.axis_size("fsdp"))])


def positions():
    return lax.axis_size("dp") // 2


def line_fetch(x):
    n = positions()
    pairs = lambda r: [
        (2 * ((p + r) % n) + c, 2 * p + c) for p in range(n) for c in range(2)
    ]
    return [x] + [lax.ppermute(x, "dp", pairs(r)) for r in range(1, n)]


def line_return(slots, kind=BF16):
    n = positions()
    pairs = lambda r: [
        (2 * p + c, 2 * ((p + r) % n) + c) for p in range(n) for c in range(2)
    ]
    return [slots[0]] + [lax.ppermute(slots[r].astype(kind), "dp", pairs(r)) for r in range(1, n)]


def add_all(parts):
    return sum(a.astype(F32) for a in parts)


def line_send(x, step, first, last):
    pairs = [(2 * p + c, 2 * (p + step) + c) for p in range(first, last + 1) for c in range(2)]
    return lax.ppermute(x, "dp", pairs)


class LineGather:
    def __init__(self, x):
        self.right, self.left = [x], [x]
        self.n = positions()

    def step(self, *others):
        s = len(self.right)
        a, b = after((self.right[-1], self.left[-1]), *others)
        self.right.append(line_send(a, 1, s - 1, self.n - 2))
        self.left.append(line_send(b, -1, 1, self.n - s))
        return self.right[-1], self.left[-1]

    def slot(self, r):
        if r == 0:
            return self.right[0]
        p = lax.axis_index("dp") // 2
        return jnp.where(p + r < self.n, self.left[r], self.right[self.n - r])


class LineScatter:
    def __init__(self):
        self.right = self.left = None
        self.s = 0
        self.n = positions()

    def step(self, to_right, to_left, *others):
        self.s += 1
        s = self.s
        a, b = to_right.astype(F32), to_left.astype(F32)
        if self.right is not None:
            a, b = a + self.right.astype(F32), b + self.left.astype(F32)
        a, b = after((a.astype(BF16), b.astype(BF16)), *others)
        self.sent = a, b
        self.right = line_send(a, 1, 0, s - 1)
        self.left = line_send(b, -1, self.n - s, self.n - 1)
        return self.right, self.left

    def total(self, own):
        if self.right is None:
            return own.astype(F32)
        return own.astype(F32) + self.right.astype(F32) + self.left.astype(F32)


def cube_size():
    return max(lax.axis_size("fsdp").bit_length() - 1, 1)


def cube_bit(part, j):
    return 1 << ((part + j) % cube_size())


def cube_masks(part):
    masks = [0]
    for j in range(cube_size()):
        masks = masks + [m ^ cube_bit(part, j) for m in masks]
    return masks


def add_pair(pair):
    return pair[0].astype(F32) + pair[1].astype(F32)


def dense_parts(slots):
    k = cube_size()
    return [jnp.concatenate(slots[part::k], axis=0) for part in range(k)]


class DenseGather:
    def __init__(self, slots):
        self.held = dense_parts(slots)
        self.j = 0

    def exchange(self, *others):
        self.held = after(self.held, *others)
        self.got = [fsdp_swap(a, cube_bit(part, self.j)) for part, a in enumerate(self.held)]
        self.j += 1
        return self.got

    def join(self):
        self.held = [jnp.concatenate(pair, axis=0) for pair in zip(self.held, self.got)]

    def swap_held(self, *others):
        self.first = core_swap(after(jnp.concatenate(self.held, axis=0), *others))
        return self.first

    def swap_got(self, *others):
        self.second = core_swap(after(jnp.concatenate(self.got, axis=0), *others))
        return self.second

    def swap_all(self, *others):
        both = jnp.concatenate(self.held + self.got, axis=0)
        both = core_swap(after(both, *others))
        size = sum(a.shape[0] for a in self.held)
        self.first, self.second = both[:size], both[size:]
        return both

    def pieces(self):
        own, other, at = [], [], 0
        for a, b in zip(self.held, self.got):
            size = a.shape[0]
            own += [a, b]
            other += [self.first[at : at + size], self.second[at : at + size]]
            at += size
        return own + other

    def columns(self, start, stop):
        return jnp.concatenate([a[:, start:stop] for a in self.pieces()], axis=0)


def block_order():
    n = positions()
    d, f = lax.axis_index("dp"), lax.axis_index("fsdp")
    order = []
    for cx in range(2):
        for part in range(cube_size()):
            for m in cube_masks(part):
                for r in range(n)[part :: cube_size()]:
                    device = ((d // 2 + r) % n) * 2 + (d % 2 ^ cx)
                    order.append(device * lax.axis_size("fsdp") + (f ^ m))
    return jnp.stack(order)


class DenseScatter:
    def __init__(self, own, other, kind=BF16):
        self.own, self.other, self.kind = own, other, kind

    def swap(self, *others):
        other = after(self.other.astype(self.kind), *others)
        self.got = core_swap(other)
        return self.got

    def cut(self, extra):
        total = add_pair((self.own, self.got))
        if extra is not None:
            total = jnp.concatenate([total, add_pair((extra.own, extra.got))], axis=1)
        n, k = positions(), cube_size()
        rows = total.shape[0] // (n * 2**k)
        self.parts, at = [], 0
        for part in range(k):
            size = 2**k * len(range(n)[part::k]) * rows
            self.parts.append(total[at : at + size])
            at += size
        self.rows = rows

    def exchange(self, i, *others, extra=None):
        j = cube_size() - 1 - i
        if i > 0:
            self.parts = [add_pair(pair) for pair in self.pairs]
        else:
            self.cut(extra)
        halves = [x.shape[0] // 2 for x in self.parts]
        sent = after([x[h:].astype(self.kind) for x, h in zip(self.parts, halves)], *others)
        self.pairs = [
            (x[:h], fsdp_swap(y, cube_bit(part, j)))
            for part, (x, y, h) in enumerate(zip(self.parts, sent, halves))
        ]
        return [b for _, b in self.pairs]

    def line(self, *others):
        n, k = positions(), cube_size()
        slots = [None] * n
        for part, pair in enumerate(self.pairs):
            got = add_pair(pair)
            for i, r in enumerate(range(n)[part::k]):
                slots[r] = got[i * self.rows : (i + 1) * self.rows]
        sent = after([x.astype(self.kind) for x in slots[1:]], *others)
        self.arrived = line_return([slots[0]] + sent, self.kind)
        return self.arrived[1:]

    def total(self):
        return add_all(self.arrived)


def dot(a, b, dims):
    return lax.dot_general(a, b, (dims, ((), ())), preferred_element_type=F32)


NN = ((1,), (0,))
NT = ((1,), (1,))
TN = ((0,), (0,))


def turn(x, cosine, sine):
    return x * cosine + pltpu.roll(x, HEAD_SIZE // 2, 1) * sine


def causal_scores(q, k):
    scores = dot(k, q, NT) * (HEAD_SIZE ** (-0.5))
    key = lax.broadcasted_iota(jnp.int32, scores.shape, 0)
    query = lax.broadcasted_iota(jnp.int32, scores.shape, 1)
    return jnp.where(key <= query, scores, MASKED)


def cost(flops, transcendentals=0):
    return pl.CostEstimate(
        flops=int(flops), transcendentals=int(transcendentals), bytes_accessed=int(flops // 400)
    )


def attention_forward_kernel(qp, kp, vp, cosine, sine, q_out, k_out, v_out, mixed_out, lse_out):
    q = turn(qp[...], cosine[...], sine[...]).astype(BF16)
    k = turn(kp[...], cosine[...], sine[...]).astype(BF16)
    v = vp[...].astype(BF16)
    q_out[...] = q
    k_out[...] = k
    v_out[...] = v
    scores = causal_scores(q, k)
    peak = jnp.max(scores, axis=0, keepdims=True)
    expo = jnp.exp(scores - peak)
    totals = jnp.sum(expo, axis=0, keepdims=True)
    lse_out[0] = peak + jnp.log(totals)
    probability = (expo * (1.0 / totals)).astype(BF16)
    mixed_out[...] = dot(probability, v, TN).astype(BF16)


def attention_forward(projected, cosine, sine):
    length = projected.shape[0]
    width = projected.shape[1] // 3
    heads = width // HEAD_SIZE
    block = (length, HEAD_SIZE)
    table = pl.BlockSpec(block, lambda h: (0, 0))
    column = pl.BlockSpec(block, lambda h: (0, h))
    rows = jax.ShapeDtypeStruct((length, width), BF16)
    return pl.pallas_call(
        attention_forward_kernel,
        grid=(heads,),
        in_specs=[
            column,
            pl.BlockSpec(block, lambda h: (0, heads + h)),
            pl.BlockSpec(block, lambda h: (0, 2 * heads + h)),
            table,
            table,
        ],
        out_specs=[column] * 4 + [pl.BlockSpec((1, 1, length), lambda h: (h, 0, 0))],
        out_shape=[rows] * 4 + [jax.ShapeDtypeStruct((heads, 1, length), F32)],
        compiler_params=pltpu.CompilerParams(vmem_limit_bytes=VMEM_LIMIT),
        cost_estimate=cost(14e9),
        name="attention_forward",
    )(projected, projected, projected, cosine, sine)


def attention_backward_kernel(q_in, k_in, v_in, d_in, lse, cosine, sine, dq_out, dk_out, dv_out):
    q, k, v, d = q_in[...], k_in[...], v_in[...], d_in[...]
    scale = HEAD_SIZE ** (-0.5)
    probability = jnp.exp(causal_scores(q, k) - lse[0])
    dv_out[...] = dot(probability.astype(BF16), d, NN).astype(BF16)
    prob_cot = dot(v, d, NT)
    row_dot = jnp.sum(probability * prob_cot, axis=0, keepdims=True)
    score_cot = (probability * (prob_cot - row_dot)).astype(BF16)
    dk = dot(score_cot, q, NN) * scale
    dq = dot(score_cot, k, TN) * scale
    dq_out[...] = turn(dq, cosine[...], -sine[...]).astype(BF16)
    dk_out[...] = turn(dk, cosine[...], -sine[...]).astype(BF16)


def attention_backward(q, k, v, mixed_cot, lse, cosine, sine):
    length, width = q.shape
    heads = width // HEAD_SIZE
    block = (length, HEAD_SIZE)
    table = pl.BlockSpec(block, lambda h: (0, 0))
    column = pl.BlockSpec(block, lambda h: (0, h))
    return pl.pallas_call(
        attention_backward_kernel,
        grid=(heads,),
        in_specs=[column] * 4
        + [pl.BlockSpec((1, 1, length), lambda h: (h, 0, 0)), table, table],
        out_specs=[column] * 3,
        out_shape=[jax.ShapeDtypeStruct((length, width), BF16)] * 3,
        compiler_params=pltpu.CompilerParams(vmem_limit_bytes=VMEM_LIMIT),
        cost_estimate=cost(15e9),
        name="attention_backward",
    )(q, k, v, mixed_cot, lse, cosine, sine)


def silu_parts(gate_value):
    sigmoid_value = jax.nn.sigmoid(gate_value)
    return (gate_value * sigmoid_value, sigmoid_value * (1.0 + gate_value * (1.0 - sigmoid_value)))


def expert_kernel(
    first, x_own, x_other, c_own, c_other, router, weights,
    x_out, c_out, h_out, g_out, u_out, cot_own, cot_other, out_own, out_other, router_out,
    picks, xs, cs, x_cots, ys, shares, backs,
):
    length, width = x_own.shape
    capacity = x_out.shape[1] // 2
    experts = router.shape[0]
    local = pl.num_programs(0)
    count = picks.shape[1] // capacity
    step = pl.program_id(0)
    sources = ((x_own, c_own), (x_other, c_other))
    w_gate, w_up, w_down = (weights[:, 0, i].reshape(-1, width) for i in range(3))
    expert_row = lax.broadcasted_iota(jnp.int32, (experts, length), 0)
    slot_row = lax.broadcasted_iota(jnp.int32, (capacity, length), 0).astype(F32)

    def row_of(table, index):
        return jnp.sum(jnp.where(expert_row == index, table, 0.0), axis=0, keepdims=True)

    @pl.when(step == 0)
    def _():
        for at, (x_ref, c_ref) in enumerate(sources):
            ranks = c_ref[length : length + experts, :length].astype(F32)
            logits = dot(router[...], x_ref[...], NT)
            expo = jnp.exp(logits - jnp.max(logits, axis=0, keepdims=True))
            shares[at] = expo * (1.0 / jnp.sum(expo, axis=0, keepdims=True))
            pick = jnp.concatenate(
                [jnp.where(slot_row == row_of(ranks, first[0] + e), 1.0, 0.0) for e in range(count)],
                axis=0,
            ).astype(BF16)
            picks[at] = pick
            x = dot(pick, x_ref[...], NN).astype(BF16)
            c = dot(pick, c_ref[:length, :], NN).astype(BF16)
            for e in range(count):
                low, high = e * capacity, (e + 1) * capacity
                xs[e, at * capacity : (at + 1) * capacity, :] = x[low:high]
                cs[e, at * capacity : (at + 1) * capacity, :] = c[low:high]

    x = xs[step]
    c = cs[step]
    gate_columns = []
    for at, (_, c_ref) in enumerate(sources):
        ranks = c_ref[length : length + experts, :length].astype(F32)
        chosen = jnp.where(ranks >= 0.0, shares[at], 0.0)
        gate = row_of(chosen, first[0] + step) / jnp.sum(chosen, axis=0, keepdims=True)
        pick = picks[at, pl.ds(pl.multiple_of(step * capacity, 32), capacity), :].astype(F32)
        gate_columns.append(jnp.sum(pick * gate, axis=1, keepdims=True))
    gates = jnp.concatenate(gate_columns, axis=0)
    x_out[0] = x
    c_out[0] = (gates * c.astype(F32)).astype(BF16)
    gate_value = dot(x, w_gate, NT)
    up_value = dot(x, w_up, NT)
    raw_cot = dot(c, w_down, NT)
    active, slope = silu_parts(gate_value)
    hidden16 = (active * up_value).astype(BF16)
    hidden = hidden16.astype(F32)
    gate_cot = jnp.sum(raw_cot * hidden, axis=1, keepdims=True)
    hidden_cot = gates * raw_cot
    h_out[0] = hidden16
    g16 = (hidden_cot * up_value * slope).astype(BF16)
    u16 = (hidden_cot * active).astype(BF16)
    g_out[0] = g16
    u_out[0] = u16
    x_cot = (dot(g16, w_gate, NN) + dot(u16, w_up, NN)).astype(BF16)
    y = dot((gates * hidden).astype(BF16), w_down, NN).astype(BF16)
    for at in range(2):
        low, high = at * capacity, (at + 1) * capacity
        rows = pl.ds(pl.multiple_of(step * capacity, 32), capacity)
        x_cots[at, rows, :] = x_cot[low:high]
        ys[at, rows, :] = y[low:high]
        pick = picks[at, rows, :].astype(F32)
        backs[at, step] = jnp.sum(pick * gate_cot[low:high], axis=0, keepdims=True)

    @pl.when(step == local - 1)
    def _():
        for at, (x_ref, c_ref) in enumerate(sources):
            ranks = c_ref[length : length + experts, :length].astype(F32)
            probability = shares[at]
            chosen = jnp.where(ranks >= 0.0, probability, 0.0)
            total = jnp.sum(chosen, axis=0, keepdims=True)
            direct = jnp.zeros_like(chosen)
            shift = jnp.zeros_like(total)
            for e in range(count):
                back = backs[at, e]
                shift += back * row_of(chosen, first[0] + e)
                direct += jnp.where(expert_row == first[0] + e, back / total, 0.0)
            prob_cot = jnp.where(ranks >= 0.0, direct - shift / (total * total), 0.0)
            inner = jnp.sum(prob_cot * probability, axis=0, keepdims=True)
            logit_cot = (probability * (prob_cot - inner)).astype(BF16)
            cot = dot(picks[at], x_cots[at], TN) + dot(logit_cot, router[...], TN)
            out = dot(picks[at], ys[at], TN)
            (cot_own, cot_other)[at][...] = cot.astype(BF16)
            (out_own, out_other)[at][...] = out.astype(BF16)
            part = dot(logit_cot, x_ref[...], NN)
            router_out[...] = part if at == 0 else router_out[...] + part


def expert_chunk(first, x_pair, c_pair, router, weights, capacity):
    length, width = x_pair[0].shape
    pieces, local, _, part, _ = weights.shape
    units = pieces * part
    experts = router.shape[0]
    whole = lambda shape: pl.BlockSpec(
        shape, lambda e, s: (0,) * len(shape), pipeline_mode=pl.Buffered(1)
    )
    per = lambda shape: pl.BlockSpec((1,) + shape, lambda e, s: (e,) + (0,) * len(shape))
    slots = 2 * capacity
    shape = jax.ShapeDtypeStruct
    return pl.pallas_call(
        expert_kernel,
        grid_spec=pltpu.PrefetchScalarGridSpec(
            num_scalar_prefetch=1,
            grid=(local,),
            in_specs=[
                whole((length, width)),
                whole((length, width)),
                whole(c_pair[0].shape),
                whole(c_pair[1].shape),
                whole((experts, width)),
                pl.BlockSpec((pieces, 1, 3, part, width), lambda e, s: (0, e, 0, 0, 0)),
            ],
            out_specs=[per((slots, width))] * 2
            + [per((slots, units))] * 3
            + [whole((length, width))] * 4
            + [whole((experts, width))],
            scratch_shapes=[
                pltpu.VMEM((2, local * capacity, length), BF16),
                pltpu.VMEM((local, slots, width), BF16),
                pltpu.VMEM((local, slots, width), BF16),
                pltpu.VMEM((2, local * capacity, width), BF16),
                pltpu.VMEM((2, local * capacity, width), BF16),
                pltpu.VMEM((2, experts, length), F32),
                pltpu.VMEM((2, local, 1, length), F32),
            ],
        ),
        out_shape=[shape((local, slots, width), BF16)] * 2
        + [shape((local, slots, units), BF16)] * 3
        + [shape((length, width), BF16)] * 4
        + [shape((experts, width), F32)],
        compiler_params=pltpu.CompilerParams(vmem_limit_bytes=VMEM_LIMIT),
        cost_estimate=cost(5e9 * 6 * slots * local / 768),
        name="expert_chunk",
    )(first.reshape(1), *x_pair, *c_pair, router, weights)


def expert_weights_kernel(*refs):
    *inputs, out = refs
    n = len(inputs) // 5
    x, c, h, g, u = (inputs[i * n : (i + 1) * n] for i in range(5))
    for i, (left, right) in enumerate(((g, x), (u, x), (h, c))):

        @pl.when(pl.program_id(1) == i)
        def _():
            rows = [jnp.concatenate([a[0] for a in side], axis=0) for side in (left, right)]
            total = dot(*rows, TN)
            out[:, 0, 0] = total.astype(BF16).reshape(out.shape[0], out.shape[3], out.shape[4])


def expert_weight_grads(chunks, pieces):
    arrays = [a[i] for i in range(5) for a in chunks]
    local, _, width = chunks[0][0].shape
    units = chunks[0][2].shape[2]
    part = units // pieces
    slots = sum(a[0].shape[1] for a in chunks)
    return pl.pallas_call(
        expert_weights_kernel,
        grid=(local, 3),
        in_specs=[pl.BlockSpec((1,) + a.shape[1:], lambda e, i: (e, 0, 0)) for a in arrays],
        out_specs=pl.BlockSpec((pieces, 1, 1, part, width), lambda e, i: (0, e, i, 0, 0)),
        out_shape=jax.ShapeDtypeStruct((pieces, local, 3, part, width), BF16),
        compiler_params=pltpu.CompilerParams(vmem_limit_bytes=VMEM_LIMIT),
        cost_estimate=cost(2 * 6 * local * slots * units * width),
        name="expert_weights",
    )(*arrays)


def split_matmul(values, matrix, dims):
    high = values.astype(BF16)
    low = (values - high.astype(F32)).astype(BF16)
    return dot(high, matrix, dims) + dot(low, matrix, dims)


def exact_matmul(values, matrix, dims):
    return lax.dot_general(
        values, matrix.astype(F32), (dims, ((), ())),
        precision=lax.Precision.HIGHEST, preferred_element_type=F32,
    )


def shards(
    tokens,
    out_cotangent,
    assignment,
    norm_gains,
    attention_weights,
    router_weights,
    shared_weights,
    expert_weights,
):
    length, width = tokens.shape
    rows = attention_weights.shape[0]
    ranks = lax.axis_size("dp")
    local = expert_weights.shape[0]
    experts = local * ranks
    capacity = length * 6 // experts
    units = shared_weights.shape[2]

    n, k = positions(), cube_size()
    half = width // 2
    halves = (slice(0, half), slice(half, width))

    small = jnp.concatenate([norm_gains, router_weights], axis=1)
    small = jnp.pad(small, ((0, 0), (0, LANES - small.shape[1])))
    packed_in = jnp.concatenate([attention_weights[:, :3].reshape(rows, 3 * width), small], axis=1)
    packed_out = attention_weights[:, 3]
    turned = jnp.transpose(expert_weights, (0, 1, 3, 2))
    slots_in = line_fetch(packed_in)

    hot = jnp.sum(
        (assignment[:, :, None] == jnp.arange(experts)[None, None, :]).astype(F32), axis=1
    )
    before = (jnp.arange(length)[:, None] < jnp.arange(length)[None, :]).astype(BF16)
    earlier = dot(hot.astype(BF16), before, TN)
    places = jnp.where(hot.T > 0, jnp.minimum(earlier, float(capacity)), -1.0).astype(BF16)
    places = jnp.pad(places, ((0, 0), (0, width - length)))
    sent = jnp.concatenate([out_cotangent, places], axis=0)

    owner = block_order()
    true_row = (owner[:, None] * rows + jnp.arange(rows)[None, :]).reshape(width)
    order = (jnp.arange(width)[:, None] == true_row[None, :]).astype(BF16)
    tokens_float = tokens.astype(F32)
    tokens_rel = dot(tokens, order, NN).astype(BF16)
    c_rel = dot(out_cotangent, order, NN).astype(BF16)
    root_one = lax.rsqrt(jnp.mean(tokens_float * tokens_float, axis=-1, keepdims=True) + EPSILON)
    position = jnp.arange(length).astype(F32)
    frequency = 10000.0 ** (-jnp.arange(HEAD_SIZE // 2).astype(F32) * (2.0 / HEAD_SIZE))
    angle = position[:, None] * frequency[None, :]
    cosine = jnp.concatenate([jnp.cos(angle), jnp.cos(angle)], axis=1)
    sine = jnp.concatenate([-jnp.sin(angle), jnp.sin(angle)], axis=1)
    done = [slots_in, sent, order, tokens_rel, c_rel, root_one, cosine, sine]

    gather_in = DenseGather(after(slots_in, *done))
    line_out = LineGather(packed_out)
    for j in range(k):
        if j > 0:
            gather_in.join()
        got = gather_in.exchange(*done)
        swapped = [gather_in.swap_held(*done)] if j == k - 1 else []
        going = []
        while len(line_out.right) < n and (j == k - 1 or len(line_out.right) < 2):
            going = line_out.step(*(done if len(line_out.right) < 3 else []))
        done = [got, swapped, going]
    swapped = gather_in.swap_got(*done)
    slots_out = [line_out.slot(r) for r in range(n)]
    gather_out = DenseGather(slots_out)
    gather_out.exchange(*done)
    cots = LineGather(sent)
    going = cots.step(*done)
    project = gather_in.columns(0, 3 * width)
    small_full = gather_in.columns(3 * width, 3 * width + LANES)

    small_true = dot(order, small_full, NN)
    gain_one = small_full[:, 0].astype(F32)
    gain_two = small_true[:, 1]
    router = small_true[:, 2 : 2 + experts].T.astype(BF16)
    unit_one = tokens_rel.astype(F32) * root_one
    normed_one = (unit_one * gain_one).astype(BF16)
    routed = lax.all_gather(after(turned, *done), "fsdp", axis=0)
    projected = dot(normed_one, project, NN)
    done = [swapped, gather_out.got, projected]
    projected = after(projected, *done)
    for j in range(1, k):
        gather_out.join()
        projected = after(projected, *gather_out.held)
        gather_out.exchange(*done)
        done = [gather_out.got]
    query, key, value, mixed, lse = attention_forward(projected, cosine, sine)
    done = [gather_out.got, mixed, going]

    swapped = gather_out.swap_all(*done)
    if len(cots.right) < n:
        cots.step(*done)
    mixed_rel = dot(after(mixed, *done), order, NN).astype(BF16)
    out_full = gather_out.columns(0, width)
    hidden_res = tokens_float + dot(mixed_rel, out_full, NN)
    root_two = lax.rsqrt(jnp.mean(hidden_res * hidden_res, axis=-1, keepdims=True) + EPSILON)
    unit_two = hidden_res * root_two
    normed_two = (unit_two * gain_two).astype(BF16)
    shared_full = lax.all_gather(
        after(shared_weights.reshape(rows, 3 * units), normed_two), ("dp", "fsdp"), axis=0, tiled=True
    )
    done = [normed_two]

    rows_two = LineGather(normed_two)
    me = lax.axis_index("dp")
    chunks, x_pairs, c_pairs = [None] * n, [None] * n, [None] * n

    def pair_up(r, *others):
        x, c = after((rows_two.slot(r), cots.slot(r)), *others)
        x_pairs[r], c_pairs[r] = (x, core_swap(x)), (c, core_swap(c))
        return x_pairs[r], c_pairs[r]

    def chunk(r, *others):
        x, c = after((x_pairs[r], c_pairs[r]), *others)
        chunks[r] = expert_chunk((me * local).astype(jnp.int32), x, c, router, routed, capacity)
        return chunks[r]

    def shared_part(*others):
        rows_, c_ = after((normed_two, out_cotangent), *others)
        gate_up = dot(rows_, shared_full[:, : 2 * units], NN)
        active, slope = silu_parts(gate_up[:, :units])
        up = gate_up[:, units:]
        hidden = (active * up).astype(BF16)
        cot = dot(c_, shared_full[:, 2 * units :], NN)
        gate_up_cot = jnp.concatenate(
            [(cot * up * slope).astype(BF16), (cot * active).astype(BF16)], axis=1
        )
        rel = dot(rows_, order, NN).astype(BF16)
        grad = [
            jnp.concatenate(
                [dot(rel[:, cut], gate_up_cot, TN).astype(BF16),
                 dot(c_rel[:, cut], hidden, TN).astype(BF16)], axis=1,
            )
            for cut in halves
        ]
        out = dot(hidden, shared_full[:, 2 * units :], NT)
        return out, dot(gate_up_cot, shared_full[:, : 2 * units], NT), grad

    for at in range(n - 1):
        going = [rows_two.step(*done), cots.right[-1], cots.left[-1]]
        if at > 0 and len(cots.right) < n:
            going.append(cots.step(*done))
        beside = []
        if at == n - 4:
            beside.append(pair_up(0, *done))
        elif at == n - 3:
            beside.append(chunk(0, *done)[9])
        elif at == n - 2:
            pair_up(n // 2, *done)
            beside.append(chunk(n // 2, *done)[9])
        done = [going, beside]

    early = sorted({1, n - 1})
    late = [r for r in range(n) if r not in early and chunks[r] is None]
    back, back_slots = LineScatter(), [None] * n
    out_sums, out_slots = LineScatter(), [None] * n

    def own_part(r, *others):
        back_slots[r] = add_pair((chunks[r][5], core_swap(after(chunks[r][6], *others))))

    def out_part(r, *others):
        got = core_swap(after(chunks[r][8], *others))
        out_slots[r] = add_pair((chunks[r][7], got))
        return got

    done = [pair_up(early[0], *done)]
    for at, r in enumerate(early):
        moved = [pair_up(q, *done) for q in (early + late)[at + 1 :][:1]]
        done = [chunk(r, *done)[9], moved]
    for r in range(n):
        if chunks[r] is not None:
            own_part(r)

    results = {}
    for s in range(1, n):
        going = back.step(back_slots[n - s], back_slots[s], *done)
        held = back.sent
        made = []
        wanted = [r for r in late if r in (s + 1, n - s - 1)]
        for r in [r for r in range(n) if chunks[r] is not None and out_slots[r] is None][:2]:
            made.append(out_part(r, *held))
        for r in wanted:
            late.remove(r)
            pair_up(r, *held)
            made.append(chunk(r, *held)[9])
        if not late and not wanted:
            if "shared" not in results:
                results["shared"] = shared_part(*held)
                scatter = DenseScatter(*results["shared"][2])
                made.append(results["shared"])
            elif "experts" not in results:
                weights = expert_weight_grads(after(chunks, *held), lax.axis_size("fsdp"))
                results["experts"] = lax.psum_scatter(weights, "fsdp", scatter_dimension=0)
                made += [weights, scatter.swap(*held)]
            elif "exchange" not in results:
                results["exchange"] = scatter.exchange(0, *held)
                made.append(results["exchange"])
        done = [going, made]
        for r in wanted:
            own_part(r, *done)
    for r in range(n):
        if out_slots[r] is None:
            out_part(r, *done)
    shared_out, shared_back, _ = results["shared"]
    expert_sum = results["experts"]
    back_sum = back.total(back_slots[0])
    router_part = sum(a[9] for a in chunks)

    going_out = out_sums.step(out_slots[n - 1], out_slots[1], *done) if n > 1 else []
    moved = [scatter.exchange(i, *done) for i in range(1, k)]
    cotangent = out_cotangent.astype(F32)
    normed_two_cot = back_sum + shared_back
    scaled = normed_two_cot * gain_two
    gain_two_grad = jnp.sum(normed_two_cot * unit_two, axis=0)
    hidden_cot = cotangent + root_two * (
        scaled - unit_two * jnp.mean(scaled * unit_two, axis=-1, keepdims=True)
    )
    attn_cot = hidden_cot.astype(BF16)
    mixed_cot = dot(dot(attn_cot, out_full, NT).astype(BF16), order, NT).astype(BF16)
    cot_parts = attention_backward(query, key, value, mixed_cot, lse, cosine, sine)
    done = [cot_parts, going_out, moved]

    cot_parts = after(cot_parts, *done)
    going_out = out_sums.step(out_slots[n - 2], out_slots[2], *done) if n > 2 else []
    projected_cot = jnp.concatenate(cot_parts, axis=1)
    in_grad = [dot(normed_one[:, cut], projected_cot, TN).astype(BF16) for cut in halves[::-1]]
    in_scatter = DenseScatter(in_grad[1], in_grad[0])
    swap_in = in_scatter.swap()
    out_grad = [dot(after(mixed_rel, *in_grad)[:, cut], attn_cot, TN).astype(BF16) for cut in halves]
    out_scatter = DenseScatter(*out_grad)
    swap_out = out_scatter.swap()
    normed_one_cot = dot(after(projected_cot, *in_grad), project, NT)
    scaled_one = normed_one_cot * gain_one
    gain_one_grad = jnp.sum(normed_one_cot * unit_one, axis=0)
    true_part = exact_matmul(
        jnp.concatenate([gain_two_grad[None, :], router_part], axis=0), order, NN
    )
    small_grad = jnp.concatenate([gain_one_grad[None, :], true_part], axis=0)
    small_grad = jnp.pad(small_grad, ((0, LANES - small_grad.shape[0]), (0, 0))).T
    small_scatter = DenseScatter(small_grad[:half], small_grad[half:], F32)
    swap_small = small_scatter.swap()
    moved = []
    done = [swap_in, swap_small, swap_out, scaled_one, going_out, moved]

    for i in range(k):
        going = [in_scatter.exchange(i, *done, extra=small_scatter if i == 0 else None)]
        if i == 0:
            token_part = after(root_one, *done) * (
                scaled_one - unit_one * jnp.mean(scaled_one * unit_one, axis=-1, keepdims=True)
            )
            token_gradient = hidden_cot + split_matmul(token_part, order, NT)
            going += [token_gradient]
            for s in range(3, n):
                going_out = out_sums.step(out_slots[n - s], out_slots[s], *done)
            going.append(going_out)
        elif i == 1:
            going += [scatter.line(*done), expert_sum]
        done = [going]
    last = [in_scatter.line(*done)]
    last += [out_scatter.exchange(i, *done) for i in range(k)]
    out_scatter.line()
    shared_gradient = scatter.total().reshape(rows, 3, units)
    in_total = in_scatter.total()
    in_gradient = in_total[:, : 3 * width].reshape(rows, 3, width)
    out_gradient = out_scatter.total()
    attention_gradient = jnp.concatenate([in_gradient, out_gradient[:, None, :]], axis=1)
    small_gradient = in_total[:, 3 * width :]
    out_sum = out_sums.total(out_slots[0])
    block_output = (hidden_res + shared_out + out_sum).astype(BF16)
    expert_gradient = jnp.transpose(expert_sum, (0, 1, 3, 2)).astype(F32)
    return (
        block_output,
        token_gradient,
        small_gradient[:, :2],
        attention_gradient,
        small_gradient[:, 2 : 2 + experts],
        shared_gradient,
        expert_gradient,
    )


def solution(mesh):
    both = ("dp", "fsdp")
    return jax.shard_map(
        shards,
        mesh=mesh,
        in_specs=(
            P(both, None),
            P(both, None),
            P(both, None),
            P(both, None),
            P(both, None, None),
            P(both, None),
            P(both, None, None),
            P("dp", None, None, "fsdp"),
        ),
        out_specs=(
            P(both, None),
            P(both, None),
            P(both, None),
            P(both, None, None),
            P(both, None),
            P(both, None, None),
            P("dp", None, None, "fsdp"),
        ),
        check_vma=False,
    )
```

time: 1110 us -> 781 us (0.70)
  waiting for transfers between devices: 469 us -> 235 us
  starting transfers between devices: 226 us -> 139 us
  Pallas kernels: 195 us -> 178 us
  between operations: 4 us -> 17.8 us
    ppermute x52 -> x20, waiting for transfers between devices: 227 us -> 67.9 us  [fsdp_swap(): lax.ppermute(x, 'fsdp', [(f, f ^ bit) for f in range(lax.axis_size('fsdp'...]
    ppermute x66 -> x30, waiting for transfers between devices: 234 us -> 121 us  [line_send(): return lax.ppermute(x, 'dp', pairs)]
    ppermute x66 -> x30, starting transfers between devices: 166 us -> 79.6 us  [line_send(): return lax.ppermute(x, 'dp', pairs)]
    ppermute x0 -> x12, starting transfers between devices: none -> 31.5 us  [the longest x9 25.4 us: line_return(): lax.ppermute(slots[r].astype(kind), 'dp', pairs(r))]
    ppermute x0 -> x12, waiting for transfers between devices: none -> 30.1 us  [the longest x9 15.6 us: line_return(): lax.ppermute(slots[r].astype(kind), 'dp', pairs(r))]
    ppermute x52 -> x20, starting transfers between devices: 51.2 us -> 23.7 us  [fsdp_swap(): lax.ppermute(x, 'fsdp', [(f, f ^ bit) for f in range(lax.axis_size('fsdp'...]
    another operation x13 -> x4, other arithmetic: 25.7 us -> 6.41 us  [the longest x3 12.5 us: shards(): routed = jnp.stack(routed)]
    convert_element_type x16 -> x12, other arithmetic: 11.2 us -> 23.9 us  [the longest x10 20 us: step(): a, b = after((a.astype(BF16), b.astype(BF16)), *others)]
  transfers between devices with their start and end apart: 162 -> 88, of which waited for: 68 -> 32; matrix products, arithmetic and copies ran while one was open for 14% -> 24% of each run, Pallas kernels for 17% -> 23%
where the time goes in v2:
time: 781 us; the launch traced here: 772 us
  waiting for transfers between devices  235 us (30%)
  Pallas kernels  178 us (23%)
  starting transfers between devices  139 us (18%)
  matrix products  89.8 us (11%)
  other arithmetic  67.1 us (9%)
  local copies, waits for them, and re-layouts  45.5 us (6%)
  between operations  17.8 us (2%)
    ppermute x30, waiting for transfers between devices, line_send(): return lax.ppermute(x, 'dp', pairs)  121 us
    pallas_call x4, Pallas kernels, expert_chunk(): pl.pallas_call(expert_kernel, grid_spec=pltpu.PrefetchScalarGridSpec(num_...  117 us
    dot_general x24, matrix products, dot(): return lax.dot_general(a, b, (dims, ((), ())), preferred_element_type=F32)  87.7 us
    ppermute x30, starting transfers between devices, line_send(): return lax.ppermute(x, 'dp', pairs)  79.6 us
    ppermute x20, waiting for transfers between devices, fsdp_swap(): lax.ppermute(x, 'fsdp', [(f, f ^ bit) for f in range(lax.axis_size('fsdp'...  67.9 us
    pallas_call x1, Pallas kernels, expert_weight_grads(): pl.pallas_call(expert_weights_kernel, grid=(local, 3), in_specs=[pl.Block...  33.5 us
    unnamed x231, local copies, waits for them, and re-layouts  30.9 us
    ppermute x9, starting transfers between devices, line_return(): lax.ppermute(slots[r].astype(kind), 'dp', pairs(r))  25.4 us
  transfers between devices with their start and end apart: 88, of which 32 were waited for; matrix products, arithmetic and copies ran while one was open for 24% of the time, Pallas kernels for 23%

profile of v2, /device:TPU:0, one launch (start us, length us, event | category | flops | bytes accessed | tf_op | source)
XLA Modules:
  0.0 772.3 jit_solution(5670853329318689781)
XLA Ops:
  28.4 14.4 %collective-permute-done.1 = bf16[40,3968]{1,0:T(8,128)(2,1)S(1)} collective-permute-done((bf16[40,3968]{1,0:T(8,128)(2,1)S(1)}, bf16[40,3968]{1,0:T(8,128)(2,1)S(1)}, u32[]{:S(2)}, u32[]{:S(2)}) %collective-permute-start.1) | collective-permute-done | bytes 317472 | tf_op jit(solution)/shard_map/ppermute | solution.py:39
  50.4 7.8 %collective-permute-done.3 = bf16[80,3968]{1,0:T(8,128)(2,1)S(1)} collective-permute-done((bf16[80,3968]{1,0:T(8,128)(2,1)S(1)}, bf16[80,3968]{1,0:T(8,128)(2,1)S(1)}, u32[]{:S(2)}, u32[]{:S(2)}) %collective-permute-start.3) | collective-permute-done | bytes 634912 | tf_op jit(solution)/shard_map/ppermute | solution.py:27
  66.3 7.1 collective-permute-done.11
  80.6 10.9 %collective-permute-done.7 = bf16[160,3968]{1,0:T(8,128)(2,1)S(1)} collective-permute-done((bf16[160,3968]{1,0:T(8,128)(2,1)S(1)}, bf16[160,3968]{1,0:T(8,128)(2,1)S(1)}, u32[]{:S(2)}, u32[]{:S(2)}) %collective-permute-start.7) | collective-permute-done | bytes 1269792 | tf_op jit(solution)/shard_map/ppermute | solution.py:27
  116.2 11.2 %fusion.98.qp.kp.vp = f32[512,3840]{1,0:T(8,128)} fusion(bf16[512,1280]{0,1:T(8,128)(2,1)S(1)} %multiply_convert_fusion.1, bf16[1280,3840]{1,0:T(8,128)(2,1)} %slice_dynamic-update-slice_fusion), kind=kOutput, calls=%fused_computation.252 | convolution fusion | flops 5033164800 | bytes 19005440 | tf_op jit(solution)/shard_map/dot_general | solution.py:233
  130.2 12.9 %attention_forward.1 = (bf16[512,1280]{1,0:T(8,128)(2,1)}, bf16[512,1280]{1,0:T(8,128)(2,1)}, bf16[512,1280]{1,0:T(8,128)(2,1)}, bf16[512,1280]{1,0:T(8,128)(2,1)}, f32[10,1,512]{2,1,0:T(1,128)}) custom-call(f32[512,3840]{1,0:T(8,128)} %fusion.98.qp.kp.vp, f32[512,3840]{1,0:T(8,128)} %fusion.98.qp.kp.vp, f32[512,3840]{1,0:T(8,128)} %fusion.98.qp.kp.vp, ...), custom_call_target="tpu_custom_call" | custom-call | flops 14000000000 | bytes 35000000 | tf_op jit(solution)/shard_map/attention_forward/pallas_call | solution.py:282
  163.9 9.1 %collective-permute-start.22 = (bf16[512,1280]{1,0:T(8,128)(2,1)}, bf16[512,1280]{1,0:T(8,128)(2,1)}, u32[]{:S(2)}, u32[]{:S(2)}) collective-permute-start(bf16[512,1280]{1,0:T(8,128)(2,1)} %multiply_convert_fusion.x_own), channel_id=1, source_target_pairs={{0,8},{4,12},{8,16},{12,20},{16,24},{20,28},{1,9},{5,13},{9,17},{1... | collective-permute-start | bytes 3932168 | tf_op jit(solution)/shard_map/ppermute | solution.py:56
  176.0 15.4 %collective-permute-done.25 = bf16[528,1280]{1,0:T(8,128)(2,1)} collective-permute-done((bf16[528,1280]{1,0:T(8,128)(2,1)S(1)}, bf16[528,1280]{1,0:T(8,128)(2,1)}, u32[]{:S(2)}, u32[]{:S(2)}) %collective-permute-start.25) | collective-permute-done | bytes 1351712 | tf_op jit(solution)/shard_map/ppermute | solution.py:56
  193.9 6.9 collective-permute-done.22
  200.8 18.3 %collective-permute-done.23 = bf16[512,1280]{1,0:T(8,128)(2,1)} collective-permute-done((bf16[512,1280]{1,0:T(8,128)(2,1)}, bf16[512,1280]{1,0:T(8,128)(2,1)}, u32[]{:S(2)}, u32[]{:S(2)}) %collective-permute-start.23) | collective-permute-done | bytes 1310752 | tf_op jit(solution)/shard_map/ppermute | solution.py:56
  225.3 10.0 %all-gather.6.cloned.1.call-done = bf16[8,3,224,1280]{3,2,1,0:T(8,128)(2,1)} async-done(((bf16[2,3,224,1280]{3,2,1,0:T(8,128)(2,1)}), bf16[8,3,224,1280]{3,2,1,0:T(8,128)(2,1)}) %all-gather.6.cloned.1.call-update) | async-done | bytes 13762576 | tf_op jit(solution)/shard_map/all_gather | solution.py:605
  235.3 29.0 %expert_chunk.4 = (bf16[2,384,1280]{2,1,0:T(8,128)(2,1)}, bf16[2,384,1280]{2,1,0:T(8,128)(2,1)}, bf16[2,384,896]{2,1,0:T(8,128)(2,1)}, bf16[2,384,896]{2,1,0:T(8...) custom-call(s32[1]{0:T(128)} %bitcast.37.first, ...), custom_call_target="tpu_custom_call" | custom-call | flops 30000001024 | bytes 75000000 | tf_op jit(solution)/shard_map/expert_chunk/pallas_call | solution.py:446
  264.4 18.3 %collective-permute-done.31 = bf16[528,1280]{1,0:T(8,128)(2,1)} collective-permute-done((bf16[528,1280]{1,0:T(8,128)(2,1)}, bf16[528,1280]{1,0:T(8,128)(2,1)}, u32[]{:S(2)}, u32[]{:S(2)}) %collective-permute-start.31) | collective-permute-done | bytes 1351712 | tf_op jit(solution)/shard_map/ppermute | solution.py:56
  292.2 29.4 %expert_chunk.5 = (bf16[2,384,1280]{2,1,0:T(8,128)(2,1)}, bf16[2,384,1280]{2,1,0:T(8,128)(2,1)}, bf16[2,384,896]{2,1,0:T(8,128)(2,1)}, bf16[2,384,896]{2,1,0:T(8...) custom-call(s32[1]{0:T(128)} %bitcast.37.first, ...), custom_call_target="tpu_custom_call" | custom-call | flops 30000001024 | bytes 75000000 | tf_op jit(solution)/shard_map/expert_chunk/pallas_call | solution.py:446
  321.6 13.8 %collective-permute-done.32 = bf16[512,1280]{1,0:T(8,128)(2,1)S(1)} collective-permute-done((bf16[512,1280]{1,0:T(8,128)(2,1)}, bf16[512,1280]{1,0:T(8,128)(2,1)S(1)}, u32[]{:S(2)}, u32[]{:S(2)}) %collective-permute-start.32) | collective-permute-done | bytes 1310752 | tf_op jit(solution)/shard_map/ppermute | solution.py:56
  342.2 29.5 %expert_chunk.6 = (bf16[2,384,1280]{2,1,0:T(8,128)(2,1)}, bf16[2,384,1280]{2,1,0:T(8,128)(2,1)}, bf16[2,384,896]{2,1,0:T(8,128)(2,1)}, bf16[2,384,896]{2,1,0:T(8...) custom-call(s32[1]{0:T(128)} %bitcast.37.first, ...), custom_call_target="tpu_custom_call" | custom-call | flops 30000001024 | bytes 75000000 | tf_op jit(solution)/shard_map/expert_chunk/pallas_call | solution.py:446
  373.2 29.3 %expert_chunk.7 = (bf16[2,384,1280]{2,1,0:T(8,128)(2,1)}, bf16[2,384,1280]{2,1,0:T(8,128)(2,1)}, bf16[2,384,896]{2,1,0:T(8,128)(2,1)}, bf16[2,384,896]{2,1,0:T(8...) custom-call(s32[1]{0:T(128)} %bitcast.37.first, ...), custom_call_target="tpu_custom_call" | custom-call | flops 30000001024 | bytes 75000000 | tf_op jit(solution)/shard_map/expert_chunk/pallas_call | solution.py:446
  416.6 5.4 fusion.11
  452.3 33.5 %expert_weights.1 = bf16[4,2,3,224,1280]{4,3,2,1,0:T(8,128)(2,1)} custom-call(bf16[2,384,1280]{2,1,0:T(8,128)(2,1)} %get-tuple-element.296.refs_0_, bf16[2,384,1280]{2,1,0:T(8,128)(2,1)} %get-tuple-element.297.refs_1_, bf16[2,384,1280]{2,1,0:T(8,128)(2,1)} %get-tuple-element.298.refs_2_, bf16[2,384,1280]{2,1,0:T(8,128)(2,1)} %get-tuple-element.299.refs_3_, ...), custom_call_target="tpu_custom_call" | custom-call | flops 42278584320 | bytes 105696464 | tf_op jit(solution)/shard_map/expert_weights/pallas_call | solution.py:502
  498.7 10.4 %collective-permute-start.52 = (bf16[512,1280]{1,0:T(8,128)(2,1)S(1)}, bf16[512,1280]{1,0:T(8,128)(2,1)S(1)}, u32[]{:S(2)}, u32[]{:S(2)}) collective-permute-start(bf16[512,1280]{1,0:T(8,128)(2,1)S(1)} %add_convert_fusion.6), channel_id=1, source_target_pairs={{0,8},{4,12},{8,16},{12,20},{16,24},{20,28},{1,9},{5,13},{9,17},{1... | collective-permute-start | bytes 3932168 | tf_op jit(solution)/shard_map/ppermute | solution.py:56
  512.1 17.0 %collective-permute-done.54 = bf16[160,2688]{1,0:T(8,128)(2,1)S(1)} collective-permute-done((bf16[160,2688]{1,0:T(8,128)(2,1)S(1)}, bf16[160,2688]{1,0:T(8,128)(2,1)S(1)}, u32[]{:S(2)}, u32[]{:S(2)}) %collective-permute-start.54) | collective-permute-done | bytes 860192 | tf_op jit(solution)/shard_map/ppermute | solution.py:27
  544.6 6.6 collective-permute-start.56
  559.3 7.6 fusion.24.d_in
  566.9 14.2 %attention_backward.1 = (bf16[512,1280]{1,0:T(8,128)(2,1)}, bf16[512,1280]{1,0:T(8,128)(2,1)}, bf16[512,1280]{1,0:T(8,128)(2,1)}) custom-call(bf16[512,1280]{1,0:T(8,128)(2,1)} %get-tuple-element.323.q_in, bf16[512,1280]{1,0:T(8,128)(2,1)} %get-tuple-element.324.k_in, bf16[512,1280]{1,0:T(8,128)(2,1)} %get-tuple-element.325.v_in, ...), custom_call_target="tpu_custom_call" | custom-call | flops 15000000512 | bytes 37500000 | tf_op jit(solution)/shard_map/attention_backward/pallas_call | solution.py:320
  597.6 26.3 %collective-permute-done.61 = bf16[512,1280]{1,0:T(8,128)(2,1)S(1)} collective-permute-done((bf16[512,1280]{1,0:T(8,128)(2,1)S(1)}, bf16[512,1280]{1,0:T(8,128)(2,1)S(1)}, u32[]{:S(2)}, u32[]{:S(2)}) %collective-permute-start.61) | collective-permute-done | bytes 1310752 | tf_op jit(solution)/shard_map/ppermute | solution.py:56
  627.2 5.5 convert_add_fusion
  632.8 7.3 multiply_reduce_fusion
  654.6 9.1 %collective-permute-start.66 = (bf16[512,1280]{1,0:T(8,128)(2,1)S(1)}, bf16[512,1280]{1,0:T(8,128)(2,1)}, u32[]{:S(2)}, u32[]{:S(2)}) collective-permute-start(bf16[512,1280]{1,0:T(8,128)(2,1)S(1)} %copy-done.41), channel_id=1, source_target_pairs={{0,8},{4,12},{8,16},{12,20},{16,24},{20,28},{1,9},{5,13},{9,17},{1... | collective-permute-start | bytes 3932168 | tf_op jit(solution)/shard_map/ppermute | solution.py:56
  678.1 15.3 %collective-permute-done.69 = bf16[160,3968]{1,0:T(8,128)(2,1)S(1)} collective-permute-done((bf16[160,3968]{1,0:T(8,128)(2,1)S(1)}, bf16[160,3968]{1,0:T(8,128)(2,1)S(1)}, u32[]{:S(2)}, u32[]{:S(2)}) %collective-permute-start.69) | collective-permute-done | bytes 1269792 | tf_op jit(solution)/shard_map/ppermute | solution.py:27
  708.4 6.5 collective-permute-done.73
  745.6 9.1 %collective-permute-start.82 = (bf16[40,1280]{1,0:T(8,128)(2,1)S(1)}, bf16[40,1280]{1,0:T(8,128)(2,1)S(1)}, u32[]{:S(2)}, u32[]{:S(2)}) collective-permute-start(bf16[40,1280]{1,0:T(8,128)(2,1)S(1)} %get-tuple-element.356), channel_id=1, source_target_pairs={{0,8},{4,12},{8,16},{12,20},{16,24},{20,28},{24,0},{28,4},{1,9},{5... | collective-permute-start | bytes 307208 | tf_op jit(solution)/shard_map/ppermute | solution.py:47
  754.8 6.0 collective-permute-done.76
  (519 shorter events, 301.6 us)
Async XLA Ops:
  8.0 227.3 %all-gather.6.cloned.1.call-start = ((), (), s32[]{:S(2)}) async-start(), calls=%async_computation.2 | async-start | bytes 17203200 | tf_op jit(solution)/shard_map/all_gather | solution.py:605
  93.8 322.8 %all-gather.4.cloned.1.call-start = ((), (), s32[]{:S(2)}) async-start(), calls=%async_computation.1 | async-start | bytes 7096320 | tf_op jit(solution)/shard_map/all_gather | solution.py:626
  101.5 47.8 %collective-permute-start.19 = (bf16[528,1280]{1,0:T(8,128)(2,1)}, bf16[528,1280]{1,0:T(8,128)(2,1)S(1)}, u32[]{:S(2)}, u32[]{:S(2)}) collective-permute-start(bf16[528,1280]{1,0:T(8,128)(2,1)} %fusion.44.c_own), channel_id=1, source_target_pairs={{0,8},{4,12},{8,16},{12,20},{16,24},{20,28},{1,9},{5,13},{9,17},{1... | collective-permute-start | bytes 4055048 | tf_op jit(solution)/shard_map/ppermute | solution.py:56
  104.7 44.7 %collective-permute-start.20 = (bf16[528,1280]{1,0:T(8,128)(2,1)}, bf16[528,1280]{1,0:T(8,128)(2,1)S(1)}, u32[]{:S(2)}, u32[]{:S(2)}) collective-permute-start(bf16[528,1280]{1,0:T(8,128)(2,1)} %fusion.44.c_own), channel_id=1, source_target_pairs={{8,0},{12,4},{16,8},{20,12},{24,16},{28,20},{9,1},{13,5},{17,9},{2... | collective-permute-start | bytes 4055048 | tf_op jit(solution)/shard_map/ppermute | solution.py:56
  153.0 38.3 %collective-permute-start.25 = (bf16[528,1280]{1,0:T(8,128)(2,1)S(1)}, bf16[528,1280]{1,0:T(8,128)(2,1)}, u32[]{:S(2)}, u32[]{:S(2)}) collective-permute-start(bf16[528,1280]{1,0:T(8,128)(2,1)S(1)} %collective-permute-done.20), channel_id=1, source_target_pairs={{8,0},{12,4},{16,8},{20,12},{9,1},{13,5},{17,9},{21,13},{10,2},{14... | collective-permute-start | bytes 4055048 | tf_op jit(solution)/shard_map/ppermute | solution.py:56
  163.3 55.7 %collective-permute-start.27 = (bf16[528,1280]{1,0:T(8,128)(2,1)}, bf16[528,1280]{1,0:T(8,128)(2,1)}, u32[]{:S(2)}, u32[]{:S(2)}) collective-permute-start(bf16[528,1280]{1,0:T(8,128)(2,1)} %fusion.44.c_own), channel_id=1, source_target_pairs={{0,4},{4,0},{8,12},{12,8},{16,20},{20,16},{24,28},{28,24},{1,5},{5... | collective-permute-start | bytes 4055048 | tf_op jit(solution)/shard_map/ppermute | solution.py:23
  163.9 36.8 %collective-permute-start.22 = (bf16[512,1280]{1,0:T(8,128)(2,1)}, bf16[512,1280]{1,0:T(8,128)(2,1)}, u32[]{:S(2)}, u32[]{:S(2)}) collective-permute-start(bf16[512,1280]{1,0:T(8,128)(2,1)} %multiply_convert_fusion.x_own), channel_id=1, source_target_pairs={{0,8},{4,12},{8,16},{12,20},{16,24},{20,28},{1,9},{5,13},{9,17},{1... | collective-permute-start | bytes 3932168 | tf_op jit(solution)/shard_map/ppermute | solution.py:56
  173.0 46.0 %collective-permute-start.23 = (bf16[512,1280]{1,0:T(8,128)(2,1)}, bf16[512,1280]{1,0:T(8,128)(2,1)}, u32[]{:S(2)}, u32[]{:S(2)}) collective-permute-start(bf16[512,1280]{1,0:T(8,128)(2,1)} %multiply_convert_fusion.x_own), channel_id=1, source_target_pairs={{8,0},{12,4},{16,8},{20,12},{24,16},{28,20},{9,1},{13,5},{17,9},{2... | collective-permute-start | bytes 3932168 | tf_op jit(solution)/shard_map/ppermute | solution.py:56
  174.3 44.7 %collective-permute-start.26 = (bf16[512,1280]{1,0:T(8,128)(2,1)}, bf16[512,1280]{1,0:T(8,128)(2,1)}, u32[]{:S(2)}, u32[]{:S(2)}) collective-permute-start(bf16[512,1280]{1,0:T(8,128)(2,1)} %multiply_convert_fusion.x_own), channel_id=1, source_target_pairs={{0,4},{4,0},{8,12},{12,8},{16,20},{20,16},{24,28},{28,24},{1,5},{5... | collective-permute-start | bytes 3932168 | tf_op jit(solution)/shard_map/ppermute | solution.py:23
  219.0 45.3 %collective-permute-start.28 = (bf16[512,1280]{1,0:T(8,128)(2,1)}, bf16[512,1280]{1,0:T(8,128)(2,1)}, u32[]{:S(2)}, u32[]{:S(2)}) collective-permute-start(bf16[512,1280]{1,0:T(8,128)(2,1)} %collective-permute-done.22), channel_id=1, source_target_pairs={{8,16},{12,20},{16,24},{20,28},{9,17},{13,21},{17,25},{21,29},{10,... | collective-permute-start | bytes 3932168 | tf_op jit(solution)/shard_map/ppermute | solution.py:56
  220.8 43.6 %collective-permute-start.29 = (bf16[512,1280]{1,0:T(8,128)(2,1)}, bf16[512,1280]{1,0:T(8,128)(2,1)}, u32[]{:S(2)}, u32[]{:S(2)}) collective-permute-start(bf16[512,1280]{1,0:T(8,128)(2,1)} %collective-permute-done.23), channel_id=1, source_target_pairs={{8,0},{12,4},{16,8},{20,12},{9,1},{13,5},{17,9},{21,13},{10,2},{14... | collective-permute-start | bytes 3932168 | tf_op jit(solution)/shard_map/ppermute | solution.py:56
  222.1 42.3 %collective-permute-start.30 = (bf16[528,1280]{1,0:T(8,128)(2,1)}, bf16[528,1280]{1,0:T(8,128)(2,1)}, u32[]{:S(2)}, u32[]{:S(2)}) collective-permute-start(bf16[528,1280]{1,0:T(8,128)(2,1)} %collective-permute-done.24), channel_id=1, source_target_pairs={{16,24},{20,28},{17,25},{21,29},{18,26},{22,30},{19,27},{23,31}} | collective-permute-start | bytes 4055048 | tf_op jit(solution)/shard_map/ppermute | solution.py:56
  223.8 58.8 %collective-permute-start.31 = (bf16[528,1280]{1,0:T(8,128)(2,1)}, bf16[528,1280]{1,0:T(8,128)(2,1)}, u32[]{:S(2)}, u32[]{:S(2)}) collective-permute-start(bf16[528,1280]{1,0:T(8,128)(2,1)} %collective-permute-done.25), channel_id=1, source_target_pairs={{8,0},{12,4},{9,1},{13,5},{10,2},{14,6},{11,3},{15,7}} | collective-permute-start | bytes 4055048 | tf_op jit(solution)/shard_map/ppermute | solution.py:56
  288.2 429.7 %reduce-scatter.4.cloned.1.call-start = ((), (), s32[]{:S(2)}) async-start(), calls=%async_computation.3 | async-start | bytes 17203200
  288.4 47.0 %collective-permute-start.32 = (bf16[512,1280]{1,0:T(8,128)(2,1)}, bf16[512,1280]{1,0:T(8,128)(2,1)S(1)}, u32[]{:S(2)}, u32[]{:S(2)}) collective-permute-start(bf16[512,1280]{1,0:T(8,128)(2,1)} %collective-permute-done.29), channel_id=1, source_target_pairs={{8,0},{12,4},{9,1},{13,5},{10,2},{14,6},{11,3},{15,7}} | collective-permute-start | bytes 3932168 | tf_op jit(solution)/shard_map/ppermute | solution.py:56
  402.8 38.0 %collective-permute-start.44 = (bf16[512,1280]{1,0:T(8,128)(2,1)}, bf16[512,1280]{1,0:T(8,128)(2,1)}, u32[]{:S(2)}, u32[]{:S(2)}) collective-permute-start(bf16[512,1280]{1,0:T(8,128)(2,1)} %get-tuple-element.266), channel_id=1, source_target_pairs={{0,4},{4,0},{8,12},{12,8},{16,20},{20,16},{24,28},{28,24},{1,5},{5... | collective-permute-start | bytes 3932168 | tf_op jit(solution)/shard_map/ppermute | solution.py:23
  407.8 33.1 %collective-permute-start.46 = (bf16[512,1280]{1,0:T(8,128)(2,1)S(1)}, bf16[512,1280]{1,0:T(8,128)(2,1)}, u32[]{:S(2)}, u32[]{:S(2)}) collective-permute-start(bf16[512,1280]{1,0:T(8,128)(2,1)S(1)} %fusion.34), channel_id=1, source_target_pairs={{24,16},{28,20},{25,17},{29,21},{26,18},{30,22},{27,19},{31,23}} | collective-permute-start | bytes 3932168 | tf_op jit(solution)/shard_map/ppermute | solution.py:56
  440.8 113.5 %collective-permute-start.58 = (bf16[512,1280]{1,0:T(8,128)(2,1)}, bf16[512,1280]{1,0:T(8,128)(2,1)}, u32[]{:S(2)}, u32[]{:S(2)}) collective-permute-start(bf16[512,1280]{1,0:T(8,128)(2,1)} %get-tuple-element.280), channel_id=1, source_target_pairs={{0,4},{4,0},{8,12},{12,8},{16,20},{20,16},{24,28},{28,24},{1,5},{5... | collective-permute-start | bytes 3932168 | tf_op jit(solution)/shard_map/ppermute | solution.py:23
  445.7 40.1 %collective-permute-start.49 = (bf16[512,1280]{1,0:T(8,128)(2,1)}, bf16[512,1280]{1,0:T(8,128)(2,1)}, u32[]{:S(2)}, u32[]{:S(2)}) collective-permute-start(bf16[512,1280]{1,0:T(8,128)(2,1)} %get-tuple-element.268), channel_id=1, source_target_pairs={{0,8},{4,12},{8,16},{12,20},{1,9},{5,13},{9,17},{13,21},{2,10},{6,... | collective-permute-start | bytes 3932168 | tf_op jit(solution)/shard_map/ppermute | solution.py:56
  450.1 38.6 %collective-permute-start.50 = (bf16[512,1280]{1,0:T(8,128)(2,1)}, bf16[512,1280]{1,0:T(8,128)(2,1)}, u32[]{:S(2)}, u32[]{:S(2)}) collective-permute-start(bf16[512,1280]{1,0:T(8,128)(2,1)} %get-tuple-element.269), channel_id=1, source_target_pairs={{16,8},{20,12},{24,16},{28,20},{17,9},{21,13},{25,17},{29,21},{18,... | collective-permute-start | bytes 3932168 | tf_op jit(solution)/shard_map/ppermute | solution.py:56
  451.8 38.9 %collective-permute-start.48 = (bf16[512,1280]{1,0:T(8,128)(2,1)}, bf16[512,1280]{1,0:T(8,128)(2,1)S(1)}, u32[]{:S(2)}, u32[]{:S(2)}) collective-permute-start(bf16[512,1280]{1,0:T(8,128)(2,1)} %get-tuple-element.273), channel_id=1, source_target_pairs={{0,4},{4,0},{8,12},{12,8},{16,20},{20,16},{24,28},{28,24},{1,5},{5... | collective-permute-start | bytes 3932168 | tf_op jit(solution)/shard_map/ppermute | solution.py:23
  451.8 39.0 %collective-permute-start.51 = (bf16[640,2688]{1,0:T(8,128)(2,1)}, bf16[640,2688]{1,0:T(8,128)(2,1)}, u32[]{:S(2)}, u32[]{:S(2)}) collective-permute-start(bf16[640,2688]{1,0:T(8,128)(2,1)} %pad_maximum_fusion.2), channel_id=1, source_target_pairs={{0,4},{4,0},{8,12},{12,8},{16,20},{20,16},{24,28},{28,24},{1,5},{5... | collective-permute-start | bytes 10321928 | tf_op jit(solution)/shard_map/ppermute | solution.py:23
  494.3 34.8 %collective-permute-start.54 = (bf16[160,2688]{1,0:T(8,128)(2,1)S(1)}, bf16[160,2688]{1,0:T(8,128)(2,1)S(1)}, u32[]{:S(2)}, u32[]{:S(2)}) collective-permute-start(bf16[160,2688]{1,0:T(8,128)(2,1)S(1)} %get-tuple-element.319), channel_id=1, source_target_pairs={{0,2},{1,3},{2,0},{3,1},{4,6},{5,7},{6,4},{7,5},{8,10},{9,11},{10,... | collective-permute-start | bytes 2580488 | tf_op jit(solution)/shard_map/ppermute | solution.py:27
  495.8 36.0 %collective-permute-start.55 = (bf16[160,2688]{1,0:T(8,128)(2,1)S(1)}, bf16[160,2688]{1,0:T(8,128)(2,1)S(1)}, u32[]{:S(2)}, u32[]{:S(2)}) collective-permute-start(bf16[160,2688]{1,0:T(8,128)(2,1)S(1)} %get-tuple-element.320), channel_id=1, source_target_pairs={{0,1},{1,0},{2,3},{3,2},{4,5},{5,4},{6,7},{7,6},{8,9},{9,8},{10,11... | collective-permute-start | bytes 2580488 | tf_op jit(solution)/shard_map/ppermute | solution.py:27
  498.7 39.2 %collective-permute-start.52 = (bf16[512,1280]{1,0:T(8,128)(2,1)S(1)}, bf16[512,1280]{1,0:T(8,128)(2,1)S(1)}, u32[]{:S(2)}, u32[]{:S(2)}) collective-permute-start(bf16[512,1280]{1,0:T(8,128)(2,1)S(1)} %add_convert_fusion.6), channel_id=1, source_target_pairs={{0,8},{4,12},{8,16},{12,20},{16,24},{20,28},{1,9},{5,13},{9,17},{1... | collective-permute-start | bytes 3932168 | tf_op jit(solution)/shard_map/ppermute | solution.py:56
  509.2 33.7 %collective-permute-start.53 = (bf16[512,1280]{1,0:T(8,128)(2,1)S(1)}, bf16[512,1280]{1,0:T(8,128)(2,1)S(1)}, u32[]{:S(2)}, u32[]{:S(2)}) collective-permute-start(bf16[512,1280]{1,0:T(8,128)(2,1)S(1)} %add_convert_fusion.5), channel_id=1, source_target_pairs={{8,0},{12,4},{16,8},{20,12},{24,16},{28,20},{9,1},{13,5},{17,9},{2... | collective-permute-start | bytes 3932168 | tf_op jit(solution)/shard_map/ppermute | solution.py:56
  542.9 38.3 %collective-permute-start.57 = (bf16[512,1280]{1,0:T(8,128)(2,1)}, bf16[512,1280]{1,0:T(8,128)(2,1)}, u32[]{:S(2)}, u32[]{:S(2)}) collective-permute-start(bf16[512,1280]{1,0:T(8,128)(2,1)} %fusion.35), channel_id=1, source_target_pairs={{24,16},{28,20},{25,17},{29,21},{26,18},{30,22},{27,19},{31,23}} | collective-permute-start | bytes 3932168 | tf_op jit(solution)/shard_map/ppermute | solution.py:56
  544.6 36.6 %collective-permute-start.56 = (bf16[512,1280]{1,0:T(8,128)(2,1)}, bf16[512,1280]{1,0:T(8,128)(2,1)}, u32[]{:S(2)}, u32[]{:S(2)}) collective-permute-start(bf16[512,1280]{1,0:T(8,128)(2,1)} %fusion.36), channel_id=1, source_target_pairs={{0,8},{4,12},{1,9},{5,13},{2,10},{6,14},{3,11},{7,15}} | collective-permute-start | bytes 3932168 | tf_op jit(solution)/shard_map/ppermute | solution.py:56
  587.5 39.7 %collective-permute-start.63 = (bf16[640,3840]{1,0:T(8,128)(2,1)S(1)}, bf16[640,3840]{1,0:T(8,128)(2,1)S(1)}, u32[]{:S(2)}, u32[]{:S(2)}) collective-permute-start(bf16[640,3840]{1,0:T(8,128)(2,1)S(1)} %convolution_convert_fusion.1), channel_id=1, source_target_pairs={{0,4},{4,0},{8,12},{12,8},{16,20},{20,16},{24,28},{28,24},{1,5},{5... | collective-permute-start | bytes 14745608 | tf_op jit(solution)/shard_map/ppermute | solution.py:23
  653.3 42.8 %collective-permute-start.67 = (bf16[512,1280]{1,0:T(8,128)(2,1)S(1)}, bf16[512,1280]{1,0:T(8,128)(2,1)S(1)}, u32[]{:S(2)}, u32[]{:S(2)}) collective-permute-start(bf16[512,1280]{1,0:T(8,128)(2,1)S(1)} %copy-done.42), channel_id=1, source_target_pairs={{8,0},{12,4},{16,8},{20,12},{24,16},{28,20},{9,1},{13,5},{17,9},{2... | collective-permute-start | bytes 3932168 | tf_op jit(solution)/shard_map/ppermute | solution.py:56
  654.6 41.5 %collective-permute-start.66 = (bf16[512,1280]{1,0:T(8,128)(2,1)S(1)}, bf16[512,1280]{1,0:T(8,128)(2,1)}, u32[]{:S(2)}, u32[]{:S(2)}) collective-permute-start(bf16[512,1280]{1,0:T(8,128)(2,1)S(1)} %copy-done.41), channel_id=1, source_target_pairs={{0,8},{4,12},{8,16},{12,20},{16,24},{20,28},{1,9},{5,13},{9,17},{1... | collective-permute-start | bytes 3932168 | tf_op jit(solution)/shard_map/ppermute | solution.py:56
  726.8 33.9 %collective-permute-start.76 = (bf16[40,3968]{1,0:T(8,128)(2,1)S(1)}, bf16[40,3968]{1,0:T(8,128)(2,1)S(1)}, u32[]{:S(2)}, u32[]{:S(2)}) collective-permute-start(bf16[40,3968]{1,0:T(8,128)(2,1)S(1)} %slice.571), channel_id=1, source_target_pairs={{0,16},{4,20},{8,24},{12,28},{16,0},{20,4},{24,8},{28,12},{1,17},{... | collective-permute-start | bytes 952328 | tf_op jit(solution)/shard_map/ppermute | solution.py:47
  (156 other events, 2055.7 us)
Sparse Core Ops, SparseCore 0:
  93.9 141.3 all-gather.5
  485.9 166.5 reduce-scatter.3
Sparse Core Ops, SparseCore 1:
  288.2 70.0 all-gather.3

commit v3 on v2

--- a/solution.py
+++ b/solution.py
@@ -68,11 +68,12 @@
         self.left.append(line_send(b, -1, 1, self.n - s))
         return self.right[-1], self.left[-1]
 
-    def slot(self, r):
+    def slot(self, r, *others):
         if r == 0:
-            return self.right[0]
+            return after(self.right[0], *others)
         p = lax.axis_index("dp") // 2
-        return jnp.where(p + r < self.n, self.left[r], self.right[self.n - r])
+        near, far = after((self.left[r], self.right[self.n - r]), *others)
+        return jnp.where(p + r < self.n, near, far)
 
 
 class LineScatter:
@@ -84,10 +85,10 @@
     def step(self, to_right, to_left, *others):
         self.s += 1
         s = self.s
-        a, b = to_right.astype(F32), to_left.astype(F32)
+        a, b = after((to_right, to_left), *others)
         if self.right is not None:
-            a, b = a + self.right.astype(F32), b + self.left.astype(F32)
-        a, b = after((a.astype(BF16), b.astype(BF16)), *others)
+            a, b = a.astype(F32) + self.right.astype(F32), b.astype(F32) + self.left.astype(F32)
+        a, b = lax.optimization_barrier((a.astype(BF16), b.astype(BF16)))
         self.sent = a, b
         self.right = line_send(a, 1, 0, s - 1)
         self.left = line_send(b, -1, self.n - s, self.n - 1)
@@ -511,6 +512,40 @@
     )(*arrays)
 
 
+def shared_kernel(x, c, c_rel, weights, order, out, back, own, other):
+    width, columns = weights.shape
+    units = columns // 3
+    half = width // 2
+    gate_value = dot(x[...], weights[:, :units], NN)
+    up = dot(x[...], weights[:, units : 2 * units], NN)
+    active, slope = silu_parts(gate_value)
+    hidden = (active * up).astype(BF16)
+    cot = dot(c[...], weights[:, 2 * units :], NN)
+    gate_cot = (cot * up * slope).astype(BF16)
+    up_cot = (cot * active).astype(BF16)
+    out[...] = dot(hidden, weights[:, 2 * units :], NT)
+    back[...] = dot(gate_cot, weights[:, :units], NT) + dot(
+        up_cot, weights[:, units : 2 * units], NT
+    )
+    rel = dot(x[...], order[...], NN).astype(BF16)
+    for cut, grad in ((slice(0, half), own), (slice(half, width), other)):
+        grad[:, :units] = dot(rel[:, cut], gate_cot, TN).astype(BF16)
+        grad[:, units : 2 * units] = dot(rel[:, cut], up_cot, TN).astype(BF16)
+        grad[:, 2 * units :] = dot(c_rel[:, cut], hidden, TN).astype(BF16)
+
+
+def shared_expert(x, c, c_rel, weights, order):
+    width, columns = weights.shape
+    shape = jax.ShapeDtypeStruct
+    return pl.pallas_call(
+        shared_kernel,
+        out_shape=[shape(x.shape, F32)] * 2 + [shape((width // 2, columns), BF16)] * 2,
+        compiler_params=pltpu.CompilerParams(vmem_limit_bytes=VMEM_LIMIT),
+        cost_estimate=cost(30e9),
+        name="shared_expert",
+    )(x, c, c_rel, weights, order)
+
+
 def split_matmul(values, matrix, dims):
     high = values.astype(BF16)
     low = (values - high.astype(F32)).astype(BF16)
@@ -593,8 +628,8 @@
     gather_out.exchange(*done)
     cots = LineGather(sent)
     going = cots.step(*done)
-    project = gather_in.columns(0, 3 * width)
-    small_full = gather_in.columns(3 * width, 3 * width + LANES)
+    packed_full = jnp.concatenate(gather_in.pieces(), axis=0)
+    project, small_full = packed_full[:, : 3 * width], packed_full[:, 3 * width :]
 
     small_true = dot(order, small_full, NN)
     gain_one = small_full[:, 0].astype(F32)
@@ -623,9 +658,6 @@
     root_two = lax.rsqrt(jnp.mean(hidden_res * hidden_res, axis=-1, keepdims=True) + EPSILON)
     unit_two = hidden_res * root_two
     normed_two = (unit_two * gain_two).astype(BF16)
-    shared_full = lax.all_gather(
-        after(shared_weights.reshape(rows, 3 * units), normed_two), ("dp", "fsdp"), axis=0, tiled=True
-    )
     done = [normed_two]
 
     rows_two = LineGather(normed_two)
@@ -633,7 +665,7 @@
     chunks, x_pairs, c_pairs = [None] * n, [None] * n, [None] * n
 
     def pair_up(r, *others):
-        x, c = after((rows_two.slot(r), cots.slot(r)), *others)
+        x, c = rows_two.slot(r, *others), cots.slot(r, *others)
         x_pairs[r], c_pairs[r] = (x, core_swap(x)), (c, core_swap(c))
         return x_pairs[r], c_pairs[r]
 
@@ -643,27 +675,13 @@
         return chunks[r]
 
     def shared_part(*others):
-        rows_, c_ = after((normed_two, out_cotangent), *others)
-        gate_up = dot(rows_, shared_full[:, : 2 * units], NN)
-        active, slope = silu_parts(gate_up[:, :units])
-        up = gate_up[:, units:]
-        hidden = (active * up).astype(BF16)
-        cot = dot(c_, shared_full[:, 2 * units :], NN)
-        gate_up_cot = jnp.concatenate(
-            [(cot * up * slope).astype(BF16), (cot * active).astype(BF16)], axis=1
-        )
-        rel = dot(rows_, order, NN).astype(BF16)
-        grad = [
-            jnp.concatenate(
-                [dot(rel[:, cut], gate_up_cot, TN).astype(BF16),
-                 dot(c_rel[:, cut], hidden, TN).astype(BF16)], axis=1,
-            )
-            for cut in halves
-        ]
-        out = dot(hidden, shared_full[:, 2 * units :], NT)
-        return out, dot(gate_up_cot, shared_full[:, : 2 * units], NT), grad
+        rows_ = after(normed_two, *others)
+        out, back, *grad = shared_expert(rows_, out_cotangent, c_rel, shared_full, order)
+        return out, back, grad
 
     for at in range(n - 1):
+        if at == n - 2:
+            done = [pair_up(n // 2, *done)]
         going = [rows_two.step(*done), cots.right[-1], cots.left[-1]]
         if at > 0 and len(cots.right) < n:
             going.append(cots.step(*done))
@@ -673,7 +691,6 @@
         elif at == n - 3:
             beside.append(chunk(0, *done)[9])
         elif at == n - 2:
-            pair_up(n // 2, *done)
             beside.append(chunk(n // 2, *done)[9])
         done = [going, beside]
 
@@ -690,6 +707,9 @@
         out_slots[r] = add_pair((chunks[r][7], got))
         return got
 
+    shared_full = lax.all_gather(
+        after(shared_weights.reshape(rows, 3 * units), *done), ("dp", "fsdp"), axis=0, tiled=True
+    )
     done = [pair_up(early[0], *done)]
     for at, r in enumerate(early):
         moved = [pair_up(q, *done) for q in (early + late)[at + 1 :][:1]]
@@ -703,24 +723,28 @@
         going = back.step(back_slots[n - s], back_slots[s], *done)
         held = back.sent
         made = []
-        wanted = [r for r in late if r in (s + 1, n - s - 1)]
+        wanted = [r for r in late if r in (s + 1, n - s - 1)] or ([0] if late == [0] else [])
         for r in [r for r in range(n) if chunks[r] is not None and out_slots[r] is None][:2]:
             made.append(out_part(r, *held))
         for r in wanted:
             late.remove(r)
-            pair_up(r, *held)
+            if x_pairs[r] is None:
+                pair_up(r, *held)
             made.append(chunk(r, *held)[9])
         if not late and not wanted:
             if "shared" not in results:
                 results["shared"] = shared_part(*held)
-                scatter = DenseScatter(*results["shared"][2])
                 made.append(results["shared"])
             elif "experts" not in results:
                 weights = expert_weight_grads(after(chunks, *held), lax.axis_size("fsdp"))
-                results["experts"] = lax.psum_scatter(weights, "fsdp", scatter_dimension=0)
+                scatter = DenseScatter(*results["shared"][2])
+                results["experts"] = weights
                 made += [weights, scatter.swap(*held)]
             elif "exchange" not in results:
-                results["exchange"] = scatter.exchange(0, *held)
+                results["experts"] = lax.psum_scatter(
+                    after(results["experts"], *done), "fsdp", scatter_dimension=0
+                )
+                results["exchange"] = scatter.exchange(0, *done)
                 made.append(results["exchange"])
         done = [going, made]
         for r in wanted:
@@ -728,13 +752,12 @@
     for r in range(n):
         if out_slots[r] is None:
             out_part(r, *done)
+    expert_sum = results["experts"]
     shared_out, shared_back, _ = results["shared"]
-    expert_sum = results["experts"]
     back_sum = back.total(back_slots[0])
     router_part = sum(a[9] for a in chunks)
 
     going_out = out_sums.step(out_slots[n - 1], out_slots[1], *done) if n > 1 else []
-    moved = [scatter.exchange(i, *done) for i in range(1, k)]
     cotangent = out_cotangent.astype(F32)
     normed_two_cot = back_sum + shared_back
     scaled = normed_two_cot * gain_two
@@ -743,6 +766,7 @@
         scaled - unit_two * jnp.mean(scaled * unit_two, axis=-1, keepdims=True)
     )
     attn_cot = hidden_cot.astype(BF16)
+    moved = [scatter.exchange(i, *done) for i in range(1, k)]
     mixed_cot = dot(dot(attn_cot, out_full, NT).astype(BF16), order, NT).astype(BF16)
     cot_parts = attention_backward(query, key, value, mixed_cot, lse, cosine, sine)
     done = [cot_parts, going_out, moved]

time: 781 us -> 746 us (0.955)
  matrix products: 89.8 us -> 63.2 us
  Pallas kernels: 178 us -> 199 us
  waiting for transfers between devices: 235 us -> 214 us
  starting transfers between devices: 139 us -> 129 us
  other arithmetic: 67.1 us -> 76.9 us
    ppermute x30, waiting for transfers between devices: 121 us -> 70 us  [line_send(): return lax.ppermute(x, 'dp', pairs)]
    dot_general x24 -> x15, matrix products: 87.7 us -> 61 us  [dot(): return lax.dot_general(a, b, (dims, ((), ())), preferred_element_type=F32)]
    pallas_call x0 -> x1, Pallas kernels: none -> 21 us  [shared_expert(): pl.pallas_call(shared_kernel, out_shape=[shape(x.shape, F32)] * 2 + [shap...]
    ppermute x20, waiting for transfers between devices: 67.9 us -> 85.5 us  [fsdp_swap(): lax.ppermute(x, 'fsdp', [(f, f ^ bit) for f in range(lax.axis_size('fsdp'...]
    all_gather x1, waiting for transfers between devices: 10 us -> 18.9 us  [shards(): routed = lax.all_gather(after(turned, *done), 'fsdp', axis=0)]
    add x8 -> x14, other arithmetic: 6.88 us -> 15.6 us  [add_pair(): return pair[0].astype(F32) + pair[1].astype(F32)]
    unnamed x231 -> x216, local copies, waits for them, and re-layouts: 30.9 us -> 25.6 us
    convert_element_type x10 -> x12, other arithmetic: 20 us -> 22.6 us  [step(): a, b = lax.optimization_barrier((a.astype(BF16), b.astype(BF16)))]
  transfers between devices with their start and end apart: 88 -> 88, of which waited for: 32 -> 32; matrix products, arithmetic and copies ran while one was open for 24% -> 20% of each run, Pallas kernels for 23% -> 27%
where the time goes in v3:
time: 746 us; the launch traced here: 736 us
  waiting for transfers between devices  214 us (29%)
  Pallas kernels  199 us (27%)
  starting transfers between devices  129 us (17%)
  other arithmetic  76.9 us (10%)
  matrix products  63.2 us (8%)
  local copies, waits for them, and re-layouts  38.4 us (5%)
  between operations  16.1 us (2%)
    pallas_call x4, Pallas kernels, expert_chunk(): pl.pallas_call(expert_kernel, grid_spec=pltpu.PrefetchScalarGridSpec(num_...  117 us
    ppermute x20, waiting for transfers between devices, fsdp_swap(): lax.ppermute(x, 'fsdp', [(f, f ^ bit) for f in range(lax.axis_size('fsdp'...  85.5 us
    ppermute x30, starting transfers between devices, line_send(): return lax.ppermute(x, 'dp', pairs)  74.2 us
    ppermute x30, waiting for transfers between devices, line_send(): return lax.ppermute(x, 'dp', pairs)  70 us
    dot_general x15, matrix products, dot(): return lax.dot_general(a, b, (dims, ((), ())), preferred_element_type=F32)  61 us
    pallas_call x1, Pallas kernels, expert_weight_grads(): pl.pallas_call(expert_weights_kernel, grid=(local, 3), in_specs=[pl.Block...  33.5 us
    unnamed x216, local copies, waits for them, and re-layouts  25.6 us
    ppermute x20, starting transfers between devices, fsdp_swap(): lax.ppermute(x, 'fsdp', [(f, f ^ bit) for f in range(lax.axis_size('fsdp'...  25 us
  transfers between devices with their start and end apart: 88, of which 32 were waited for; matrix products, arithmetic and copies ran while one was open for 20% of the time, Pallas kernels for 27%

profile of v3, /device:TPU:0, one launch (start us, length us, event | category | flops | bytes accessed | tf_op | source)
XLA Modules:
  0.0 736.4 jit_solution(7104684587073072616)
XLA Ops:
  29.3 12.8 %collective-permute-done.1 = bf16[40,3968]{1,0:T(8,128)(2,1)S(1)} collective-permute-done((bf16[40,3968]{1,0:T(8,128)(2,1)S(1)}, bf16[40,3968]{1,0:T(8,128)(2,1)S(1)}, u32[]{:S(2)}, u32[]{:S(2)}) %collective-permute-start.1) | collective-permute-done | bytes 317472 | tf_op jit(solution)/shard_map/ppermute | solution.py:39
  49.7 7.8 %collective-permute-done.4 = bf16[80,3968]{1,0:T(8,128)(2,1)S(1)} collective-permute-done((bf16[80,3968]{1,0:T(8,128)(2,1)S(1)}, bf16[80,3968]{1,0:T(8,128)(2,1)S(1)}, u32[]{:S(2)}, u32[]{:S(2)}) %collective-permute-start.4) | collective-permute-done | bytes 634912 | tf_op jit(solution)/shard_map/ppermute | solution.py:27
  63.1 8.1 %collective-permute-done.11 = bf16[40,1280]{1,0:T(8,128)(2,1)S(1)} collective-permute-done((bf16[40,1280]{1,0:T(8,128)(2,1)S(1)}, bf16[40,1280]{1,0:T(8,128)(2,1)S(1)}, u32[]{:S(2)}, u32[]{:S(2)}) %collective-permute-start.11) | collective-permute-done | bytes 102432 | tf_op jit(solution)/shard_map/ppermute | solution.py:56
  73.2 5.2 collective-permute-done.13
  78.5 10.9 %collective-permute-done.7 = bf16[160,3968]{1,0:T(8,128)(2,1)S(1)} collective-permute-done((bf16[160,3968]{1,0:T(8,128)(2,1)S(1)}, bf16[160,3968]{1,0:T(8,128)(2,1)S(1)}, u32[]{:S(2)}, u32[]{:S(2)}) %collective-permute-start.7) | collective-permute-done | bytes 1269792 | tf_op jit(solution)/shard_map/ppermute | solution.py:27
  113.4 7.5 %fusion.3.qp.kp.vp = f32[512,3840]{1,0:T(8,128)} fusion(bf16[512,1280]{0,1:T(8,128)(2,1)S(1)} %multiply_convert_fusion.1, bf16[1280,3968]{1,0:T(8,128)(2,1)S(1)} %slice_dynamic-update-slice_fusion), kind=kOutput, calls=%fused_computation.9 | convolution fusion | flops 5033164800 | bytes 19005440 | tf_op jit(solution)/shard_map/dot_general | solution.py:234
  123.5 13.0 %attention_forward.1 = (bf16[512,1280]{1,0:T(8,128)(2,1)}, bf16[512,1280]{1,0:T(8,128)(2,1)}, bf16[512,1280]{1,0:T(8,128)(2,1)}, bf16[512,1280]{1,0:T(8,128)(2,1)}, f32[10,1,512]{2,1,0:T(1,128)}) custom-call(f32[512,3840]{1,0:T(8,128)} %fusion.3.qp.kp.vp, f32[512,3840]{1,0:T(8,128)} %fusion.3.qp.kp.vp, f32[512,3840]{1,0:T(8,128)} %fusion.3.qp.kp.vp, ...), custom_call_target="tpu_custom_call" | custom-call | flops 14000000000 | bytes 35000000 | tf_op jit(solution)/shard_map/attention_forward/pallas_call | solution.py:283
  155.1 11.6 %collective-permute-start.22 = (bf16[512,1280]{1,0:T(8,128)(2,1)}, bf16[512,1280]{1,0:T(8,128)(2,1)}, u32[]{:S(2)}, u32[]{:S(2)}) collective-permute-start(bf16[512,1280]{1,0:T(8,128)(2,1)} %multiply_convert_fusion.x_own.x), channel_id=1, source_target_pairs={{0,8},{4,12},{8,16},{12,20},{16,24},{20,28},{1,9},{5,13},{9,17},{1... | collective-permute-start | bytes 3932168 | tf_op jit(solution)/shard_map/ppermute | solution.py:56
  169.9 15.8 %collective-permute-done.25 = bf16[528,1280]{1,0:T(8,128)(2,1)} collective-permute-done((bf16[528,1280]{1,0:T(8,128)(2,1)}, bf16[528,1280]{1,0:T(8,128)(2,1)}, u32[]{:S(2)}, u32[]{:S(2)}) %collective-permute-start.25) | collective-permute-done | bytes 1351712 | tf_op jit(solution)/shard_map/ppermute | solution.py:56
  185.7 9.0 %collective-permute-done.22 = bf16[512,1280]{1,0:T(8,128)(2,1)} collective-permute-done((bf16[512,1280]{1,0:T(8,128)(2,1)}, bf16[512,1280]{1,0:T(8,128)(2,1)}, u32[]{:S(2)}, u32[]{:S(2)}) %collective-permute-start.22) | collective-permute-done | bytes 1310752 | tf_op jit(solution)/shard_map/ppermute | solution.py:56
  194.7 18.4 %collective-permute-done.23 = bf16[512,1280]{1,0:T(8,128)(2,1)} collective-permute-done((bf16[512,1280]{1,0:T(8,128)(2,1)}, bf16[512,1280]{1,0:T(8,128)(2,1)}, u32[]{:S(2)}, u32[]{:S(2)}) %collective-permute-start.23) | collective-permute-done | bytes 1310752 | tf_op jit(solution)/shard_map/ppermute | solution.py:56
  218.4 18.9 %all-gather.6.cloned.1.call-done = bf16[8,3,224,1280]{3,2,1,0:T(8,128)(2,1)} async-done(((bf16[2,3,224,1280]{3,2,1,0:T(8,128)(2,1)}), bf16[8,3,224,1280]{3,2,1,0:T(8,128)(2,1)}) %all-gather.6.cloned.1.call-update) | async-done | bytes 13762576 | tf_op jit(solution)/shard_map/all_gather | solution.py:640
  237.2 29.2 %expert_chunk.4 = (bf16[2,384,1280]{2,1,0:T(8,128)(2,1)}, bf16[2,384,1280]{2,1,0:T(8,128)(2,1)}, bf16[2,384,896]{2,1,0:T(8,128)(2,1)}, bf16[2,384,896]{2,1,0:T(8...) custom-call(s32[1]{0:T(128)} %bitcast.37.first, ...), custom_call_target="tpu_custom_call" | custom-call | flops 30000001024 | bytes 75000000 | tf_op jit(solution)/shard_map/expert_chunk/pallas_call | solution.py:447
  266.5 8.7 %collective-permute-done.29 = bf16[512,1280]{1,0:T(8,128)(2,1)} collective-permute-done((bf16[512,1280]{1,0:T(8,128)(2,1)}, bf16[512,1280]{1,0:T(8,128)(2,1)}, u32[]{:S(2)}, u32[]{:S(2)}) %collective-permute-start.29) | collective-permute-done | bytes 1310752 | tf_op jit(solution)/shard_map/ppermute | solution.py:56
  287.1 29.2 %expert_chunk.5 = (bf16[2,384,1280]{2,1,0:T(8,128)(2,1)}, bf16[2,384,1280]{2,1,0:T(8,128)(2,1)}, bf16[2,384,896]{2,1,0:T(8,128)(2,1)}, bf16[2,384,896]{2,1,0:T(8...) custom-call(s32[1]{0:T(128)} %bitcast.37.first, ...), custom_call_target="tpu_custom_call" | custom-call | flops 30000001024 | bytes 75000000 | tf_op jit(solution)/shard_map/expert_chunk/pallas_call | solution.py:447
  327.4 29.5 %expert_chunk.6 = (bf16[2,384,1280]{2,1,0:T(8,128)(2,1)}, bf16[2,384,1280]{2,1,0:T(8,128)(2,1)}, bf16[2,384,896]{2,1,0:T(8,128)(2,1)}, bf16[2,384,896]{2,1,0:T(8...) custom-call(s32[1]{0:T(128)} %bitcast.37.first, ...), custom_call_target="tpu_custom_call" | custom-call | flops 30000001024 | bytes 75000000 | tf_op jit(solution)/shard_map/expert_chunk/pallas_call | solution.py:447
  358.5 29.4 %expert_chunk.7 = (bf16[2,384,1280]{2,1,0:T(8,128)(2,1)}, bf16[2,384,1280]{2,1,0:T(8,128)(2,1)}, bf16[2,384,896]{2,1,0:T(8,128)(2,1)}, bf16[2,384,896]{2,1,0:T(8...) custom-call(s32[1]{0:T(128)} %bitcast.37.first, ...), custom_call_target="tpu_custom_call" | custom-call | flops 30000001024 | bytes 75000000 | tf_op jit(solution)/shard_map/expert_chunk/pallas_call | solution.py:447
  397.0 5.9 collective-permute-start.45
  406.8 21.0 %shared_expert.1 = (f32[512,1280]{1,0:T(8,128)}, f32[512,1280]{1,0:T(8,128)}, bf16[640,2688]{1,0:T(8,128)(2,1)}, bf16[640,2688]{1,0:T(8,128)(2,1)}) custom-call(bf16[512,1280]{1,0:T(8,128)(2,1)} %multiply_convert_fusion.x_own.x, bf16[512,1280]{1,0:T(8,128)(2,1)} %c.1, bf16[512,1280]{1,0:T(8,128)(2,1)} %fusion.26.c_rel, ...), custom_call_target="tpu_custom_call" | custom-call | flops 30000001024 | bytes 75000000 | tf_op jit(solution)/shard_map/shared_expert/pallas_call | solution.py:540
  435.8 5.5 collective-permute-start.49
  444.0 33.5 %expert_weights.1 = bf16[4,2,3,224,1280]{4,3,2,1,0:T(8,128)(2,1)} custom-call(bf16[2,384,1280]{2,1,0:T(8,128)(2,1)} %get-tuple-element.346.refs_0_, bf16[2,384,1280]{2,1,0:T(8,128)(2,1)} %get-tuple-element.347.refs_1_, bf16[2,384,1280]{2,1,0:T(8,128)(2,1)} %get-tuple-element.348.refs_2_, bf16[2,384,1280]{2,1,0:T(8,128)(2,1)} %get-tuple-element.349.refs_3_, ...), custom_call_target="tpu_custom_call" | custom-call | flops 42278584320 | bytes 105696464 | tf_op jit(solution)/shard_map/expert_weights/pallas_call | solution.py:503
  493.9 27.4 %collective-permute-done.55 = bf16[160,2688]{1,0:T(8,128)(2,1)S(1)} collective-permute-done((bf16[160,2688]{1,0:T(8,128)(2,1)S(1)}, bf16[160,2688]{1,0:T(8,128)(2,1)S(1)}, u32[]{:S(2)}, u32[]{:S(2)}) %collective-permute-start.55) | collective-permute-done | bytes 860192 | tf_op jit(solution)/shard_map/ppermute | solution.py:27
  539.4 7.6 %fusion.24.d_in = bf16[512,1280]{1,0:T(8,128)(2,1)} fusion(s32[1280]{0:T(1024)S(1)} %copy-done.76, bf16[1280,1280]{1,0:T(8,128)(2,1)} %copy-done.72, f32[512,1280]{1,0:T(8,128)} %multiply_add_fusion), kind=kOutput, calls=%fused_computation.40 | convolution fusion | flops 3359047680 | bytes 7214080 | tf_op jit(solution)/shard_map/dot_general | solution.py:234
  547.0 14.3 %attention_backward.1 = (bf16[512,1280]{1,0:T(8,128)(2,1)}, bf16[512,1280]{1,0:T(8,128)(2,1)}, bf16[512,1280]{1,0:T(8,128)(2,1)}) custom-call(bf16[512,1280]{1,0:T(8,128)(2,1)} %get-tuple-element.318.q_in, bf16[512,1280]{1,0:T(8,128)(2,1)} %get-tuple-element.319.k_in, bf16[512,1280]{1,0:T(8,128)(2,1)} %get-tuple-element.320.v_in, ...), custom_call_target="tpu_custom_call" | custom-call | flops 15000000512 | bytes 37500000 | tf_op jit(solution)/shard_map/attention_backward/pallas_call | solution.py:321
  586.5 5.2 convert_add_fusion
  591.8 7.1 multiply_reduce_fusion
  618.5 8.5 %collective-permute-start.66 = (bf16[512,1280]{1,0:T(8,128)(2,1)S(1)}, bf16[512,1280]{1,0:T(8,128)(2,1)S(1)}, u32[]{:S(2)}, u32[]{:S(2)}) collective-permute-start(bf16[512,1280]{1,0:T(8,128)(2,1)S(1)} %add_convert_fusion.2), channel_id=1, source_target_pairs={{0,8},{4,12},{8,16},{12,20},{16,24},{20,28},{1,9},{5,13},{9,17},{1... | collective-permute-start | bytes 3932168 | tf_op jit(solution)/shard_map/ppermute | solution.py:56
  635.3 6.6 fusion.14
  642.8 16.1 %collective-permute-done.68 = bf16[160,3968]{1,0:T(8,128)(2,1)S(1)} collective-permute-done((bf16[160,3968]{1,0:T(8,128)(2,1)S(1)}, bf16[160,3968]{1,0:T(8,128)(2,1)S(1)}, u32[]{:S(2)}, u32[]{:S(2)}) %collective-permute-start.68) | collective-permute-done | bytes 1269792 | tf_op jit(solution)/shard_map/ppermute | solution.py:27
  674.0 7.5 %collective-permute-done.73 = bf16[40,2688]{1,0:T(8,128)(2,1)S(1)} collective-permute-done((bf16[40,2688]{1,0:T(8,128)(2,1)S(1)}, bf16[40,2688]{1,0:T(8,128)(2,1)S(1)}, u32[]{:S(2)}, u32[]{:S(2)}) %collective-permute-start.73) | collective-permute-done | bytes 215072 | tf_op jit(solution)/shard_map/ppermute | solution.py:47
  707.4 5.2 collective-permute-start.82
  718.9 8.9 %collective-permute-done.83 = bf16[40,1280]{1,0:T(8,128)(2,1)S(1)} collective-permute-done((bf16[40,1280]{1,0:T(8,128)(2,1)S(1)}, bf16[40,1280]{1,0:T(8,128)(2,1)S(1)}, u32[]{:S(2)}, u32[]{:S(2)}) %collective-permute-start.83) | collective-permute-done | bytes 102432 | tf_op jit(solution)/shard_map/ppermute | solution.py:47
  (503 shorter events, 274.9 us)
Async XLA Ops:
  7.2 230.1 %all-gather.6.cloned.1.call-start = ((), (), s32[]{:S(2)}) async-start(), calls=%async_computation.2 | async-start | bytes 17203200 | tf_op jit(solution)/shard_map/all_gather | solution.py:640
  92.4 314.4 %all-gather.4.cloned.1.call-start = ((), (), s32[]{:S(2)}) async-start(), calls=%async_computation.1 | async-start | bytes 7096320 | tf_op jit(solution)/shard_map/all_gather | solution.py:710
  95.7 45.2 %collective-permute-start.19 = (bf16[528,1280]{1,0:T(8,128)(2,1)S(1)}, bf16[528,1280]{1,0:T(8,128)(2,1)S(1)}, u32[]{:S(2)}, u32[]{:S(2)}) collective-permute-start(bf16[528,1280]{1,0:T(8,128)(2,1)S(1)} %copy-done.29), channel_id=1, source_target_pairs={{0,8},{4,12},{8,16},{12,20},{16,24},{20,28},{1,9},{5,13},{9,17},{1... | collective-permute-start | bytes 4055048 | tf_op jit(solution)/shard_map/ppermute | solution.py:56
  98.8 42.1 %collective-permute-start.20 = (bf16[528,1280]{1,0:T(8,128)(2,1)S(1)}, bf16[528,1280]{1,0:T(8,128)(2,1)}, u32[]{:S(2)}, u32[]{:S(2)}) collective-permute-start(bf16[528,1280]{1,0:T(8,128)(2,1)S(1)} %copy-done.29), channel_id=1, source_target_pairs={{8,0},{12,4},{16,8},{20,12},{24,16},{28,20},{9,1},{13,5},{17,9},{2... | collective-permute-start | bytes 4055048 | tf_op jit(solution)/shard_map/ppermute | solution.py:56
  144.8 41.0 %collective-permute-start.25 = (bf16[528,1280]{1,0:T(8,128)(2,1)}, bf16[528,1280]{1,0:T(8,128)(2,1)}, u32[]{:S(2)}, u32[]{:S(2)}) collective-permute-start(bf16[528,1280]{1,0:T(8,128)(2,1)} %collective-permute-done.20), channel_id=1, source_target_pairs={{8,0},{12,4},{16,8},{20,12},{9,1},{13,5},{17,9},{21,13},{10,2},{14... | collective-permute-start | bytes 4055048 | tf_op jit(solution)/shard_map/ppermute | solution.py:56
  154.9 58.3 %collective-permute-start.27 = (bf16[528,1280]{1,0:T(8,128)(2,1)S(1)}, bf16[528,1280]{1,0:T(8,128)(2,1)}, u32[]{:S(2)}, u32[]{:S(2)}) collective-permute-start(bf16[528,1280]{1,0:T(8,128)(2,1)S(1)} %copy-done.29), channel_id=1, source_target_pairs={{0,4},{4,0},{8,12},{12,8},{16,20},{20,16},{24,28},{28,24},{1,5},{5... | collective-permute-start | bytes 4055048 | tf_op jit(solution)/shard_map/ppermute | solution.py:23
  155.1 39.6 %collective-permute-start.22 = (bf16[512,1280]{1,0:T(8,128)(2,1)}, bf16[512,1280]{1,0:T(8,128)(2,1)}, u32[]{:S(2)}, u32[]{:S(2)}) collective-permute-start(bf16[512,1280]{1,0:T(8,128)(2,1)} %multiply_convert_fusion.x_own.x), channel_id=1, source_target_pairs={{0,8},{4,12},{8,16},{12,20},{16,24},{20,28},{1,9},{5,13},{9,17},{1... | collective-permute-start | bytes 3932168 | tf_op jit(solution)/shard_map/ppermute | solution.py:56
  166.7 46.4 %collective-permute-start.23 = (bf16[512,1280]{1,0:T(8,128)(2,1)}, bf16[512,1280]{1,0:T(8,128)(2,1)}, u32[]{:S(2)}, u32[]{:S(2)}) collective-permute-start(bf16[512,1280]{1,0:T(8,128)(2,1)} %multiply_convert_fusion.x_own.x), channel_id=1, source_target_pairs={{8,0},{12,4},{16,8},{20,12},{24,16},{28,20},{9,1},{13,5},{17,9},{2... | collective-permute-start | bytes 3932168 | tf_op jit(solution)/shard_map/ppermute | solution.py:56
  169.1 44.0 %collective-permute-start.26 = (bf16[512,1280]{1,0:T(8,128)(2,1)}, bf16[512,1280]{1,0:T(8,128)(2,1)}, u32[]{:S(2)}, u32[]{:S(2)}) collective-permute-start(bf16[512,1280]{1,0:T(8,128)(2,1)} %multiply_convert_fusion.x_own.x), channel_id=1, source_target_pairs={{0,4},{4,0},{8,12},{12,8},{16,20},{20,16},{24,28},{28,24},{1,5},{5... | collective-permute-start | bytes 3932168 | tf_op jit(solution)/shard_map/ppermute | solution.py:23
  213.1 62.0 %collective-permute-start.30 = (bf16[528,1280]{1,0:T(8,128)(2,1)}, bf16[528,1280]{1,0:T(8,128)(2,1)S(1)}, u32[]{:S(2)}, u32[]{:S(2)}) collective-permute-start(bf16[528,1280]{1,0:T(8,128)(2,1)} %copy-done.32), channel_id=1, source_target_pairs={{16,24},{20,28},{17,25},{21,29},{18,26},{22,30},{19,27},{23,31}} | collective-permute-start | bytes 4055048 | tf_op jit(solution)/shard_map/ppermute | solution.py:56
  213.9 61.3 %collective-permute-start.31 = (bf16[528,1280]{1,0:T(8,128)(2,1)}, bf16[528,1280]{1,0:T(8,128)(2,1)S(1)}, u32[]{:S(2)}, u32[]{:S(2)}) collective-permute-start(bf16[528,1280]{1,0:T(8,128)(2,1)} %collective-permute-done.25), channel_id=1, source_target_pairs={{8,0},{12,4},{9,1},{13,5},{10,2},{14,6},{11,3},{15,7}} | collective-permute-start | bytes 4055048 | tf_op jit(solution)/shard_map/ppermute | solution.py:56
  215.2 51.3 %collective-permute-start.28 = (bf16[512,1280]{1,0:T(8,128)(2,1)}, bf16[512,1280]{1,0:T(8,128)(2,1)}, u32[]{:S(2)}, u32[]{:S(2)}) collective-permute-start(bf16[512,1280]{1,0:T(8,128)(2,1)} %collective-permute-done.22), channel_id=1, source_target_pairs={{8,16},{12,20},{16,24},{20,28},{9,17},{13,21},{17,25},{21,29},{10,... | collective-permute-start | bytes 3932168 | tf_op jit(solution)/shard_map/ppermute | solution.py:56
  216.9 58.2 %collective-permute-start.29 = (bf16[512,1280]{1,0:T(8,128)(2,1)}, bf16[512,1280]{1,0:T(8,128)(2,1)}, u32[]{:S(2)}, u32[]{:S(2)}) collective-permute-start(bf16[512,1280]{1,0:T(8,128)(2,1)} %collective-permute-done.23), channel_id=1, source_target_pairs={{8,0},{12,4},{16,8},{20,12},{9,1},{13,5},{17,9},{21,13},{10,2},{14... | collective-permute-start | bytes 3932168 | tf_op jit(solution)/shard_map/ppermute | solution.py:56
  283.8 33.0 %collective-permute-start.34 = (bf16[512,1280]{1,0:T(8,128)(2,1)}, bf16[512,1280]{1,0:T(8,128)(2,1)}, u32[]{:S(2)}, u32[]{:S(2)}) collective-permute-start(bf16[512,1280]{1,0:T(8,128)(2,1)} %collective-permute-done.29), channel_id=1, source_target_pairs={{8,0},{12,4},{9,1},{13,5},{10,2},{14,6},{11,3},{15,7}} | collective-permute-start | bytes 3932168 | tf_op jit(solution)/shard_map/ppermute | solution.py:56
  316.9 370.1 %reduce-scatter.4.cloned.1.call-start = ((), (), s32[]{:S(2)}) async-start(), calls=%async_computation.3 | async-start | bytes 17203200
  397.0 33.5 %collective-permute-start.45 = (bf16[512,1280]{1,0:T(8,128)(2,1)}, bf16[512,1280]{1,0:T(8,128)(2,1)}, u32[]{:S(2)}, u32[]{:S(2)}) collective-permute-start(bf16[512,1280]{1,0:T(8,128)(2,1)} %convert_element_type.371), channel_id=1, source_target_pairs={{0,8},{4,12},{1,9},{5,13},{2,10},{6,14},{3,11},{7,15}} | collective-permute-start | bytes 3932168 | tf_op jit(solution)/shard_map/ppermute | solution.py:56
  435.8 42.2 %collective-permute-start.49 = (bf16[512,1280]{1,0:T(8,128)(2,1)}, bf16[512,1280]{1,0:T(8,128)(2,1)}, u32[]{:S(2)}, u32[]{:S(2)}) collective-permute-start(bf16[512,1280]{1,0:T(8,128)(2,1)} %add_convert_fusion.8), channel_id=1, source_target_pairs={{0,8},{4,12},{8,16},{12,20},{1,9},{5,13},{9,17},{13,21},{2,10},{6,... | collective-permute-start | bytes 3932168 | tf_op jit(solution)/shard_map/ppermute | solution.py:56
  441.3 36.7 %collective-permute-start.50 = (bf16[512,1280]{1,0:T(8,128)(2,1)}, bf16[512,1280]{1,0:T(8,128)(2,1)}, u32[]{:S(2)}, u32[]{:S(2)}) collective-permute-start(bf16[512,1280]{1,0:T(8,128)(2,1)} %add_convert_fusion.7), channel_id=1, source_target_pairs={{16,8},{20,12},{24,16},{28,20},{17,9},{21,13},{25,17},{29,21},{18,... | collective-permute-start | bytes 3932168 | tf_op jit(solution)/shard_map/ppermute | solution.py:56
  443.4 34.6 %collective-permute-start.52 = (bf16[640,2688]{1,0:T(8,128)(2,1)}, bf16[640,2688]{1,0:T(8,128)(2,1)}, u32[]{:S(2)}, u32[]{:S(2)}) collective-permute-start(bf16[640,2688]{1,0:T(8,128)(2,1)} %get-tuple-element.366), channel_id=1, source_target_pairs={{0,4},{4,0},{8,12},{12,8},{16,20},{20,16},{24,28},{28,24},{1,5},{5... | collective-permute-start | bytes 10321928 | tf_op jit(solution)/shard_map/ppermute | solution.py:23
  443.5 34.0 %collective-permute-start.51 = (bf16[512,1280]{1,0:T(8,128)(2,1)}, bf16[512,1280]{1,0:T(8,128)(2,1)}, u32[]{:S(2)}, u32[]{:S(2)}) collective-permute-start(bf16[512,1280]{1,0:T(8,128)(2,1)} %get-tuple-element.324), channel_id=1, source_target_pairs={{0,4},{4,0},{8,12},{12,8},{16,20},{20,16},{24,28},{28,24},{1,5},{5... | collective-permute-start | bytes 3932168 | tf_op jit(solution)/shard_map/ppermute | solution.py:23
  444.0 34.0 %collective-permute-start.47 = (bf16[512,1280]{1,0:T(8,128)(2,1)}, bf16[512,1280]{1,0:T(8,128)(2,1)}, u32[]{:S(2)}, u32[]{:S(2)}) collective-permute-start(bf16[512,1280]{1,0:T(8,128)(2,1)} %get-tuple-element.317), channel_id=1, source_target_pairs={{0,4},{4,0},{8,12},{12,8},{16,20},{20,16},{24,28},{28,24},{1,5},{5... | collective-permute-start | bytes 3932168 | tf_op jit(solution)/shard_map/ppermute | solution.py:23
  477.5 56.7 %collective-permute-start.48 = (bf16[512,1280]{1,0:T(8,128)(2,1)}, bf16[512,1280]{1,0:T(8,128)(2,1)}, u32[]{:S(2)}, u32[]{:S(2)}) collective-permute-start(bf16[512,1280]{1,0:T(8,128)(2,1)} %get-tuple-element.322), channel_id=1, source_target_pairs={{0,4},{4,0},{8,12},{12,8},{16,20},{20,16},{24,28},{28,24},{1,5},{5... | collective-permute-start | bytes 3932168 | tf_op jit(solution)/shard_map/ppermute | solution.py:23
  482.1 39.2 %collective-permute-start.55 = (bf16[160,2688]{1,0:T(8,128)(2,1)S(1)}, bf16[160,2688]{1,0:T(8,128)(2,1)S(1)}, u32[]{:S(2)}, u32[]{:S(2)}) collective-permute-start(bf16[160,2688]{1,0:T(8,128)(2,1)S(1)} %get-tuple-element.375), channel_id=1, source_target_pairs={{0,2},{1,3},{2,0},{3,1},{4,6},{5,7},{6,4},{7,5},{8,10},{9,11},{10,... | collective-permute-start | bytes 2580488 | tf_op jit(solution)/shard_map/ppermute | solution.py:27
  484.0 40.1 %collective-permute-start.56 = (bf16[160,2688]{1,0:T(8,128)(2,1)S(1)}, bf16[160,2688]{1,0:T(8,128)(2,1)S(1)}, u32[]{:S(2)}, u32[]{:S(2)}) collective-permute-start(bf16[160,2688]{1,0:T(8,128)(2,1)S(1)} %get-tuple-element.376), channel_id=1, source_target_pairs={{0,1},{1,0},{2,3},{3,2},{4,5},{5,4},{6,7},{7,6},{8,9},{9,8},{10,11... | collective-permute-start | bytes 2580488 | tf_op jit(solution)/shard_map/ppermute | solution.py:27
  489.6 35.8 %collective-permute-start.53 = (bf16[512,1280]{1,0:T(8,128)(2,1)S(1)}, bf16[512,1280]{1,0:T(8,128)(2,1)S(1)}, u32[]{:S(2)}, u32[]{:S(2)}) collective-permute-start(bf16[512,1280]{1,0:T(8,128)(2,1)S(1)} %add_convert_fusion.6), channel_id=1, source_target_pairs={{0,8},{4,12},{8,16},{12,20},{16,24},{20,28},{1,9},{5,13},{9,17},{1... | collective-permute-start | bytes 3932168 | tf_op jit(solution)/shard_map/ppermute | solution.py:56
  490.9 34.4 %collective-permute-start.54 = (bf16[512,1280]{1,0:T(8,128)(2,1)S(1)}, bf16[512,1280]{1,0:T(8,128)(2,1)S(1)}, u32[]{:S(2)}, u32[]{:S(2)}) collective-permute-start(bf16[512,1280]{1,0:T(8,128)(2,1)S(1)} %add_convert_fusion.5), channel_id=1, source_target_pairs={{8,0},{12,4},{16,8},{20,12},{24,16},{28,20},{9,1},{13,5},{17,9},{2... | collective-permute-start | bytes 3932168 | tf_op jit(solution)/shard_map/ppermute | solution.py:56
  525.4 35.9 %collective-permute-start.59 = (bf16[80,2688]{1,0:T(8,128)(2,1)}, bf16[80,2688]{1,0:T(8,128)(2,1)S(1)}, u32[]{:S(2)}, u32[]{:S(2)}) collective-permute-start(bf16[80,2688]{1,0:T(8,128)(2,1)} %slice.437), channel_id=1, source_target_pairs={{0,1},{1,0},{2,3},{3,2},{4,5},{5,4},{6,7},{7,6},{8,9},{9,8},{10,11... | collective-permute-start | bytes 1290248 | tf_op jit(solution)/shard_map/ppermute | solution.py:27
  527.5 33.8 %collective-permute-start.60 = (bf16[80,2688]{1,0:T(8,128)(2,1)S(1)}, bf16[80,2688]{1,0:T(8,128)(2,1)}, u32[]{:S(2)}, u32[]{:S(2)}) collective-permute-start(bf16[80,2688]{1,0:T(8,128)(2,1)S(1)} %slice.436), channel_id=1, source_target_pairs={{0,2},{1,3},{2,0},{3,1},{4,6},{5,7},{6,4},{7,5},{8,10},{9,11},{10,... | collective-permute-start | bytes 1290248 | tf_op jit(solution)/shard_map/ppermute | solution.py:27
  612.5 46.5 %collective-permute-start.68 = (bf16[160,3968]{1,0:T(8,128)(2,1)S(1)}, bf16[160,3968]{1,0:T(8,128)(2,1)S(1)}, u32[]{:S(2)}, u32[]{:S(2)}) collective-permute-start(bf16[160,3968]{1,0:T(8,128)(2,1)S(1)} %get-tuple-element.397), channel_id=1, source_target_pairs={{0,2},{1,3},{2,0},{3,1},{4,6},{5,7},{6,4},{7,5},{8,10},{9,11},{10,... | collective-permute-start | bytes 3809288 | tf_op jit(solution)/shard_map/ppermute | solution.py:27
  614.2 45.8 %collective-permute-start.69 = (bf16[160,3968]{1,0:T(8,128)(2,1)S(1)}, bf16[160,3968]{1,0:T(8,128)(2,1)}, u32[]{:S(2)}, u32[]{:S(2)}) collective-permute-start(bf16[160,3968]{1,0:T(8,128)(2,1)S(1)} %get-tuple-element.398), channel_id=1, source_target_pairs={{0,1},{1,0},{2,3},{3,2},{4,5},{5,4},{6,7},{7,6},{8,9},{9,8},{10,11... | collective-permute-start | bytes 3809288 | tf_op jit(solution)/shard_map/ppermute | solution.py:27
  618.5 44.1 %collective-permute-start.66 = (bf16[512,1280]{1,0:T(8,128)(2,1)S(1)}, bf16[512,1280]{1,0:T(8,128)(2,1)S(1)}, u32[]{:S(2)}, u32[]{:S(2)}) collective-permute-start(bf16[512,1280]{1,0:T(8,128)(2,1)S(1)} %add_convert_fusion.2), channel_id=1, source_target_pairs={{0,8},{4,12},{8,16},{12,20},{16,24},{20,28},{1,9},{5,13},{9,17},{1... | collective-permute-start | bytes 3932168 | tf_op jit(solution)/shard_map/ppermute | solution.py:56
  626.9 35.7 %collective-permute-start.67 = (bf16[512,1280]{1,0:T(8,128)(2,1)S(1)}, bf16[512,1280]{1,0:T(8,128)(2,1)S(1)}, u32[]{:S(2)}, u32[]{:S(2)}) collective-permute-start(bf16[512,1280]{1,0:T(8,128)(2,1)S(1)} %add_convert_fusion.1), channel_id=1, source_target_pairs={{8,0},{12,4},{16,8},{20,12},{24,16},{28,20},{9,1},{13,5},{17,9},{2... | collective-permute-start | bytes 3932168 | tf_op jit(solution)/shard_map/ppermute | solution.py:56
  (152 other events, 1849.3 us)
Sparse Core Ops, SparseCore 0:
  92.5 144.6 all-gather.5
  317.0 75.4 all-gather.3
  478.2 172.0 reduce-scatter.3

commit v4 on v3

--- a/solution.py
+++ b/solution.py
@@ -780,42 +780,42 @@
     out_grad = [dot(after(mixed_rel, *in_grad)[:, cut], attn_cot, TN).astype(BF16) for cut in halves]
     out_scatter = DenseScatter(*out_grad)
     swap_out = out_scatter.swap()
-    normed_one_cot = dot(after(projected_cot, *in_grad), project, NT)
-    scaled_one = normed_one_cot * gain_one
-    gain_one_grad = jnp.sum(normed_one_cot * unit_one, axis=0)
     true_part = exact_matmul(
         jnp.concatenate([gain_two_grad[None, :], router_part], axis=0), order, NN
     )
-    small_grad = jnp.concatenate([gain_one_grad[None, :], true_part], axis=0)
-    small_grad = jnp.pad(small_grad, ((0, LANES - small_grad.shape[0]), (0, 0))).T
-    small_scatter = DenseScatter(small_grad[:half], small_grad[half:], F32)
-    swap_small = small_scatter.swap()
-    moved = []
-    done = [swap_in, swap_small, swap_out, scaled_one, going_out, moved]
+    done = [swap_in, swap_out]
 
     for i in range(k):
-        going = [in_scatter.exchange(i, *done, extra=small_scatter if i == 0 else None)]
+        going = [in_scatter.exchange(i, *done)]
         if i == 0:
-            token_part = after(root_one, *done) * (
+            normed_one_cot = dot(after(projected_cot, *done), project, NT)
+            scaled_one = normed_one_cot * gain_one
+            gain_one_grad = jnp.sum(normed_one_cot * unit_one, axis=0)
+            small_grad = jnp.concatenate([gain_one_grad[None, :], true_part], axis=0)
+            small_grad = jnp.pad(small_grad, ((0, LANES - small_grad.shape[0]), (0, 0))).T
+            small_scatter = DenseScatter(small_grad[:half], small_grad[half:], F32)
+            token_part = root_one * (
                 scaled_one - unit_one * jnp.mean(scaled_one * unit_one, axis=-1, keepdims=True)
             )
             token_gradient = hidden_cot + split_matmul(token_part, order, NT)
-            going += [token_gradient]
+            going += [token_gradient, small_grad]
             for s in range(3, n):
-                going_out = out_sums.step(out_slots[n - s], out_slots[s], *done)
+                going_out = out_sums.step(out_slots[n - s], out_slots[s], *done, normed_one_cot)
             going.append(going_out)
         elif i == 1:
-            going += [scatter.line(*done), expert_sum]
+            going += [scatter.line(*done), expert_sum, small_scatter.swap(*done)]
         done = [going]
     last = [in_scatter.line(*done)]
-    last += [out_scatter.exchange(i, *done) for i in range(k)]
+    last += [
+        out_scatter.exchange(i, *done, extra=small_scatter if i == 0 else None) for i in range(k)
+    ]
     out_scatter.line()
     shared_gradient = scatter.total().reshape(rows, 3, units)
-    in_total = in_scatter.total()
-    in_gradient = in_total[:, : 3 * width].reshape(rows, 3, width)
-    out_gradient = out_scatter.total()
+    in_gradient = in_scatter.total().reshape(rows, 3, width)
+    out_total = out_scatter.total()
+    out_gradient = out_total[:, :width]
     attention_gradient = jnp.concatenate([in_gradient, out_gradient[:, None, :]], axis=1)
-    small_gradient = in_total[:, 3 * width :]
+    small_gradient = out_total[:, width:]
     out_sum = out_sums.total(out_slots[0])
     block_output = (hidden_res + shared_out + out_sum).astype(BF16)
     expert_gradient = jnp.transpose(expert_sum, (0, 1, 3, 2)).astype(F32)

time: 746 us -> 745 us (level)
    unnamed x216 -> x212, local copies, waits for them, and re-layouts: 25.6 us -> 25.6 us
  transfers between devices with their start and end apart: 88 -> 88, of which waited for: 32 -> 35; matrix products, arithmetic and copies ran while one was open for 20% -> 20% of each run, Pallas kernels for 27% -> 27%
where the time goes in v4:
time: 745 us; the launch traced here: 734 us
  waiting for transfers between devices  213 us (29%)
  Pallas kernels  200 us (27%)
  starting transfers between devices  127 us (17%)
  other arithmetic  78.1 us (10%)
  matrix products  58.7 us (8%)
  local copies, waits for them, and re-layouts  42 us (6%)
  between operations  15.8 us (2%)
    pallas_call x4, Pallas kernels, expert_chunk(): pl.pallas_call(expert_kernel, grid_spec=pltpu.PrefetchScalarGridSpec(num_...  118 us
    ppermute x20, waiting for transfers between devices, fsdp_swap(): lax.ppermute(x, 'fsdp', [(f, f ^ bit) for f in range(lax.axis_size('fsdp'...  84.2 us
    ppermute x30, waiting for transfers between devices, line_send(): return lax.ppermute(x, 'dp', pairs)  73.9 us
    ppermute x30, starting transfers between devices, line_send(): return lax.ppermute(x, 'dp', pairs)  70.9 us
    dot_general x15, matrix products, dot(): return lax.dot_general(a, b, (dims, ((), ())), preferred_element_type=F32)  55.9 us
    pallas_call x1, Pallas kernels, expert_weight_grads(): pl.pallas_call(expert_weights_kernel, grid=(local, 3), in_specs=[pl.Block...  33.8 us
    ppermute x20, starting transfers between devices, fsdp_swap(): lax.ppermute(x, 'fsdp', [(f, f ^ bit) for f in range(lax.axis_size('fsdp'...  25.7 us
    unnamed x212, local copies, waits for them, and re-layouts  25.6 us
  transfers between devices with their start and end apart: 88, of which 35 were waited for; matrix products, arithmetic and copies ran while one was open for 20% of the time, Pallas kernels for 27%

profile of v4, /device:TPU:0, one launch (start us, length us, event | category | flops | bytes accessed | tf_op | source)
XLA Modules:
  0.0 734.3 jit_solution(2065215174181916765)
XLA Ops:
  10.0 5.1 collective-permute-start
  29.4 12.7 %collective-permute-done.1 = bf16[40,3968]{1,0:T(8,128)(2,1)S(1)} collective-permute-done((bf16[40,3968]{1,0:T(8,128)(2,1)S(1)}, bf16[40,3968]{1,0:T(8,128)(2,1)S(1)}, u32[]{:S(2)}, u32[]{:S(2)}) %collective-permute-start.1) | collective-permute-done | bytes 317472 | tf_op jit(solution)/shard_map/ppermute | solution.py:39
  49.7 7.8 %collective-permute-done.4 = bf16[80,3968]{1,0:T(8,128)(2,1)S(1)} collective-permute-done((bf16[80,3968]{1,0:T(8,128)(2,1)S(1)}, bf16[80,3968]{1,0:T(8,128)(2,1)S(1)}, u32[]{:S(2)}, u32[]{:S(2)}) %collective-permute-start.4) | collective-permute-done | bytes 634912 | tf_op jit(solution)/shard_map/ppermute | solution.py:27
  63.1 8.1 %collective-permute-done.11 = bf16[40,1280]{1,0:T(8,128)(2,1)S(1)} collective-permute-done((bf16[40,1280]{1,0:T(8,128)(2,1)S(1)}, bf16[40,1280]{1,0:T(8,128)(2,1)S(1)}, u32[]{:S(2)}, u32[]{:S(2)}) %collective-permute-start.11) | collective-permute-done | bytes 102432 | tf_op jit(solution)/shard_map/ppermute | solution.py:56
  73.2 5.2 collective-permute-done.13
  78.5 10.9 %collective-permute-done.7 = bf16[160,3968]{1,0:T(8,128)(2,1)S(1)} collective-permute-done((bf16[160,3968]{1,0:T(8,128)(2,1)S(1)}, bf16[160,3968]{1,0:T(8,128)(2,1)S(1)}, u32[]{:S(2)}, u32[]{:S(2)}) %collective-permute-start.7) | collective-permute-done | bytes 1269792 | tf_op jit(solution)/shard_map/ppermute | solution.py:27
  113.4 7.5 %fusion.2.qp.kp.vp = f32[512,3840]{1,0:T(8,128)} fusion(bf16[512,1280]{0,1:T(8,128)(2,1)S(1)} %multiply_convert_fusion.1, bf16[1280,3968]{1,0:T(8,128)(2,1)S(1)} %slice_dynamic-update-slice_fusion), kind=kOutput, calls=%fused_computation.3 | convolution fusion | flops 5033164800 | bytes 19005440 | tf_op jit(solution)/shard_map/dot_general | solution.py:234
  123.5 12.9 %attention_forward.1 = (bf16[512,1280]{1,0:T(8,128)(2,1)}, bf16[512,1280]{1,0:T(8,128)(2,1)}, bf16[512,1280]{1,0:T(8,128)(2,1)}, bf16[512,1280]{1,0:T(8,128)(2,1)}, f32[10,1,512]{2,1,0:T(1,128)}) custom-call(f32[512,3840]{1,0:T(8,128)} %fusion.2.qp.kp.vp, f32[512,3840]{1,0:T(8,128)} %fusion.2.qp.kp.vp, f32[512,3840]{1,0:T(8,128)} %fusion.2.qp.kp.vp, ...), custom_call_target="tpu_custom_call" | custom-call | flops 14000000000 | bytes 35000000 | tf_op jit(solution)/shard_map/attention_forward/pallas_call | solution.py:283
  155.1 11.7 %collective-permute-start.22 = (bf16[512,1280]{1,0:T(8,128)(2,1)}, bf16[512,1280]{1,0:T(8,128)(2,1)}, u32[]{:S(2)}, u32[]{:S(2)}) collective-permute-start(bf16[512,1280]{1,0:T(8,128)(2,1)} %multiply_convert_fusion.x_own.x), channel_id=1, source_target_pairs={{0,8},{4,12},{8,16},{12,20},{16,24},{20,28},{1,9},{5,13},{9,17},{1... | collective-permute-start | bytes 3932168 | tf_op jit(solution)/shard_map/ppermute | solution.py:56
  170.0 15.7 %collective-permute-done.25 = bf16[528,1280]{1,0:T(8,128)(2,1)} collective-permute-done((bf16[528,1280]{1,0:T(8,128)(2,1)}, bf16[528,1280]{1,0:T(8,128)(2,1)}, u32[]{:S(2)}, u32[]{:S(2)}) %collective-permute-start.25) | collective-permute-done | bytes 1351712 | tf_op jit(solution)/shard_map/ppermute | solution.py:56
  185.7 9.0 %collective-permute-done.22 = bf16[512,1280]{1,0:T(8,128)(2,1)} collective-permute-done((bf16[512,1280]{1,0:T(8,128)(2,1)}, bf16[512,1280]{1,0:T(8,128)(2,1)}, u32[]{:S(2)}, u32[]{:S(2)}) %collective-permute-start.22) | collective-permute-done | bytes 1310752 | tf_op jit(solution)/shard_map/ppermute | solution.py:56
  194.7 18.4 %collective-permute-done.23 = bf16[512,1280]{1,0:T(8,128)(2,1)} collective-permute-done((bf16[512,1280]{1,0:T(8,128)(2,1)}, bf16[512,1280]{1,0:T(8,128)(2,1)}, u32[]{:S(2)}, u32[]{:S(2)}) %collective-permute-start.23) | collective-permute-done | bytes 1310752 | tf_op jit(solution)/shard_map/ppermute | solution.py:56
  218.4 18.9 %all-gather.6.cloned.1.call-done = bf16[8,3,224,1280]{3,2,1,0:T(8,128)(2,1)} async-done(((bf16[2,3,224,1280]{3,2,1,0:T(8,128)(2,1)}), bf16[8,3,224,1280]{3,2,1,0:T(8,128)(2,1)}) %all-gather.6.cloned.1.call-update) | async-done | bytes 13762576 | tf_op jit(solution)/shard_map/all_gather | solution.py:640
  237.3 29.2 %expert_chunk.4 = (bf16[2,384,1280]{2,1,0:T(8,128)(2,1)}, bf16[2,384,1280]{2,1,0:T(8,128)(2,1)}, bf16[2,384,896]{2,1,0:T(8,128)(2,1)}, bf16[2,384,896]{2,1,0:T(8...) custom-call(s32[1]{0:T(128)} %bitcast.37.first, ...), custom_call_target="tpu_custom_call" | custom-call | flops 30000001024 | bytes 75000000 | tf_op jit(solution)/shard_map/expert_chunk/pallas_call | solution.py:447
  266.6 8.6 %collective-permute-done.29 = bf16[512,1280]{1,0:T(8,128)(2,1)} collective-permute-done((bf16[512,1280]{1,0:T(8,128)(2,1)}, bf16[512,1280]{1,0:T(8,128)(2,1)}, u32[]{:S(2)}, u32[]{:S(2)}) %collective-permute-start.29) | collective-permute-done | bytes 1310752 | tf_op jit(solution)/shard_map/ppermute | solution.py:56
  287.1 29.2 %expert_chunk.5 = (bf16[2,384,1280]{2,1,0:T(8,128)(2,1)}, bf16[2,384,1280]{2,1,0:T(8,128)(2,1)}, bf16[2,384,896]{2,1,0:T(8,128)(2,1)}, bf16[2,384,896]{2,1,0:T(8...) custom-call(s32[1]{0:T(128)} %bitcast.37.first, ...), custom_call_target="tpu_custom_call" | custom-call | flops 30000001024 | bytes 75000000 | tf_op jit(solution)/shard_map/expert_chunk/pallas_call | solution.py:447
  327.4 29.6 %expert_chunk.6 = (bf16[2,384,1280]{2,1,0:T(8,128)(2,1)}, bf16[2,384,1280]{2,1,0:T(8,128)(2,1)}, bf16[2,384,896]{2,1,0:T(8,128)(2,1)}, bf16[2,384,896]{2,1,0:T(8...) custom-call(s32[1]{0:T(128)} %bitcast.37.first, ...), custom_call_target="tpu_custom_call" | custom-call | flops 30000001024 | bytes 75000000 | tf_op jit(solution)/shard_map/expert_chunk/pallas_call | solution.py:447
  358.6 29.4 %expert_chunk.7 = (bf16[2,384,1280]{2,1,0:T(8,128)(2,1)}, bf16[2,384,1280]{2,1,0:T(8,128)(2,1)}, bf16[2,384,896]{2,1,0:T(8,128)(2,1)}, bf16[2,384,896]{2,1,0:T(8...) custom-call(s32[1]{0:T(128)} %bitcast.37.first, ...), custom_call_target="tpu_custom_call" | custom-call | flops 30000001024 | bytes 75000000 | tf_op jit(solution)/shard_map/expert_chunk/pallas_call | solution.py:447
  397.0 6.1 collective-permute-start.45
  407.0 21.0 %shared_expert.1 = (f32[512,1280]{1,0:T(8,128)}, f32[512,1280]{1,0:T(8,128)}, bf16[640,2688]{1,0:T(8,128)(2,1)}, bf16[640,2688]{1,0:T(8,128)(2,1)}) custom-call(bf16[512,1280]{1,0:T(8,128)(2,1)} %multiply_convert_fusion.x_own.x, bf16[512,1280]{1,0:T(8,128)(2,1)} %c.1, bf16[512,1280]{1,0:T(8,128)(2,1)} %fusion.26.c_rel, ...), custom_call_target="tpu_custom_call" | custom-call | flops 30000001024 | bytes 75000000 | tf_op jit(solution)/shard_map/shared_expert/pallas_call | solution.py:540
  435.9 5.5 collective-permute-start.49
  443.9 33.8 %expert_weights.1 = bf16[4,2,3,224,1280]{4,3,2,1,0:T(8,128)(2,1)} custom-call(bf16[2,384,1280]{2,1,0:T(8,128)(2,1)} %get-tuple-element.346.refs_0_, bf16[2,384,1280]{2,1,0:T(8,128)(2,1)} %get-tuple-element.347.refs_1_, bf16[2,384,1280]{2,1,0:T(8,128)(2,1)} %get-tuple-element.348.refs_2_, bf16[2,384,1280]{2,1,0:T(8,128)(2,1)} %get-tuple-element.349.refs_3_, ...), custom_call_target="tpu_custom_call" | custom-call | flops 42278584320 | bytes 105696464 | tf_op jit(solution)/shard_map/expert_weights/pallas_call | solution.py:503
  494.2 27.3 %collective-permute-done.55 = bf16[160,2688]{1,0:T(8,128)(2,1)S(1)} collective-permute-done((bf16[160,2688]{1,0:T(8,128)(2,1)S(1)}, bf16[160,2688]{1,0:T(8,128)(2,1)S(1)}, u32[]{:S(2)}, u32[]{:S(2)}) %collective-permute-start.55) | collective-permute-done | bytes 860192 | tf_op jit(solution)/shard_map/ppermute | solution.py:27
  539.6 7.6 %fusion.24.d_in = bf16[512,1280]{1,0:T(8,128)(2,1)} fusion(s32[1280]{0:T(1024)S(1)} %copy-done.80, bf16[1280,1280]{1,0:T(8,128)(2,1)} %copy-done.76, f32[512,1280]{1,0:T(8,128)} %multiply_add_fusion), kind=kOutput, calls=%fused_computation.40 | convolution fusion | flops 3359047680 | bytes 7214080 | tf_op jit(solution)/shard_map/dot_general | solution.py:234
  547.2 14.5 %attention_backward.1 = (bf16[512,1280]{1,0:T(8,128)(2,1)}, bf16[512,1280]{1,0:T(8,128)(2,1)}, bf16[512,1280]{1,0:T(8,128)(2,1)}) custom-call(bf16[512,1280]{1,0:T(8,128)(2,1)} %get-tuple-element.318.q_in, bf16[512,1280]{1,0:T(8,128)(2,1)} %get-tuple-element.319.k_in, bf16[512,1280]{1,0:T(8,128)(2,1)} %get-tuple-element.320.v_in, ...), custom_call_target="tpu_custom_call" | custom-call | flops 15000000512 | bytes 37500000 | tf_op jit(solution)/shard_map/attention_backward/pallas_call | solution.py:321
  578.1 5.2 convert_add_fusion
  597.7 9.6 %fusion = f32[512,1280]{1,0:T(8,128)} fusion(bf16[512,3840]{1,0:T(8,128)(2,1)S(1)} %constant_dynamic-update-slice_fusion.12, bf16[1280,3968]{1,0:T(8,128)(2,1)} %copy-done.65), kind=kOutput, calls=%fused_computation.1 | convolution fusion | flops 5033164800 | bytes 16384000 | tf_op jit(solution)/shard_map/dot_general | solution.py:234
  622.3 6.4 collective-permute-start.65
  638.5 13.5 %collective-permute-done.67 = bf16[160,3840]{1,0:T(8,128)(2,1)} collective-permute-done((bf16[160,3840]{1,0:T(8,128)(2,1)}, bf16[160,3840]{1,0:T(8,128)(2,1)}, u32[]{:S(2)}, u32[]{:S(2)}) %collective-permute-start.67) | collective-permute-done | bytes 1228832 | tf_op jit(solution)/shard_map/ppermute | solution.py:27
  671.1 6.5 collective-permute-done.73
  707.9 5.4 collective-permute-start.79
  716.6 8.1 %collective-permute-done.80 = bf16[40,1408]{1,0:T(8,128)(2,1)S(1)} collective-permute-done((bf16[40,1408]{1,0:T(8,128)(2,1)S(1)}, bf16[40,1408]{1,0:T(8,128)(2,1)S(1)}, u32[]{:S(2)}, u32[]{:S(2)}) %collective-permute-start.80) | collective-permute-done | bytes 112672 | tf_op jit(solution)/shard_map/ppermute | solution.py:47
  (500 shorter events, 278.1 us)
Async XLA Ops:
  7.2 230.1 %all-gather.6.cloned.1.call-start = ((), (), s32[]{:S(2)}) async-start(), calls=%async_computation.2 | async-start | bytes 17203200 | tf_op jit(solution)/shard_map/all_gather | solution.py:640
  92.4 314.6 %all-gather.4.cloned.1.call-start = ((), (), s32[]{:S(2)}) async-start(), calls=%async_computation.1 | async-start | bytes 7096320 | tf_op jit(solution)/shard_map/all_gather | solution.py:710
  95.7 45.2 %collective-permute-start.19 = (bf16[528,1280]{1,0:T(8,128)(2,1)S(1)}, bf16[528,1280]{1,0:T(8,128)(2,1)S(1)}, u32[]{:S(2)}, u32[]{:S(2)}) collective-permute-start(bf16[528,1280]{1,0:T(8,128)(2,1)S(1)} %copy-done.37), channel_id=1, source_target_pairs={{0,8},{4,12},{8,16},{12,20},{16,24},{20,28},{1,9},{5,13},{9,17},{1... | collective-permute-start | bytes 4055048 | tf_op jit(solution)/shard_map/ppermute | solution.py:56
  98.9 42.1 %collective-permute-start.20 = (bf16[528,1280]{1,0:T(8,128)(2,1)S(1)}, bf16[528,1280]{1,0:T(8,128)(2,1)}, u32[]{:S(2)}, u32[]{:S(2)}) collective-permute-start(bf16[528,1280]{1,0:T(8,128)(2,1)S(1)} %copy-done.37), channel_id=1, source_target_pairs={{8,0},{12,4},{16,8},{20,12},{24,16},{28,20},{9,1},{13,5},{17,9},{2... | collective-permute-start | bytes 4055048 | tf_op jit(solution)/shard_map/ppermute | solution.py:56
  144.8 41.0 %collective-permute-start.25 = (bf16[528,1280]{1,0:T(8,128)(2,1)}, bf16[528,1280]{1,0:T(8,128)(2,1)}, u32[]{:S(2)}, u32[]{:S(2)}) collective-permute-start(bf16[528,1280]{1,0:T(8,128)(2,1)} %collective-permute-done.20), channel_id=1, source_target_pairs={{8,0},{12,4},{16,8},{20,12},{9,1},{13,5},{17,9},{21,13},{10,2},{14... | collective-permute-start | bytes 4055048 | tf_op jit(solution)/shard_map/ppermute | solution.py:56
  154.9 58.3 %collective-permute-start.27 = (bf16[528,1280]{1,0:T(8,128)(2,1)S(1)}, bf16[528,1280]{1,0:T(8,128)(2,1)}, u32[]{:S(2)}, u32[]{:S(2)}) collective-permute-start(bf16[528,1280]{1,0:T(8,128)(2,1)S(1)} %copy-done.37), channel_id=1, source_target_pairs={{0,4},{4,0},{8,12},{12,8},{16,20},{20,16},{24,28},{28,24},{1,5},{5... | collective-permute-start | bytes 4055048 | tf_op jit(solution)/shard_map/ppermute | solution.py:23
  155.1 39.6 %collective-permute-start.22 = (bf16[512,1280]{1,0:T(8,128)(2,1)}, bf16[512,1280]{1,0:T(8,128)(2,1)}, u32[]{:S(2)}, u32[]{:S(2)}) collective-permute-start(bf16[512,1280]{1,0:T(8,128)(2,1)} %multiply_convert_fusion.x_own.x), channel_id=1, source_target_pairs={{0,8},{4,12},{8,16},{12,20},{16,24},{20,28},{1,9},{5,13},{9,17},{1... | collective-permute-start | bytes 3932168 | tf_op jit(solution)/shard_map/ppermute | solution.py:56
  166.8 46.4 %collective-permute-start.23 = (bf16[512,1280]{1,0:T(8,128)(2,1)}, bf16[512,1280]{1,0:T(8,128)(2,1)}, u32[]{:S(2)}, u32[]{:S(2)}) collective-permute-start(bf16[512,1280]{1,0:T(8,128)(2,1)} %multiply_convert_fusion.x_own.x), channel_id=1, source_target_pairs={{8,0},{12,4},{16,8},{20,12},{24,16},{28,20},{9,1},{13,5},{17,9},{2... | collective-permute-start | bytes 3932168 | tf_op jit(solution)/shard_map/ppermute | solution.py:56
  169.2 43.9 %collective-permute-start.26 = (bf16[512,1280]{1,0:T(8,128)(2,1)}, bf16[512,1280]{1,0:T(8,128)(2,1)}, u32[]{:S(2)}, u32[]{:S(2)}) collective-permute-start(bf16[512,1280]{1,0:T(8,128)(2,1)} %multiply_convert_fusion.x_own.x), channel_id=1, source_target_pairs={{0,4},{4,0},{8,12},{12,8},{16,20},{20,16},{24,28},{28,24},{1,5},{5... | collective-permute-start | bytes 3932168 | tf_op jit(solution)/shard_map/ppermute | solution.py:23
  213.1 62.0 %collective-permute-start.30 = (bf16[528,1280]{1,0:T(8,128)(2,1)}, bf16[528,1280]{1,0:T(8,128)(2,1)S(1)}, u32[]{:S(2)}, u32[]{:S(2)}) collective-permute-start(bf16[528,1280]{1,0:T(8,128)(2,1)} %copy-done.40), channel_id=1, source_target_pairs={{16,24},{20,28},{17,25},{21,29},{18,26},{22,30},{19,27},{23,31}} | collective-permute-start | bytes 4055048 | tf_op jit(solution)/shard_map/ppermute | solution.py:56
  213.9 61.3 %collective-permute-start.31 = (bf16[528,1280]{1,0:T(8,128)(2,1)}, bf16[528,1280]{1,0:T(8,128)(2,1)S(1)}, u32[]{:S(2)}, u32[]{:S(2)}) collective-permute-start(bf16[528,1280]{1,0:T(8,128)(2,1)} %collective-permute-done.25), channel_id=1, source_target_pairs={{8,0},{12,4},{9,1},{13,5},{10,2},{14,6},{11,3},{15,7}} | collective-permute-start | bytes 4055048 | tf_op jit(solution)/shard_map/ppermute | solution.py:56
  215.2 51.4 %collective-permute-start.28 = (bf16[512,1280]{1,0:T(8,128)(2,1)}, bf16[512,1280]{1,0:T(8,128)(2,1)}, u32[]{:S(2)}, u32[]{:S(2)}) collective-permute-start(bf16[512,1280]{1,0:T(8,128)(2,1)} %collective-permute-done.22), channel_id=1, source_target_pairs={{8,16},{12,20},{16,24},{20,28},{9,17},{13,21},{17,25},{21,29},{10,... | collective-permute-start | bytes 3932168 | tf_op jit(solution)/shard_map/ppermute | solution.py:56
  216.9 58.2 %collective-permute-start.29 = (bf16[512,1280]{1,0:T(8,128)(2,1)}, bf16[512,1280]{1,0:T(8,128)(2,1)}, u32[]{:S(2)}, u32[]{:S(2)}) collective-permute-start(bf16[512,1280]{1,0:T(8,128)(2,1)} %collective-permute-done.23), channel_id=1, source_target_pairs={{8,0},{12,4},{16,8},{20,12},{9,1},{13,5},{17,9},{21,13},{10,2},{14... | collective-permute-start | bytes 3932168 | tf_op jit(solution)/shard_map/ppermute | solution.py:56
  283.8 33.0 %collective-permute-start.34 = (bf16[512,1280]{1,0:T(8,128)(2,1)}, bf16[512,1280]{1,0:T(8,128)(2,1)}, u32[]{:S(2)}, u32[]{:S(2)}) collective-permute-start(bf16[512,1280]{1,0:T(8,128)(2,1)} %collective-permute-done.29), channel_id=1, source_target_pairs={{8,0},{12,4},{9,1},{13,5},{10,2},{14,6},{11,3},{15,7}} | collective-permute-start | bytes 3932168 | tf_op jit(solution)/shard_map/ppermute | solution.py:56
  316.9 365.6 %reduce-scatter.4.cloned.1.call-start = ((), (), s32[]{:S(2)}) async-start(), calls=%async_computation.3 | async-start | bytes 17203200
  324.9 32.6 %collective-permute-start.39 = (bf16[528,1280]{1,0:T(8,128)(2,1)S(1)}, bf16[528,1280]{1,0:T(8,128)(2,1)S(1)}, u32[]{:S(2)}, u32[]{:S(2)}) collective-permute-start(bf16[528,1280]{1,0:T(8,128)(2,1)S(1)} %broadcast_select_fusion.c_own), channel_id=1, source_target_pairs={{0,4},{4,0},{8,12},{12,8},{16,20},{20,16},{24,28},{28,24},{1,5},{5... | collective-permute-start | bytes 4055048 | tf_op jit(solution)/shard_map/ppermute | solution.py:23
  397.0 33.7 %collective-permute-start.45 = (bf16[512,1280]{1,0:T(8,128)(2,1)}, bf16[512,1280]{1,0:T(8,128)(2,1)}, u32[]{:S(2)}, u32[]{:S(2)}) collective-permute-start(bf16[512,1280]{1,0:T(8,128)(2,1)} %convert_element_type.371), channel_id=1, source_target_pairs={{0,8},{4,12},{1,9},{5,13},{2,10},{6,14},{3,11},{7,15}} | collective-permute-start | bytes 3932168 | tf_op jit(solution)/shard_map/ppermute | solution.py:56
  435.9 42.3 %collective-permute-start.49 = (bf16[512,1280]{1,0:T(8,128)(2,1)}, bf16[512,1280]{1,0:T(8,128)(2,1)}, u32[]{:S(2)}, u32[]{:S(2)}) collective-permute-start(bf16[512,1280]{1,0:T(8,128)(2,1)} %add_convert_fusion.8), channel_id=1, source_target_pairs={{0,8},{4,12},{8,16},{12,20},{1,9},{5,13},{9,17},{13,21},{2,10},{6,... | collective-permute-start | bytes 3932168 | tf_op jit(solution)/shard_map/ppermute | solution.py:56
  441.4 36.9 %collective-permute-start.50 = (bf16[512,1280]{1,0:T(8,128)(2,1)}, bf16[512,1280]{1,0:T(8,128)(2,1)}, u32[]{:S(2)}, u32[]{:S(2)}) collective-permute-start(bf16[512,1280]{1,0:T(8,128)(2,1)} %add_convert_fusion.7), channel_id=1, source_target_pairs={{16,8},{20,12},{24,16},{28,20},{17,9},{21,13},{25,17},{29,21},{18,... | collective-permute-start | bytes 3932168 | tf_op jit(solution)/shard_map/ppermute | solution.py:56
  443.3 35.0 %collective-permute-start.52 = (bf16[640,2688]{1,0:T(8,128)(2,1)}, bf16[640,2688]{1,0:T(8,128)(2,1)}, u32[]{:S(2)}, u32[]{:S(2)}) collective-permute-start(bf16[640,2688]{1,0:T(8,128)(2,1)} %get-tuple-element.366), channel_id=1, source_target_pairs={{0,4},{4,0},{8,12},{12,8},{16,20},{20,16},{24,28},{28,24},{1,5},{5... | collective-permute-start | bytes 10321928 | tf_op jit(solution)/shard_map/ppermute | solution.py:23
  443.4 34.4 %collective-permute-start.51 = (bf16[512,1280]{1,0:T(8,128)(2,1)}, bf16[512,1280]{1,0:T(8,128)(2,1)}, u32[]{:S(2)}, u32[]{:S(2)}) collective-permute-start(bf16[512,1280]{1,0:T(8,128)(2,1)} %get-tuple-element.324), channel_id=1, source_target_pairs={{0,4},{4,0},{8,12},{12,8},{16,20},{20,16},{24,28},{28,24},{1,5},{5... | collective-permute-start | bytes 3932168 | tf_op jit(solution)/shard_map/ppermute | solution.py:23
  443.9 34.4 %collective-permute-start.47 = (bf16[512,1280]{1,0:T(8,128)(2,1)}, bf16[512,1280]{1,0:T(8,128)(2,1)}, u32[]{:S(2)}, u32[]{:S(2)}) collective-permute-start(bf16[512,1280]{1,0:T(8,128)(2,1)} %get-tuple-element.317), channel_id=1, source_target_pairs={{0,4},{4,0},{8,12},{12,8},{16,20},{20,16},{24,28},{28,24},{1,5},{5... | collective-permute-start | bytes 3932168 | tf_op jit(solution)/shard_map/ppermute | solution.py:23
  477.8 56.8 %collective-permute-start.48 = (bf16[512,1280]{1,0:T(8,128)(2,1)}, bf16[512,1280]{1,0:T(8,128)(2,1)}, u32[]{:S(2)}, u32[]{:S(2)}) collective-permute-start(bf16[512,1280]{1,0:T(8,128)(2,1)} %get-tuple-element.322), channel_id=1, source_target_pairs={{0,4},{4,0},{8,12},{12,8},{16,20},{20,16},{24,28},{28,24},{1,5},{5... | collective-permute-start | bytes 3932168 | tf_op jit(solution)/shard_map/ppermute | solution.py:23
  482.3 39.3 %collective-permute-start.55 = (bf16[160,2688]{1,0:T(8,128)(2,1)S(1)}, bf16[160,2688]{1,0:T(8,128)(2,1)S(1)}, u32[]{:S(2)}, u32[]{:S(2)}) collective-permute-start(bf16[160,2688]{1,0:T(8,128)(2,1)S(1)} %get-tuple-element.375), channel_id=1, source_target_pairs={{0,2},{1,3},{2,0},{3,1},{4,6},{5,7},{6,4},{7,5},{8,10},{9,11},{10,... | collective-permute-start | bytes 2580488 | tf_op jit(solution)/shard_map/ppermute | solution.py:27
  484.2 40.2 %collective-permute-start.56 = (bf16[160,2688]{1,0:T(8,128)(2,1)S(1)}, bf16[160,2688]{1,0:T(8,128)(2,1)S(1)}, u32[]{:S(2)}, u32[]{:S(2)}) collective-permute-start(bf16[160,2688]{1,0:T(8,128)(2,1)S(1)} %get-tuple-element.376), channel_id=1, source_target_pairs={{0,1},{1,0},{2,3},{3,2},{4,5},{5,4},{6,7},{7,6},{8,9},{9,8},{10,11... | collective-permute-start | bytes 2580488 | tf_op jit(solution)/shard_map/ppermute | solution.py:27
  489.9 35.8 %collective-permute-start.53 = (bf16[512,1280]{1,0:T(8,128)(2,1)S(1)}, bf16[512,1280]{1,0:T(8,128)(2,1)S(1)}, u32[]{:S(2)}, u32[]{:S(2)}) collective-permute-start(bf16[512,1280]{1,0:T(8,128)(2,1)S(1)} %add_convert_fusion.6), channel_id=1, source_target_pairs={{0,8},{4,12},{8,16},{12,20},{16,24},{20,28},{1,9},{5,13},{9,17},{1... | collective-permute-start | bytes 3932168 | tf_op jit(solution)/shard_map/ppermute | solution.py:56
  491.3 34.4 %collective-permute-start.54 = (bf16[512,1280]{1,0:T(8,128)(2,1)S(1)}, bf16[512,1280]{1,0:T(8,128)(2,1)S(1)}, u32[]{:S(2)}, u32[]{:S(2)}) collective-permute-start(bf16[512,1280]{1,0:T(8,128)(2,1)S(1)} %add_convert_fusion.5), channel_id=1, source_target_pairs={{8,0},{12,4},{16,8},{20,12},{24,16},{28,20},{9,1},{13,5},{17,9},{2... | collective-permute-start | bytes 3932168 | tf_op jit(solution)/shard_map/ppermute | solution.py:56
  525.7 36.0 %collective-permute-start.59 = (bf16[80,2688]{1,0:T(8,128)(2,1)}, bf16[80,2688]{1,0:T(8,128)(2,1)S(1)}, u32[]{:S(2)}, u32[]{:S(2)}) collective-permute-start(bf16[80,2688]{1,0:T(8,128)(2,1)} %slice.436), channel_id=1, source_target_pairs={{0,1},{1,0},{2,3},{3,2},{4,5},{5,4},{6,7},{7,6},{8,9},{9,8},{10,11... | collective-permute-start | bytes 1290248 | tf_op jit(solution)/shard_map/ppermute | solution.py:27
  527.8 33.9 %collective-permute-start.60 = (bf16[80,2688]{1,0:T(8,128)(2,1)S(1)}, bf16[80,2688]{1,0:T(8,128)(2,1)}, u32[]{:S(2)}, u32[]{:S(2)}) collective-permute-start(bf16[80,2688]{1,0:T(8,128)(2,1)S(1)} %slice.435), channel_id=1, source_target_pairs={{0,2},{1,3},{2,0},{3,1},{4,6},{5,7},{6,4},{7,5},{8,10},{9,11},{10,... | collective-permute-start | bytes 1290248 | tf_op jit(solution)/shard_map/ppermute | solution.py:27
  595.5 56.4 %collective-permute-start.67 = (bf16[160,3840]{1,0:T(8,128)(2,1)}, bf16[160,3840]{1,0:T(8,128)(2,1)}, u32[]{:S(2)}, u32[]{:S(2)}) collective-permute-start(bf16[160,3840]{1,0:T(8,128)(2,1)} %get-tuple-element.396), channel_id=1, source_target_pairs={{0,2},{1,3},{2,0},{3,1},{4,6},{5,7},{6,4},{7,5},{8,10},{9,11},{10,... | collective-permute-start | bytes 3686408 | tf_op jit(solution)/shard_map/ppermute | solution.py:27
  597.7 56.1 %collective-permute-start.68 = (bf16[160,3840]{1,0:T(8,128)(2,1)}, bf16[160,3840]{1,0:T(8,128)(2,1)}, u32[]{:S(2)}, u32[]{:S(2)}) collective-permute-start(bf16[160,3840]{1,0:T(8,128)(2,1)} %get-tuple-element.397), channel_id=1, source_target_pairs={{0,1},{1,0},{2,3},{3,2},{4,5},{5,4},{6,7},{7,6},{8,9},{9,8},{10,11... | collective-permute-start | bytes 3686408 | tf_op jit(solution)/shard_map/ppermute | solution.py:27
  622.3 34.0 %collective-permute-start.65 = (bf16[512,1280]{1,0:T(8,128)(2,1)S(1)}, bf16[512,1280]{1,0:T(8,128)(2,1)S(1)}, u32[]{:S(2)}, u32[]{:S(2)}) collective-permute-start(bf16[512,1280]{1,0:T(8,128)(2,1)S(1)} %add_convert_fusion.2), channel_id=1, source_target_pairs={{0,8},{4,12},{8,16},{12,20},{16,24},{20,28},{1,9},{5,13},{9,17},{1... | collective-permute-start | bytes 3932168 | tf_op jit(solution)/shard_map/ppermute | solution.py:56
  (150 other events, 1818.6 us)
Sparse Core Ops, SparseCore 0:
  92.5 144.7 all-gather.5
  317.0 75.3 all-gather.3
  478.4 181.9 reduce-scatter.3

commit v5 on v4

--- a/solution.py
+++ b/solution.py
@@ -773,7 +773,7 @@
 
     cot_parts = after(cot_parts, *done)
     going_out = out_sums.step(out_slots[n - 2], out_slots[2], *done) if n > 2 else []
-    projected_cot = jnp.concatenate(cot_parts, axis=1)
+    projected_cot = jnp.concatenate(after(cot_parts, *(out_sums.sent if n > 2 else [])), axis=1)
     in_grad = [dot(normed_one[:, cut], projected_cot, TN).astype(BF16) for cut in halves[::-1]]
     in_scatter = DenseScatter(in_grad[1], in_grad[0])
     swap_in = in_scatter.swap()
@@ -783,7 +783,7 @@
     true_part = exact_matmul(
         jnp.concatenate([gain_two_grad[None, :], router_part], axis=0), order, NN
     )
-    done = [swap_in, swap_out]
+    done = [swap_in, swap_out, going_out]
 
     for i in range(k):
         going = [in_scatter.exchange(i, *done)]

time: 745 us -> 762 us (1.023)
  waiting for transfers between devices: 213 us -> 224 us
    ppermute x30, waiting for transfers between devices: 73.9 us -> 98.3 us  [line_send(): return lax.ppermute(x, 'dp', pairs)]
    ppermute x20, waiting for transfers between devices: 84.2 us -> 69.6 us  [fsdp_swap(): lax.ppermute(x, 'fsdp', [(f, f ^ bit) for f in range(lax.axis_size('fsdp'...]
    unnamed x212 -> x220, local copies, waits for them, and re-layouts: 25.6 us -> 25.8 us
  transfers between devices with their start and end apart: 88 -> 88, of which waited for: 35 -> 35; matrix products, arithmetic and copies ran while one was open for 20% -> 21% of each run, Pallas kernels for 27% -> 26%
where the time goes in v5:
time: 762 us; the launch traced here: 751 us
  waiting for transfers between devices  224 us (29%)
  Pallas kernels  199 us (26%)
  starting transfers between devices  127 us (17%)
  other arithmetic  84.5 us (11%)
  matrix products  57.8 us (8%)
  local copies, waits for them, and re-layouts  43.1 us (6%)
  between operations  16 us (2%)
    pallas_call x4, Pallas kernels, expert_chunk(): pl.pallas_call(expert_kernel, grid_spec=pltpu.PrefetchScalarGridSpec(num_...  117 us
    ppermute x30, waiting for transfers between devices, line_send(): return lax.ppermute(x, 'dp', pairs)  98.3 us
    ppermute x30, starting transfers between devices, line_send(): return lax.ppermute(x, 'dp', pairs)  73 us
    ppermute x20, waiting for transfers between devices, fsdp_swap(): lax.ppermute(x, 'fsdp', [(f, f ^ bit) for f in range(lax.axis_size('fsdp'...  69.6 us
    dot_general x15, matrix products, dot(): return lax.dot_general(a, b, (dims, ((), ())), preferred_element_type=F32)  55 us
    pallas_call x1, Pallas kernels, expert_weight_grads(): pl.pallas_call(expert_weights_kernel, grid=(local, 3), in_specs=[pl.Block...  33.4 us
    unnamed x220, local copies, waits for them, and re-layouts  25.8 us
    ppermute x20, starting transfers between devices, fsdp_swap(): lax.ppermute(x, 'fsdp', [(f, f ^ bit) for f in range(lax.axis_size('fsdp'...  25.2 us
  transfers between devices with their start and end apart: 88, of which 35 were waited for; matrix products, arithmetic and copies ran while one was open for 21% of the time, Pallas kernels for 26%

profile of v5, /device:TPU:0, one launch (start us, length us, event | category | flops | bytes accessed | tf_op | source)
XLA Modules:
  0.0 751.5 jit_solution(15255067005346796743)
XLA Ops:
  29.4 12.8 %collective-permute-done.1 = bf16[40,3968]{1,0:T(8,128)(2,1)S(1)} collective-permute-done((bf16[40,3968]{1,0:T(8,128)(2,1)S(1)}, bf16[40,3968]{1,0:T(8,128)(2,1)S(1)}, u32[]{:S(2)}, u32[]{:S(2)}) %collective-permute-start.1) | collective-permute-done | bytes 317472 | tf_op jit(solution)/shard_map/ppermute | solution.py:39
  49.7 7.8 %collective-permute-done.4 = bf16[80,3968]{1,0:T(8,128)(2,1)S(1)} collective-permute-done((bf16[80,3968]{1,0:T(8,128)(2,1)S(1)}, bf16[80,3968]{1,0:T(8,128)(2,1)S(1)}, u32[]{:S(2)}, u32[]{:S(2)}) %collective-permute-start.4) | collective-permute-done | bytes 634912 | tf_op jit(solution)/shard_map/ppermute | solution.py:27
  63.1 8.1 %collective-permute-done.11 = bf16[40,1280]{1,0:T(8,128)(2,1)S(1)} collective-permute-done((bf16[40,1280]{1,0:T(8,128)(2,1)S(1)}, bf16[40,1280]{1,0:T(8,128)(2,1)S(1)}, u32[]{:S(2)}, u32[]{:S(2)}) %collective-permute-start.11) | collective-permute-done | bytes 102432 | tf_op jit(solution)/shard_map/ppermute | solution.py:56
  78.5 10.9 %collective-permute-done.7 = bf16[160,3968]{1,0:T(8,128)(2,1)S(1)} collective-permute-done((bf16[160,3968]{1,0:T(8,128)(2,1)S(1)}, bf16[160,3968]{1,0:T(8,128)(2,1)S(1)}, u32[]{:S(2)}, u32[]{:S(2)}) %collective-permute-start.7) | collective-permute-done | bytes 1269792 | tf_op jit(solution)/shard_map/ppermute | solution.py:27
  113.1 7.5 fusion.2.qp.kp.vp
  123.2 13.0 %attention_forward.1 = (bf16[512,1280]{1,0:T(8,128)(2,1)}, bf16[512,1280]{1,0:T(8,128)(2,1)}, bf16[512,1280]{1,0:T(8,128)(2,1)}, bf16[512,1280]{1,0:T(8,128)(2,1)}, f32[10,1,512]{2,1,0:T(1,128)}) custom-call(f32[512,3840]{1,0:T(8,128)} %fusion.2.qp.kp.vp, f32[512,3840]{1,0:T(8,128)} %fusion.2.qp.kp.vp, f32[512,3840]{1,0:T(8,128)} %fusion.2.qp.kp.vp, ...), custom_call_target="tpu_custom_call" | custom-call | flops 14000000000 | bytes 35000000 | tf_op jit(solution)/shard_map/attention_forward/pallas_call | solution.py:283
  154.7 11.5 %collective-permute-start.22 = (bf16[512,1280]{1,0:T(8,128)(2,1)}, bf16[512,1280]{1,0:T(8,128)(2,1)}, u32[]{:S(2)}, u32[]{:S(2)}) collective-permute-start(bf16[512,1280]{1,0:T(8,128)(2,1)} %multiply_convert_fusion.x_own.x), channel_id=1, source_target_pairs={{0,8},{4,12},{8,16},{12,20},{16,24},{20,28},{1,9},{5,13},{9,17},{1... | collective-permute-start | bytes 3932168 | tf_op jit(solution)/shard_map/ppermute | solution.py:56
  169.4 15.7 %collective-permute-done.25 = bf16[528,1280]{1,0:T(8,128)(2,1)} collective-permute-done((bf16[528,1280]{1,0:T(8,128)(2,1)}, bf16[528,1280]{1,0:T(8,128)(2,1)}, u32[]{:S(2)}, u32[]{:S(2)}) %collective-permute-start.25) | collective-permute-done | bytes 1351712 | tf_op jit(solution)/shard_map/ppermute | solution.py:56
  185.1 8.9 %collective-permute-done.22 = bf16[512,1280]{1,0:T(8,128)(2,1)} collective-permute-done((bf16[512,1280]{1,0:T(8,128)(2,1)}, bf16[512,1280]{1,0:T(8,128)(2,1)}, u32[]{:S(2)}, u32[]{:S(2)}) %collective-permute-start.22) | collective-permute-done | bytes 1310752 | tf_op jit(solution)/shard_map/ppermute | solution.py:56
  194.1 18.5 %collective-permute-done.23 = bf16[512,1280]{1,0:T(8,128)(2,1)} collective-permute-done((bf16[512,1280]{1,0:T(8,128)(2,1)}, bf16[512,1280]{1,0:T(8,128)(2,1)}, u32[]{:S(2)}, u32[]{:S(2)}) %collective-permute-start.23) | collective-permute-done | bytes 1310752 | tf_op jit(solution)/shard_map/ppermute | solution.py:56
  218.0 19.1 %all-gather.6.cloned.1.call-done = bf16[8,3,224,1280]{3,2,1,0:T(8,128)(2,1)} async-done(((bf16[2,3,224,1280]{3,2,1,0:T(8,128)(2,1)}), bf16[8,3,224,1280]{3,2,1,0:T(8,128)(2,1)}) %all-gather.6.cloned.1.call-update) | async-done | bytes 13762576 | tf_op jit(solution)/shard_map/all_gather | solution.py:640
  237.1 29.1 %expert_chunk.4 = (bf16[2,384,1280]{2,1,0:T(8,128)(2,1)}, bf16[2,384,1280]{2,1,0:T(8,128)(2,1)}, bf16[2,384,896]{2,1,0:T(8,128)(2,1)}, bf16[2,384,896]{2,1,0:T(8...) custom-call(s32[1]{0:T(128)} %bitcast.37.first, ...), custom_call_target="tpu_custom_call" | custom-call | flops 30000001024 | bytes 75000000 | tf_op jit(solution)/shard_map/expert_chunk/pallas_call | solution.py:447
  266.2 8.3 %collective-permute-done.29 = bf16[512,1280]{1,0:T(8,128)(2,1)} collective-permute-done((bf16[512,1280]{1,0:T(8,128)(2,1)}, bf16[512,1280]{1,0:T(8,128)(2,1)}, u32[]{:S(2)}, u32[]{:S(2)}) %collective-permute-start.29) | collective-permute-done | bytes 1310752 | tf_op jit(solution)/shard_map/ppermute | solution.py:56
  286.4 29.3 %expert_chunk.5 = (bf16[2,384,1280]{2,1,0:T(8,128)(2,1)}, bf16[2,384,1280]{2,1,0:T(8,128)(2,1)}, bf16[2,384,896]{2,1,0:T(8,128)(2,1)}, bf16[2,384,896]{2,1,0:T(8...) custom-call(s32[1]{0:T(128)} %bitcast.37.first, ...), custom_call_target="tpu_custom_call" | custom-call | flops 30000001024 | bytes 75000000 | tf_op jit(solution)/shard_map/expert_chunk/pallas_call | solution.py:447
  326.9 29.4 %expert_chunk.6 = (bf16[2,384,1280]{2,1,0:T(8,128)(2,1)}, bf16[2,384,1280]{2,1,0:T(8,128)(2,1)}, bf16[2,384,896]{2,1,0:T(8,128)(2,1)}, bf16[2,384,896]{2,1,0:T(8...) custom-call(s32[1]{0:T(128)} %bitcast.37.first, ...), custom_call_target="tpu_custom_call" | custom-call | flops 30000001024 | bytes 75000000 | tf_op jit(solution)/shard_map/expert_chunk/pallas_call | solution.py:447
  357.7 29.6 %expert_chunk.7 = (bf16[2,384,1280]{2,1,0:T(8,128)(2,1)}, bf16[2,384,1280]{2,1,0:T(8,128)(2,1)}, bf16[2,384,896]{2,1,0:T(8,128)(2,1)}, bf16[2,384,896]{2,1,0:T(8...) custom-call(s32[1]{0:T(128)} %bitcast.37.first, ...), custom_call_target="tpu_custom_call" | custom-call | flops 30000001024 | bytes 75000000 | tf_op jit(solution)/shard_map/expert_chunk/pallas_call | solution.py:447
  396.5 6.1 collective-permute-start.45
  406.4 21.1 %shared_expert.1 = (f32[512,1280]{1,0:T(8,128)}, f32[512,1280]{1,0:T(8,128)}, bf16[640,2688]{1,0:T(8,128)(2,1)}, bf16[640,2688]{1,0:T(8,128)(2,1)}) custom-call(bf16[512,1280]{1,0:T(8,128)(2,1)} %multiply_convert_fusion.x_own.x, bf16[512,1280]{1,0:T(8,128)(2,1)} %c.1, bf16[512,1280]{1,0:T(8,128)(2,1)} %fusion.26.c_rel, ...), custom_call_target="tpu_custom_call" | custom-call | flops 30000001024 | bytes 75000000 | tf_op jit(solution)/shard_map/shared_expert/pallas_call | solution.py:540
  435.5 5.5 collective-permute-start.49
  443.6 33.4 %expert_weights.1 = bf16[4,2,3,224,1280]{4,3,2,1,0:T(8,128)(2,1)} custom-call(bf16[2,384,1280]{2,1,0:T(8,128)(2,1)} %get-tuple-element.349.refs_0_, bf16[2,384,1280]{2,1,0:T(8,128)(2,1)} %get-tuple-element.350.refs_1_, bf16[2,384,1280]{2,1,0:T(8,128)(2,1)} %get-tuple-element.351.refs_2_, bf16[2,384,1280]{2,1,0:T(8,128)(2,1)} %get-tuple-element.352.refs_3_, ...), custom_call_target="tpu_custom_call" | custom-call | flops 42278584320 | bytes 105696464 | tf_op jit(solution)/shard_map/expert_weights/pallas_call | solution.py:503
  480.8 5.8 convert_add_fusion.1
  501.3 22.0 %collective-permute-done.55 = bf16[160,2688]{1,0:T(8,128)(2,1)} collective-permute-done((bf16[160,2688]{1,0:T(8,128)(2,1)}, bf16[160,2688]{1,0:T(8,128)(2,1)}, u32[]{:S(2)}, u32[]{:S(2)}) %collective-permute-start.55) | collective-permute-done | bytes 860192 | tf_op jit(solution)/shard_map/ppermute | solution.py:27
  544.7 7.9 %fusion.24.d_in = bf16[512,1280]{1,0:T(8,128)(2,1)} fusion(s32[1280]{0:T(1024)S(1)} %copy-done.82, bf16[1280,1280]{1,0:T(8,128)(2,1)} %copy-done.78, f32[512,1280]{1,0:T(8,128)} %multiply_add_fusion), kind=kOutput, calls=%fused_computation.40 | convolution fusion | flops 3359047680 | bytes 7214080 | tf_op jit(solution)/shard_map/dot_general | solution.py:234
  552.6 14.2 %attention_backward.1 = (bf16[512,1280]{1,0:T(8,128)(2,1)}, bf16[512,1280]{1,0:T(8,128)(2,1)}, bf16[512,1280]{1,0:T(8,128)(2,1)}) custom-call(bf16[512,1280]{1,0:T(8,128)(2,1)} %get-tuple-element.321.q_in, bf16[512,1280]{1,0:T(8,128)(2,1)} %get-tuple-element.322.k_in, bf16[512,1280]{1,0:T(8,128)(2,1)} %get-tuple-element.323.v_in, ...), custom_call_target="tpu_custom_call" | custom-call | flops 15000000512 | bytes 37500000 | tf_op jit(solution)/shard_map/attention_backward/pallas_call | solution.py:321
  587.3 5.3 convert_add_fusion
  596.9 16.4 %collective-permute-done.63 = bf16[512,1280]{1,0:T(8,128)(2,1)} collective-permute-done((bf16[512,1280]{1,0:T(8,128)(2,1)}, bf16[512,1280]{1,0:T(8,128)(2,1)}, u32[]{:S(2)}, u32[]{:S(2)}) %collective-permute-start.63) | collective-permute-done | bytes 1310752 | tf_op jit(solution)/shard_map/ppermute | solution.py:56
  618.0 9.3 %fusion = f32[512,1280]{1,0:T(8,128)} fusion(bf16[512,3840]{1,0:T(8,128)(2,1)S(1)} %constant_dynamic-update-slice_fusion.12, bf16[1280,3968]{1,0:T(8,128)(2,1)} %copy-done.67), kind=kOutput, calls=%fused_computation.1 | convolution fusion | flops 5033164800 | bytes 16384000 | tf_op jit(solution)/shard_map/dot_general | solution.py:234
  641.0 7.4 collective-permute-start.65
  658.3 6.1 collective-permute-done.67
  666.9 8.6 %collective-permute-done.65 = bf16[512,1280]{1,0:T(8,128)(2,1)S(1)} collective-permute-done((bf16[512,1280]{1,0:T(8,128)(2,1)S(1)}, bf16[512,1280]{1,0:T(8,128)(2,1)S(1)}, u32[]{:S(2)}, u32[]{:S(2)}) %collective-permute-start.65) | collective-permute-done | bytes 1310752 | tf_op jit(solution)/shard_map/ppermute | solution.py:56
  690.1 6.1 collective-permute-done.73
  733.0 8.6 %collective-permute-done.80 = bf16[40,1408]{1,0:T(8,128)(2,1)S(1)} collective-permute-done((bf16[40,1408]{1,0:T(8,128)(2,1)S(1)}, bf16[40,1408]{1,0:T(8,128)(2,1)S(1)}, u32[]{:S(2)}, u32[]{:S(2)}) %collective-permute-start.80) | collective-permute-done | bytes 112672 | tf_op jit(solution)/shard_map/ppermute | solution.py:47
  (509 shorter events, 292.1 us)
Async XLA Ops:
  7.2 229.9 %all-gather.6.cloned.1.call-start = ((), (), s32[]{:S(2)}) async-start(), calls=%async_computation.2 | async-start | bytes 17203200 | tf_op jit(solution)/shard_map/all_gather | solution.py:640
  92.5 313.9 %all-gather.4.cloned.1.call-start = ((), (), s32[]{:S(2)}) async-start(), calls=%async_computation.1 | async-start | bytes 7096320 | tf_op jit(solution)/shard_map/all_gather | solution.py:710
  95.7 44.8 %collective-permute-start.19 = (bf16[528,1280]{1,0:T(8,128)(2,1)S(1)}, bf16[528,1280]{1,0:T(8,128)(2,1)S(1)}, u32[]{:S(2)}, u32[]{:S(2)}) collective-permute-start(bf16[528,1280]{1,0:T(8,128)(2,1)S(1)} %copy-done.38), channel_id=1, source_target_pairs={{0,8},{4,12},{8,16},{12,20},{16,24},{20,28},{1,9},{5,13},{9,17},{1... | collective-permute-start | bytes 4055048 | tf_op jit(solution)/shard_map/ppermute | solution.py:56
  98.9 41.7 %collective-permute-start.20 = (bf16[528,1280]{1,0:T(8,128)(2,1)S(1)}, bf16[528,1280]{1,0:T(8,128)(2,1)}, u32[]{:S(2)}, u32[]{:S(2)}) collective-permute-start(bf16[528,1280]{1,0:T(8,128)(2,1)S(1)} %copy-done.38), channel_id=1, source_target_pairs={{8,0},{12,4},{16,8},{20,12},{24,16},{28,20},{9,1},{13,5},{17,9},{2... | collective-permute-start | bytes 4055048 | tf_op jit(solution)/shard_map/ppermute | solution.py:56
  144.4 40.7 %collective-permute-start.25 = (bf16[528,1280]{1,0:T(8,128)(2,1)}, bf16[528,1280]{1,0:T(8,128)(2,1)}, u32[]{:S(2)}, u32[]{:S(2)}) collective-permute-start(bf16[528,1280]{1,0:T(8,128)(2,1)} %collective-permute-done.20), channel_id=1, source_target_pairs={{8,0},{12,4},{16,8},{20,12},{9,1},{13,5},{17,9},{21,13},{10,2},{14... | collective-permute-start | bytes 4055048 | tf_op jit(solution)/shard_map/ppermute | solution.py:56
  154.5 58.0 %collective-permute-start.27 = (bf16[528,1280]{1,0:T(8,128)(2,1)S(1)}, bf16[528,1280]{1,0:T(8,128)(2,1)}, u32[]{:S(2)}, u32[]{:S(2)}) collective-permute-start(bf16[528,1280]{1,0:T(8,128)(2,1)S(1)} %copy-done.38), channel_id=1, source_target_pairs={{0,4},{4,0},{8,12},{12,8},{16,20},{20,16},{24,28},{28,24},{1,5},{5... | collective-permute-start | bytes 4055048 | tf_op jit(solution)/shard_map/ppermute | solution.py:23
  154.7 39.3 %collective-permute-start.22 = (bf16[512,1280]{1,0:T(8,128)(2,1)}, bf16[512,1280]{1,0:T(8,128)(2,1)}, u32[]{:S(2)}, u32[]{:S(2)}) collective-permute-start(bf16[512,1280]{1,0:T(8,128)(2,1)} %multiply_convert_fusion.x_own.x), channel_id=1, source_target_pairs={{0,8},{4,12},{8,16},{12,20},{16,24},{20,28},{1,9},{5,13},{9,17},{1... | collective-permute-start | bytes 3932168 | tf_op jit(solution)/shard_map/ppermute | solution.py:56
  166.2 46.3 %collective-permute-start.23 = (bf16[512,1280]{1,0:T(8,128)(2,1)}, bf16[512,1280]{1,0:T(8,128)(2,1)}, u32[]{:S(2)}, u32[]{:S(2)}) collective-permute-start(bf16[512,1280]{1,0:T(8,128)(2,1)} %multiply_convert_fusion.x_own.x), channel_id=1, source_target_pairs={{8,0},{12,4},{16,8},{20,12},{24,16},{28,20},{9,1},{13,5},{17,9},{2... | collective-permute-start | bytes 3932168 | tf_op jit(solution)/shard_map/ppermute | solution.py:56
  168.6 43.9 %collective-permute-start.26 = (bf16[512,1280]{1,0:T(8,128)(2,1)}, bf16[512,1280]{1,0:T(8,128)(2,1)}, u32[]{:S(2)}, u32[]{:S(2)}) collective-permute-start(bf16[512,1280]{1,0:T(8,128)(2,1)} %multiply_convert_fusion.x_own.x), channel_id=1, source_target_pairs={{0,4},{4,0},{8,12},{12,8},{16,20},{20,16},{24,28},{28,24},{1,5},{5... | collective-permute-start | bytes 3932168 | tf_op jit(solution)/shard_map/ppermute | solution.py:23
  212.5 62.0 %collective-permute-start.30 = (bf16[528,1280]{1,0:T(8,128)(2,1)}, bf16[528,1280]{1,0:T(8,128)(2,1)S(1)}, u32[]{:S(2)}, u32[]{:S(2)}) collective-permute-start(bf16[528,1280]{1,0:T(8,128)(2,1)} %copy-done.41), channel_id=1, source_target_pairs={{16,24},{20,28},{17,25},{21,29},{18,26},{22,30},{19,27},{23,31}} | collective-permute-start | bytes 4055048 | tf_op jit(solution)/shard_map/ppermute | solution.py:56
  213.3 61.3 %collective-permute-start.31 = (bf16[528,1280]{1,0:T(8,128)(2,1)}, bf16[528,1280]{1,0:T(8,128)(2,1)S(1)}, u32[]{:S(2)}, u32[]{:S(2)}) collective-permute-start(bf16[528,1280]{1,0:T(8,128)(2,1)} %collective-permute-done.25), channel_id=1, source_target_pairs={{8,0},{12,4},{9,1},{13,5},{10,2},{14,6},{11,3},{15,7}} | collective-permute-start | bytes 4055048 | tf_op jit(solution)/shard_map/ppermute | solution.py:56
  214.6 51.6 %collective-permute-start.28 = (bf16[512,1280]{1,0:T(8,128)(2,1)}, bf16[512,1280]{1,0:T(8,128)(2,1)}, u32[]{:S(2)}, u32[]{:S(2)}) collective-permute-start(bf16[512,1280]{1,0:T(8,128)(2,1)} %collective-permute-done.22), channel_id=1, source_target_pairs={{8,16},{12,20},{16,24},{20,28},{9,17},{13,21},{17,25},{21,29},{10,... | collective-permute-start | bytes 3932168 | tf_op jit(solution)/shard_map/ppermute | solution.py:56
  216.3 58.2 %collective-permute-start.29 = (bf16[512,1280]{1,0:T(8,128)(2,1)}, bf16[512,1280]{1,0:T(8,128)(2,1)}, u32[]{:S(2)}, u32[]{:S(2)}) collective-permute-start(bf16[512,1280]{1,0:T(8,128)(2,1)} %collective-permute-done.23), channel_id=1, source_target_pairs={{8,0},{12,4},{16,8},{20,12},{9,1},{13,5},{17,9},{21,13},{10,2},{14... | collective-permute-start | bytes 3932168 | tf_op jit(solution)/shard_map/ppermute | solution.py:56
  283.2 33.0 %collective-permute-start.34 = (bf16[512,1280]{1,0:T(8,128)(2,1)}, bf16[512,1280]{1,0:T(8,128)(2,1)}, u32[]{:S(2)}, u32[]{:S(2)}) collective-permute-start(bf16[512,1280]{1,0:T(8,128)(2,1)} %collective-permute-done.29), channel_id=1, source_target_pairs={{8,0},{12,4},{9,1},{13,5},{10,2},{14,6},{11,3},{15,7}} | collective-permute-start | bytes 3932168 | tf_op jit(solution)/shard_map/ppermute | solution.py:56
  316.3 384.8 %reduce-scatter.4.cloned.1.call-start = ((), (), s32[]{:S(2)}) async-start(), calls=%async_computation.3 | async-start | bytes 17203200
  324.4 32.3 %collective-permute-start.39 = (bf16[528,1280]{1,0:T(8,128)(2,1)S(1)}, bf16[528,1280]{1,0:T(8,128)(2,1)S(1)}, u32[]{:S(2)}, u32[]{:S(2)}) collective-permute-start(bf16[528,1280]{1,0:T(8,128)(2,1)S(1)} %broadcast_select_fusion.c_own), channel_id=1, source_target_pairs={{0,4},{4,0},{8,12},{12,8},{16,20},{20,16},{24,28},{28,24},{1,5},{5... | collective-permute-start | bytes 4055048 | tf_op jit(solution)/shard_map/ppermute | solution.py:23
  394.6 145.1 %collective-permute-start.48 = (bf16[512,1280]{1,0:T(8,128)(2,1)}, bf16[512,1280]{1,0:T(8,128)(2,1)}, u32[]{:S(2)}, u32[]{:S(2)}) collective-permute-start(bf16[512,1280]{1,0:T(8,128)(2,1)} %get-tuple-element.325), channel_id=1, source_target_pairs={{0,4},{4,0},{8,12},{12,8},{16,20},{20,16},{24,28},{28,24},{1,5},{5... | collective-permute-start | bytes 3932168 | tf_op jit(solution)/shard_map/ppermute | solution.py:23
  396.5 33.7 %collective-permute-start.45 = (bf16[512,1280]{1,0:T(8,128)(2,1)}, bf16[512,1280]{1,0:T(8,128)(2,1)}, u32[]{:S(2)}, u32[]{:S(2)}) collective-permute-start(bf16[512,1280]{1,0:T(8,128)(2,1)} %convert_element_type.371), channel_id=1, source_target_pairs={{0,8},{4,12},{1,9},{5,13},{2,10},{6,14},{3,11},{7,15}} | collective-permute-start | bytes 3932168 | tf_op jit(solution)/shard_map/ppermute | solution.py:56
  435.5 52.2 %collective-permute-start.49 = (bf16[512,1280]{1,0:T(8,128)(2,1)}, bf16[512,1280]{1,0:T(8,128)(2,1)}, u32[]{:S(2)}, u32[]{:S(2)}) collective-permute-start(bf16[512,1280]{1,0:T(8,128)(2,1)} %add_convert_fusion.8), channel_id=1, source_target_pairs={{0,8},{4,12},{8,16},{12,20},{1,9},{5,13},{9,17},{13,21},{2,10},{6,... | collective-permute-start | bytes 3932168 | tf_op jit(solution)/shard_map/ppermute | solution.py:56
  441.0 46.8 %collective-permute-start.50 = (bf16[512,1280]{1,0:T(8,128)(2,1)}, bf16[512,1280]{1,0:T(8,128)(2,1)}, u32[]{:S(2)}, u32[]{:S(2)}) collective-permute-start(bf16[512,1280]{1,0:T(8,128)(2,1)} %add_convert_fusion.7), channel_id=1, source_target_pairs={{16,8},{20,12},{24,16},{28,20},{17,9},{21,13},{25,17},{29,21},{18,... | collective-permute-start | bytes 3932168 | tf_op jit(solution)/shard_map/ppermute | solution.py:56
  443.1 37.8 %collective-permute-start.52 = (bf16[640,2688]{1,0:T(8,128)(2,1)}, bf16[640,2688]{1,0:T(8,128)(2,1)}, u32[]{:S(2)}, u32[]{:S(2)}) collective-permute-start(bf16[640,2688]{1,0:T(8,128)(2,1)} %get-tuple-element.369), channel_id=1, source_target_pairs={{0,4},{4,0},{8,12},{12,8},{16,20},{20,16},{24,28},{28,24},{1,5},{5... | collective-permute-start | bytes 10321928 | tf_op jit(solution)/shard_map/ppermute | solution.py:23
  443.1 33.9 %collective-permute-start.51 = (bf16[512,1280]{1,0:T(8,128)(2,1)}, bf16[512,1280]{1,0:T(8,128)(2,1)}, u32[]{:S(2)}, u32[]{:S(2)}) collective-permute-start(bf16[512,1280]{1,0:T(8,128)(2,1)} %get-tuple-element.327), channel_id=1, source_target_pairs={{0,4},{4,0},{8,12},{12,8},{16,20},{20,16},{24,28},{28,24},{1,5},{5... | collective-permute-start | bytes 3932168 | tf_op jit(solution)/shard_map/ppermute | solution.py:23
  487.7 35.6 %collective-permute-start.55 = (bf16[160,2688]{1,0:T(8,128)(2,1)}, bf16[160,2688]{1,0:T(8,128)(2,1)}, u32[]{:S(2)}, u32[]{:S(2)}) collective-permute-start(bf16[160,2688]{1,0:T(8,128)(2,1)} %get-tuple-element.378), channel_id=1, source_target_pairs={{0,2},{1,3},{2,0},{3,1},{4,6},{5,7},{6,4},{7,5},{8,10},{9,11},{10,... | collective-permute-start | bytes 2580488 | tf_op jit(solution)/shard_map/ppermute | solution.py:27
  489.6 37.5 %collective-permute-start.56 = (bf16[160,2688]{1,0:T(8,128)(2,1)S(1)}, bf16[160,2688]{1,0:T(8,128)(2,1)}, u32[]{:S(2)}, u32[]{:S(2)}) collective-permute-start(bf16[160,2688]{1,0:T(8,128)(2,1)S(1)} %get-tuple-element.379), channel_id=1, source_target_pairs={{0,1},{1,0},{2,3},{3,2},{4,5},{5,4},{6,7},{7,6},{8,9},{9,8},{10,11... | collective-permute-start | bytes 2580488 | tf_op jit(solution)/shard_map/ppermute | solution.py:27
  496.8 32.9 %collective-permute-start.53 = (bf16[512,1280]{1,0:T(8,128)(2,1)S(1)}, bf16[512,1280]{1,0:T(8,128)(2,1)S(1)}, u32[]{:S(2)}, u32[]{:S(2)}) collective-permute-start(bf16[512,1280]{1,0:T(8,128)(2,1)S(1)} %add_convert_fusion.6), channel_id=1, source_target_pairs={{0,8},{4,12},{8,16},{12,20},{16,24},{20,28},{1,9},{5,13},{9,17},{1... | collective-permute-start | bytes 3932168 | tf_op jit(solution)/shard_map/ppermute | solution.py:56
  498.3 32.3 %collective-permute-start.54 = (bf16[512,1280]{1,0:T(8,128)(2,1)S(1)}, bf16[512,1280]{1,0:T(8,128)(2,1)S(1)}, u32[]{:S(2)}, u32[]{:S(2)}) collective-permute-start(bf16[512,1280]{1,0:T(8,128)(2,1)S(1)} %add_convert_fusion.5), channel_id=1, source_target_pairs={{8,0},{12,4},{16,8},{20,12},{24,16},{28,20},{9,1},{13,5},{17,9},{2... | collective-permute-start | bytes 3932168 | tf_op jit(solution)/shard_map/ppermute | solution.py:56
  530.7 36.1 %collective-permute-start.59 = (bf16[80,2688]{1,0:T(8,128)(2,1)}, bf16[80,2688]{1,0:T(8,128)(2,1)S(1)}, u32[]{:S(2)}, u32[]{:S(2)}) collective-permute-start(bf16[80,2688]{1,0:T(8,128)(2,1)} %slice.436), channel_id=1, source_target_pairs={{0,1},{1,0},{2,3},{3,2},{4,5},{5,4},{6,7},{7,6},{8,9},{9,8},{10,11... | collective-permute-start | bytes 1290248 | tf_op jit(solution)/shard_map/ppermute | solution.py:27
  532.3 34.5 %collective-permute-start.60 = (bf16[80,2688]{1,0:T(8,128)(2,1)S(1)}, bf16[80,2688]{1,0:T(8,128)(2,1)}, u32[]{:S(2)}, u32[]{:S(2)}) collective-permute-start(bf16[80,2688]{1,0:T(8,128)(2,1)S(1)} %slice.435), channel_id=1, source_target_pairs={{0,2},{1,3},{2,0},{3,1},{4,6},{5,7},{6,4},{7,5},{8,10},{9,11},{10,... | collective-permute-start | bytes 1290248 | tf_op jit(solution)/shard_map/ppermute | solution.py:27
  534.8 32.0 %collective-permute-start.57 = (bf16[512,1280]{1,0:T(8,128)(2,1)}, bf16[512,1280]{1,0:T(8,128)(2,1)}, u32[]{:S(2)}, u32[]{:S(2)}) collective-permute-start(bf16[512,1280]{1,0:T(8,128)(2,1)} %convert_element_type.399), channel_id=1, source_target_pairs={{0,8},{4,12},{1,9},{5,13},{2,10},{6,14},{3,11},{7,15}} | collective-permute-start | bytes 3932168 | tf_op jit(solution)/shard_map/ppermute | solution.py:56
  614.6 49.8 %collective-permute-start.67 = (bf16[160,3840]{1,0:T(8,128)(2,1)}, bf16[160,3840]{1,0:T(8,128)(2,1)}, u32[]{:S(2)}, u32[]{:S(2)}) collective-permute-start(bf16[160,3840]{1,0:T(8,128)(2,1)} %get-tuple-element.402), channel_id=1, source_target_pairs={{0,2},{1,3},{2,0},{3,1},{4,6},{5,7},{6,4},{7,5},{8,10},{9,11},{10,... | collective-permute-start | bytes 3686408 | tf_op jit(solution)/shard_map/ppermute | solution.py:27
  616.2 48.2 %collective-permute-start.68 = (bf16[160,3840]{1,0:T(8,128)(2,1)}, bf16[160,3840]{1,0:T(8,128)(2,1)}, u32[]{:S(2)}, u32[]{:S(2)}) collective-permute-start(bf16[160,3840]{1,0:T(8,128)(2,1)} %get-tuple-element.403), channel_id=1, source_target_pairs={{0,1},{1,0},{2,3},{3,2},{4,5},{5,4},{6,7},{7,6},{8,9},{9,8},{10,11... | collective-permute-start | bytes 3686408 | tf_op jit(solution)/shard_map/ppermute | solution.py:27
  641.0 34.5 %collective-permute-start.65 = (bf16[512,1280]{1,0:T(8,128)(2,1)S(1)}, bf16[512,1280]{1,0:T(8,128)(2,1)S(1)}, u32[]{:S(2)}, u32[]{:S(2)}) collective-permute-start(bf16[512,1280]{1,0:T(8,128)(2,1)S(1)} %add_convert_fusion.2), channel_id=1, source_target_pairs={{0,8},{4,12},{8,16},{12,20},{16,24},{20,28},{1,9},{5,13},{9,17},{1... | collective-permute-start | bytes 3932168 | tf_op jit(solution)/shard_map/ppermute | solution.py:56
  (154 other events, 1884.6 us)
Sparse Core Ops, SparseCore 0:
  92.6 144.4 all-gather.5
  316.4 75.4 all-gather.3
  492.0 168.2 reduce-scatter.3
